TPU v7x, 32 devices: a whole 2x2x4 slice. The times are simulated.
32 devices in a mesh: dom: 16 (over z, y, core), feat: 2 (over x).
Axes of the slice: x: 2, y: 2, z: 4, core: 2. Of those that a mesh axis runs over, the one named last changes fastest.
Arguments:
- features: bfloat16 [256, 8192], P('feat', 'dom'), may hold values from -6 to 6
- in_degree: int32 [8192], P('dom'), may hold values from 16 to 64
- send_rows: int32 [16, 16, 16], P('dom'), may hold values from 0 to 511
- send_count: int32 [16, 16], P('dom'), may hold values from 0 to 16, as said below
- hub_owner: int32 [4], replicated, may hold values from 0 to 15, as said below
- hub_rows: int32 [4, 128], replicated, may hold values from 0 to 511
- local_dest: int32 [256], P('dom'), may hold values from 0 to 3
- local_source: int32 [256], P('dom'), may hold values from 0 to 3
- local_tiles: bfloat16 [256, 128, 128], P('dom'), may hold values from 0 to 1
- border_dest: int32 [256], P('dom'), may hold values from 0 to 3
- border_source: int32 [256], P('dom'), may hold values from 0 to 1
- border_tiles: bfloat16 [256, 128, 128], P('dom'), may hold values from 0 to 1
- hub_dest: int32 [256], P('dom'), may hold values from 0 to 3
- hub_source: int32 [256], P('dom'), may hold values from 0 to 3
- hub_tiles: bfloat16 [256, 128, 128], P('dom'), may hold values from 0 to 1
- self_weight: bfloat16 [256, 256], P('feat'), may hold values from -0.375 to 0.375
- neighbor_weight: bfloat16 [256, 256], P('feat'), may hold values from -0.375 to 0.375
- out_bias: float32 [256], P('feat'), may hold values from -3 to 3
Outputs:
- updated: bfloat16 [256, 8192], P('feat', 'dom')
Inputs may be any that keep to these rules, and one draw needn't show every extreme that they name: send_count[q, p] of the 16 slots from q to p are live; in every draw some destinations receive 16 live rows from every source. Hub block b belongs to partition hub_owner[b]; one partition owns exactly 2 blocks, every other partition at most one.
All inputs are finite; a program needn't handle non-finite values.
Results may differ from a plain program's by a relative error of at most 0.0034.
Values may be sent and summed in bfloat16 or wider, within the bound.
No kernel may reach another device: no remote copies, remote signals or barrier semaphores. Data moves between devices by JAX's collectives and lax.ppermute only.
A program may use at most 64 MiB of HBM per device.

v0:
```python
import jax
import jax.numpy as jnp
from jax import lax
from jax.sharding import PartitionSpec as P

HOWN = 2


def tile_terms(blocks, targets, source, tile_values, row_blocks):
    picked = jnp.take(blocks, source, axis=1)
    partial_value = jnp.einsum(
        "ftk,tik->fti", picked, tile_values, preferred_element_type=jnp.float32
    )
    onehot = (targets[:, None] == jnp.arange(row_blocks, dtype=jnp.int32)[None, :]).astype(
        jnp.float32
    )
    return jnp.einsum("fti,tr->fri", partial_value, onehot, precision=lax.Precision.HIGHEST)


def shards(
    features,
    in_degree,
    send_rows,
    send_count,
    hub_owner,
    hub_rows,
    local_dest,
    local_source,
    local_tiles,
    border_dest,
    border_source,
    border_tiles,
    hub_dest,
    hub_source,
    hub_tiles,
    self_weight,
    neighbor_weight,
    out_bias,
):
    feat_rows, vertex_count = features.shape
    tile_size = local_tiles.shape[1]
    row_blocks = vertex_count // tile_size
    partitions = lax.axis_size("dom")
    capacity = send_rows.shape[2]
    own_blocks = features.reshape(feat_rows, row_blocks, tile_size)
    local_sum = tile_terms(own_blocks, local_dest, local_source, local_tiles, row_blocks)
    pick_rows = send_rows[0].reshape(-1)
    outgoing = jnp.take(features, pick_rows, axis=1).reshape(feat_rows, partitions, capacity)
    alive_slots = (jnp.arange(capacity, dtype=jnp.int32)[None, :] < send_count[0][:, None]).astype(
        jnp.bfloat16
    )
    outgoing = outgoing * alive_slots[None]
    incoming = lax.all_to_all(outgoing, "dom", split_axis=1, concat_axis=1, tiled=True)
    border_blocks = incoming.reshape(feat_rows, partitions * capacity // tile_size, tile_size)
    border_sum = tile_terms(border_blocks, border_dest, border_source, border_tiles, row_blocks)
    hub_count = hub_owner.shape[0]
    position = lax.axis_index("dom")
    block_ids = jnp.arange(hub_count, dtype=jnp.int32)
    earlier = block_ids[:, None] > block_ids[None, :]
    same_owner = hub_owner[:, None] == hub_owner[None, :]
    order_rank = jnp.sum((earlier & same_owner).astype(jnp.int32), axis=1)
    owned_here = hub_owner == position
    choose = (
        owned_here[None, :] & (order_rank[None, :] == jnp.arange(HOWN, dtype=jnp.int32)[:, None])
    ).astype(jnp.int32)
    slot_rows = jnp.sum(choose[:, :, None] * hub_rows[None], axis=1)
    owned_blocks = jnp.take(features, slot_rows.reshape(-1), axis=1).reshape(
        feat_rows, HOWN, tile_size
    )
    everyone = lax.all_gather(owned_blocks, "dom", axis=1, tiled=True)
    hub_blocks = jnp.take(everyone, hub_owner * HOWN + order_rank, axis=1)
    hub_sum = tile_terms(hub_blocks, hub_dest, hub_source, hub_tiles, row_blocks)
    degree = in_degree.astype(jnp.float32).reshape(row_blocks, tile_size)
    aggregate = (
        ((local_sum + border_sum + hub_sum) / degree[None])
        .astype(jnp.bfloat16)
        .reshape(feat_rows, vertex_count)
    )
    running = jnp.dot(
        self_weight,
        lax.all_gather(features, "feat", axis=0, tiled=True),
        preferred_element_type=jnp.float32,
    )
    combined = running + jnp.dot(
        neighbor_weight,
        lax.all_gather(aggregate, "feat", axis=0, tiled=True),
        preferred_element_type=jnp.float32,
    )
    return jnp.maximum(combined + out_bias[:, None], 0.0).astype(jnp.bfloat16)


def solution(mesh):
    placed = (
        P("feat", "dom"),
        P("dom"),
        P("dom", None, None),
        P("dom", None),
        P(),
        P(),
        P("dom"),
        P("dom"),
        P("dom", None, None),
        P("dom"),
        P("dom"),
        P("dom", None, None),
        P("dom"),
        P("dom"),
        P("dom", None, None),
        P("feat", None),
        P("feat", None),
        P("feat"),
    )
    return jax.shard_map(
        shards, mesh=mesh, in_specs=placed, out_specs=P("feat", "dom"), check_vma=False
    )
```

profile of v0, /device:TPU:0, one launch (start us, length us, event | category | flops | bytes accessed | tf_op | source)
XLA Modules:
  0.0 80.8 jit_solution(9627374421501627303)
XLA Ops:
  6.5 0.8 %reshape_squeeze.3 = s32[256]{0:T(256)S(1)} reshape(s32[1,16,16]{2,1,0:T(8,128)} %param.24) | data formatting | bytes 2048 | tf_op jit(solution)/shard_map/reshape;squeeze | solution.py:47
  7.4 1.0 %copy.61 = bf16[128,512]{0,1:T(8,128)(2,1)S(1)} copy(bf16[128,512]{1,0:T(8,128)(2,1)} %param.22) | data formatting | bytes 262144 | tf_op args[0]
  8.4 0.6 copy-done.11
  9.2 0.9 %gather_fusion.3 = bf16[256,128]{1,0:T(8,128)(2,1)S(1)} fusion(bf16[128,512]{0,1:T(8,128)(2,1)S(1)} %copy.61, s32[1024]{0:T(1024)S(1)} %pad_clamp_fusion.4), kind=kCustom, calls=%fused_computation.1.clone | custom fusion | bytes 132096 | tf_op jit(solution)/shard_map/jit(_take)/gather | solution.py:48
  10.1 0.7 broadcast_multiply_fusion
  10.9 7.4 %all-to-all-start = ((bf16[128,16,16]{0,2,1:T(8,128)(2,1)}), bf16[128,16,16]{0,2,1:T(8,128)(2,1)S(1)}, u32[]{:S(2)}, u32[]{:S(2)}) async-start(bf16[128,16,16]{0,2,1:T(8,128)(2,1)} %broadcast_multiply_fusion), calls=%async_computation | async-start | bytes 131072 | tf_op jit(solution)/shard_map/all_to_all | solution.py:53
  18.3 0.6 copy-done.12
  18.9 0.2 convert_reduce_fusion
  19.1 0.7 copy-done.6
  19.9 0.9 %gather_fusion.4 = bf16[256,128]{1,0:T(8,128)(2,1)S(1)} fusion(bf16[128,512]{0,1:T(8,128)(2,1)S(1)} %copy.61, s32[1024]{0:T(1024)S(1)} %pad_clamp_fusion.2), kind=kCustom, calls=%fused_computation.3.clone | custom fusion | bytes 132096 | tf_op jit(solution)/shard_map/jit(_take)/gather | solution.py:67
  20.9 0.7 copy.68
  21.6 0.6 copy-done.13
  22.3 0.6 copy-done.14
  23.1 0.6 gather_fusion.2
  23.8 0.6 copy-done.7
  24.5 0.5 convolution_bitcast_fusion.2
  25.1 1.1 %fusion.7 = f32[4,128,128]{2,0,1:T(4,128)S(1)} fusion(f32[128,16,128]{2,0,1:T(8,128)S(1)} %convolution_bitcast_fusion.2, s32[16]{0:T(128)S(1)} %copy-done.8), kind=kOutput, calls=%fused_computation.20 | convolution fusion | flops 12582976 | bytes 1310784 | tf_op jit(solution)/shard_map/fti,tr->fri/dot_general | solution.py:17
  26.2 6.5 %all_gather.9 = bf16[256,512]{1,0:T(8,128)(2,1)S(1)} all-gather(bf16[128,512]{1,0:T(8,128)(2,1)S(1)} %copy-done.3), channel_id=1, replica_groups=mesh['dom'=16,'feat'=2] {'feat'}, dimensions={0}, use_global_device_ids=true | all-gather | bytes 393216 | tf_op jit(solution)/shard_map/all_gather | solution.py:81
  32.9 0.6 gather_fusion
  33.5 0.4 copy-done.1
  33.9 0.5 convolution_bitcast_fusion.1
  34.6 1.1 %convolution_add_fusion.1 = f32[4,128,128]{2,0,1:T(4,128)S(1)} fusion(f32[4,128,128]{2,0,1:T(4,128)S(1)} %fusion.7, f32[128,16,128]{2,0,1:T(8,128)S(1)} %convolution_bitcast_fusion.1, s32[16]{0:T(128)S(1)} %copy-done.9), kind=kOutput, calls=%fused_computation.10 | convolution fusion | flops 12648512 | bytes 1572928 | tf_op jit(solution)/shard_map/fti,tr->fri/dot_general | solution.py:17
  35.6 25.4 %all-gather.2.cloned.1.call-done = bf16[128,32,128]{2,0,1:T(8,128)(2,1)} async-done(((bf16[128,2,128]{2,0,1:T(8,128)(2,1)}), bf16[128,32,128]{2,0,1:T(8,128)(2,1)}) %all-gather.2.cloned.1.call-update) | async-done | bytes 1048592 | tf_op jit(solution)/shard_map/all_gather | solution.py:70
  61.0 1.8 %gather_fusion.1 = bf16[4,128,128]{2,1,0:T(8,128)(2,1)S(1)} fusion(bf16[128,32,128]{2,0,1:T(8,128)(2,1)} %all-gather.2.cloned.1.call-done, s32[1024]{0:T(1024)S(1)} %pad_clamp_fusion.1), kind=kCustom, calls=%fused_computation.5 | custom fusion | bytes 262160 | tf_op jit(solution)/shard_map/jit(_take)/gather | solution.py:71
  62.9 0.6 gather_fusion.5
  63.6 0.4 copy-done.2
  64.0 0.5 convolution_bitcast_fusion
  64.6 1.1 %fusion.3 = bf16[4,128,128]{2,0,1:T(4,128)(2,1)S(1)} fusion(f32[4,128,128]{2,0,1:T(4,128)S(1)} %convolution_add_fusion.1, f32[128,16,128]{2,0,1:T(8,128)S(1)} %convolution_bitcast_fusion, f32[4,128]{1,0:T(4,128)S(1)} %convert_bitcast_fusion, s32[16]{0:T(128)S(1)} %copy-done.16), kind=kOutput, calls=%fused_computation.16 | convolution fusion | flops 12779584 | bytes 1443904 | tf_op jit(solution)/shard_map/fti,tr->fri/dot_general | solution.py:17
  65.7 6.5 %all_gather.11 = bf16[256,512]{1,0:T(8,128)(2,1)S(1)} all-gather(bf16[128,512]{1,0:T(8,128)(2,1)S(1)} %bitcast.56), channel_id=1, replica_groups=mesh['dom'=16,'feat'=2] {'feat'}, dimensions={0}, use_global_device_ids=true | all-gather | bytes 393216 | tf_op jit(solution)/shard_map/all_gather | solution.py:86
  72.2 0.2 convolution_bitcast_fusion.3
  72.4 0.6 copy-done.5
  73.1 0.8 %fusion.4 = bf16[128,512]{1,0:T(8,128)(2,1)} fusion(f32[128,512]{1,0:T(8,128)S(1)} %convolution_bitcast_fusion.3, bf16[128,256]{1,0:T(8,128)(2,1)S(1)} %copy-done.5, bf16[256,512]{1,0:T(8,128)(2,1)S(1)} %all_gather.9, f32[128]{0:T(128)S(1)} %copy-done.10), kind=kOutput, calls=%fused_computation.17 | convolution fusion | flops 33816576 | bytes 721408 | tf_op jit(solution)/shard_map/dot_general | solution.py:79
  (55 shorter events, 1.3 us)
Async XLA Ops:
  6.5 17.9 %copy-start = (bf16[16,128,128]{2,1,0:T(8,128)(2,1)S(1)}, bf16[16,128,128]{2,1,0:T(8,128)(2,1)}, u32[]{:S(2)}) copy-start(bf16[16,128,128]{2,1,0:T(8,128)(2,1)} %param.30) | copy-start | bytes 1572868
  8.4 0.7 copy-start.11
  10.9 21.9 %all-to-all-start = ((bf16[128,16,16]{0,2,1:T(8,128)(2,1)}), bf16[128,16,16]{0,2,1:T(8,128)(2,1)S(1)}, u32[]{:S(2)}, u32[]{:S(2)}) async-start(bf16[128,16,16]{0,2,1:T(8,128)(2,1)} %broadcast_multiply_fusion), calls=%async_computation | async-start | bytes 131072 | tf_op jit(solution)/shard_map/all_to_all | solution.py:53
  18.3 0.7 copy-start.12
  18.3 42.8 %all-gather.2.cloned.1.call-start = ((), (), s32[]{:S(2)}) async-start(), calls=%async_computation.1 | async-start | bytes 1114112 | tf_op jit(solution)/shard_map/all_gather | solution.py:70
  19.1 0.7 copy-start.6
  21.6 0.7 copy-start.13
  22.3 0.7 copy-start.14
  23.1 0.7 copy-start.15
  23.8 0.7 copy-start.7
  24.5 0.7 copy-start.8
  25.1 1.1 %copy-start.3 = (bf16[128,512]{1,0:T(8,128)(2,1)S(1)}, bf16[128,512]{1,0:T(8,128)(2,1)}, u32[]{:S(2)}) copy-start(bf16[128,512]{1,0:T(8,128)(2,1)} %param.22) | copy-start | bytes 393220
  32.9 1.0 %copy-start.1 = (bf16[16,128,128]{2,1,0:T(8,128)(2,1)S(1)}, bf16[16,128,128]{2,1,0:T(8,128)(2,1)}, u32[]{:S(2)}) copy-start(bf16[16,128,128]{2,1,0:T(8,128)(2,1)} %param.33) | copy-start | bytes 1572868
  33.9 0.7 copy-start.9
  62.9 1.0 %copy-start.2 = (bf16[16,128,128]{2,1,0:T(8,128)(2,1)S(1)}, bf16[16,128,128]{2,1,0:T(8,128)(2,1)}, u32[]{:S(2)}) copy-start(bf16[16,128,128]{2,1,0:T(8,128)(2,1)} %param.36) | copy-start | bytes 1572868
  64.0 0.7 copy-start.16
  65.7 6.5 %copy-start.4 = (bf16[128,256]{1,0:T(8,128)(2,1)S(1)}, bf16[128,256]{1,0:T(8,128)(2,1)}, u32[]{:S(2)}) copy-start(bf16[128,256]{1,0:T(8,128)(2,1)} %param.38) | copy-start | bytes 196612
  72.2 0.8 %copy-start.5 = (bf16[128,256]{1,0:T(8,128)(2,1)S(1)}, bf16[128,256]{1,0:T(8,128)(2,1)}, u32[]{:S(2)}) copy-start(bf16[128,256]{1,0:T(8,128)(2,1)} %param.37) | copy-start | bytes 196612
  72.2 0.8 %copy-start.10 = (f32[128]{0:T(128)S(1)}, f32[128]{0:T(128)}, u32[]{:S(2)}) copy-start(f32[128]{0:T(128)} %param.39) | copy-start | bytes 1540
Sparse Core Ops, SparseCore 0:
  21.7 39.2 all-gather.1
where the time goes:
time: 81.3 us; the launch traced here: 80.8 us
  waiting for transfers between devices  25.4 us (31%)
  local copies, waits for them, and re-layouts  14 us (17%)
  between operations  13.7 us (17%)
  blocking collectives  13 us (16%)
  starting transfers between devices  7.43 us (9%)
  matrix products  5.74 us (7%)
  other arithmetic  1.48 us (2%)
    all_gather x1, waiting for transfers between devices, shards(): everyone = lax.all_gather(owned_blocks, 'dom', axis=1, tiled=True)  25.4 us
    all_to_all x1, starting transfers between devices, shards(): lax.all_to_all(outgoing, 'dom', split_axis=1, concat_axis=1, tiled=True)  7.38 us
    unnamed x36, local copies, waits for them, and re-layouts  6.72 us
    all_gather x1, blocking collectives, shards(): lax.all_gather(features, 'feat', axis=0, tiled=True)  6.51 us
    all_gather x1, blocking collectives, shards(): lax.all_gather(aggregate, 'feat', axis=0, tiled=True)  6.47 us
    dot_general x3, matrix products, tile_terms(): jnp.einsum('fti,tr->fri', partial_value, onehot, precision=lax.Precision....  3.16 us
    gather x3, local copies, waits for them, and re-layouts, tile_terms(): picked = jnp.take(blocks, source, axis=1)  1.94 us
    gather x1, local copies, waits for them, and re-layouts, shards(): hub_blocks = jnp.take(everyone, hub_owner * HOWN + order_rank, axis=1)  1.79 us
  transfers between devices with their start and end apart: 2, of which 1 were waited for; matrix products, arithmetic and copies ran while one was open for 8% of the time, Pallas kernels for 0%

commit v1 on v0

v1 whole, which is shorter than its diff:
```python
import functools

import jax
import jax.numpy as jnp
from jax import lax
from jax.experimental import pallas as pl
from jax.experimental.pallas import tpu as pltpu
from jax.sharding import PartitionSpec as P

BF16 = jnp.bfloat16
F32 = jnp.float32
VM = pl.BlockSpec(memory_space=pltpu.VMEM)
SM = pl.BlockSpec(memory_space=pltpu.SMEM)


def call(body, outs, specs, scratch=(), flops=0, size=0, name=None):
    return pl.pallas_call(
        body,
        out_shape=outs,
        in_specs=specs,
        out_specs=jax.tree.map(lambda _: VM, outs),
        scratch_shapes=scratch,
        compiler_params=pltpu.CompilerParams(vmem_limit_bytes=24 << 20),
        cost_estimate=pl.CostEstimate(flops=flops, bytes_accessed=size, transcendentals=0),
        name=name,
    )


def rows(ref, start, size, step):
    return ref[pl.ds(pl.multiple_of(start, step), size), :]


def column(row):
    m = row.shape[1]
    down = lax.broadcasted_iota(jnp.int32, (m, m), 0)
    across = lax.broadcasted_iota(jnp.int32, (m, m), 1)
    return jnp.sum(jnp.where(down == across, row, jnp.zeros_like(row)), axis=1, keepdims=True)


def pick(owner, features, send_rows, send_count, hub_rows, keep, message, hub_keep, gathered):
    me = lax.axis_index("dom")
    bit = me & 1
    parts, cap = send_rows.shape[1:]
    blocks, tile = hub_rows.shape
    vertices = features.shape[1]
    half = tile // 2
    shape = (parts, cap, cap)
    slot = lax.broadcasted_iota(jnp.int32, shape, 1)
    across = lax.broadcasted_iota(jnp.int32, shape, 2)
    lists = jnp.sum(
        jnp.where(slot == across, send_rows[0][:, None, :], 0), axis=2, keepdims=True
    )
    shape = (parts, cap, parts)
    target = lax.broadcasted_iota(jnp.int32, shape, 0)
    across = lax.broadcasted_iota(jnp.int32, shape, 2)
    count = jnp.sum(
        jnp.where(target == across, send_count[...][None], 0), axis=2, keepdims=True
    )
    slot = lax.broadcasted_iota(jnp.int32, (parts, cap, 1), 1)
    lists = jnp.where(slot < count, lists, -1).reshape(parts * cap, 1)
    contract = (((1,), (1,)), ((), ()))

    def select(index):
        vertex = lax.broadcasted_iota(jnp.int32, (index.shape[0], vertices), 1)
        onehot = (vertex == index).astype(F32).astype(BF16)
        return lax.dot_general(onehot, features[...], contract, preferred_element_type=F32).astype(BF16)

    gathered[: parts * cap, :] = select(lists)
    for b in range(blocks):
        index = column(jnp.where(owner[b] == me, hub_rows[b : b + 1, :], -1))
        gathered[parts * cap + b * tile : parts * cap + (b + 1) * tile, :] = select(index)
    for group in range(parts // 2):
        there = slice(group * cap, (group + 1) * cap)
        keep[there, :] = rows(gathered, (2 * group + bit) * cap, cap, cap)
        message[there, :] = rows(gathered, (2 * group + 1 - bit) * cap, cap, cap)
    top = parts * cap
    for b in range(blocks):
        there = slice(b * half, (b + 1) * half)
        hub_keep[there, :] = rows(gathered, top + b * tile + bit * half, half, half)
        message[top // 2 + b * half : top // 2 + (b + 1) * half, :] = rows(
            gathered, top + b * tile + (1 - bit) * half, half, half
        )


def step(k, parts, cap, last, keep, hub, received, *outs):
    me = lax.axis_index("dom")
    bit = (me >> k) & 1
    border = parts * cap // 2
    merged = hub[hub.shape[0] - (received.shape[0] - border) :, :] + received[border:, :]
    run = (1 << k) * cap
    if last:
        lists, message = outs
        lists[pl.ds(pl.multiple_of(bit * run, run), run), :] = keep[...]
        lists[pl.ds(pl.multiple_of((1 - bit) * run, run), run), :] = received[:border, :]
        message[...] = merged
        return
    next_keep, message = outs
    ahead = (me >> (k + 1)) & 1
    for pair in range(parts >> (k + 2)):
        stay, go = (2 * pair + ahead) * run, (2 * pair + 1 - ahead) * run
        mine = pl.ds(pl.multiple_of((2 * pair + bit) * run, run), run)
        theirs = pl.ds(pl.multiple_of((2 * pair + 1 - bit) * run, run), run)
        next_keep[mine, :] = rows(keep, stay, run, run)
        next_keep[theirs, :] = rows(received, stay, run, run)
        message[mine, :] = rows(keep, go, run, run)
        message[theirs, :] = rows(received, go, run, run)
    message[border:, :] = merged


def add_tiles(dest, source, tiles, products, total, operand, contract):
    count, tile, _ = tiles.shape
    for t in range(count):
        products[t] = lax.dot_general(
            tiles[t], operand(source[t]), contract, preferred_element_type=F32
        )
    for t in range(count):
        there = pl.ds(pl.multiple_of(dest[t] * tile, tile), tile)
        total[there, :] = total[there, :] + products[t]


def local_terms(dest, source, features, tiles, in_degree, total, degree, products):
    tile = tiles.shape[1]
    total[...] = jnp.zeros_like(total)
    add_tiles(
        dest, source, tiles, products, total,
        lambda s: features[:, pl.ds(pl.multiple_of(s * tile, tile), tile)],
        (((1,), (1,)), ((), ())),
    )
    for r in range(total.shape[0] // tile):
        row = in_degree[:, r * tile : (r + 1) * tile].astype(F32)
        degree[r * tile : (r + 1) * tile, :] = column(row)


def border_terms(dest, source, lists, tiles, before, total, products):
    tile = tiles.shape[1]
    total[...] = before[...]
    add_tiles(
        dest, source, tiles, products, total,
        lambda s: rows(lists, s * tile, tile, tile), (((1,), (0,)), ((), ())),
    )


def hub_terms(dest, source, mine, theirs, tiles, before, degree, aggregate, hubs, total, products):
    tile = tiles.shape[1]
    half = tile // 2
    bit = lax.axis_index("dom") & 1
    for b in range(mine.shape[0] // half):
        there = slice(b * half, (b + 1) * half)
        hubs[pl.ds(pl.multiple_of(b * tile + bit * half, half), half), :] = mine[there, :]
        hubs[pl.ds(pl.multiple_of(b * tile + (1 - bit) * half, half), half), :] = theirs[there, :]
    total[...] = before[...]
    add_tiles(
        dest, source, tiles, products, total,
        lambda s: rows(hubs, s * tile, tile, tile), (((1,), (0,)), ((), ())),
    )
    aggregate[...] = (total[...] / degree[...]).astype(BF16)


def own_part(self_weight, neighbor_weight, out_bias, features, others, aggregate, base):
    width = features.shape[0]
    place = lax.axis_index("feat")
    mine = pl.ds(pl.multiple_of(place * width, width), width)
    theirs = pl.ds(pl.multiple_of((1 - place) * width, width), width)
    base[...] = (
        jnp.dot(self_weight[:, mine], features[...], preferred_element_type=F32)
        + jnp.dot(self_weight[:, theirs], others[...], preferred_element_type=F32)
        + lax.dot_general(
            neighbor_weight[:, mine], aggregate[...], (((1,), (1,)), ((), ())),
            preferred_element_type=F32,
        )
        + column(out_bias[...])
    )


def other_part(neighbor_weight, aggregate, base, updated):
    width = aggregate.shape[1]
    place = lax.axis_index("feat")
    theirs = pl.ds(pl.multiple_of((1 - place) * width, width), width)
    combined = base[...] + lax.dot_general(
        neighbor_weight[:, theirs], aggregate[...], (((1,), (1,)), ((), ())),
        preferred_element_type=F32,
    )
    updated[...] = jnp.maximum(combined, 0.0).astype(BF16)


def shards(
    features, in_degree, send_rows, send_count, hub_owner, hub_rows,
    local_dest, local_source, local_tiles, border_dest, border_source, border_tiles,
    hub_dest, hub_source, hub_tiles, self_weight, neighbor_weight, out_bias,
):
    width, vertices = features.shape
    count, tile, _ = local_tiles.shape
    parts, feats = lax.axis_size("dom"), lax.axis_size("feat")
    cap = send_rows.shape[2]
    blocks = hub_owner.shape[0]
    steps = parts.bit_length() - 1
    border, hub = parts * cap // 2, blocks * tile // 2
    like = lambda *shape, kind=BF16: jax.ShapeDtypeStruct(shape, kind)
    products = pltpu.VMEM((count, tile, width), F32)
    work = 2 * count * tile * tile * width

    def swap(x, k):
        return lax.ppermute(x, "dom", [(i, i ^ (1 << k)) for i in range(parts)])

    if feats == 2:
        others = lax.ppermute(features, "feat", [(0, 1), (1, 0)])
    keep, message, held = call(
        pick,
        (like(border, width), like(border + hub, width), like(hub, width)),
        [SM, VM, VM, VM, VM],
        [pltpu.VMEM((2 * (border + hub), width), BF16)],
        name="pick",
    )(hub_owner, features, send_rows, send_count, hub_rows)
    total, degree = call(
        local_terms, (like(vertices, width, kind=F32), like(vertices, 1, kind=F32)),
        [SM, SM, VM, VM, VM], [products], flops=work, size=local_tiles.size * 2, name="local",
    )(local_dest, local_source, features, local_tiles, in_degree.reshape(1, vertices))
    for k in range(steps):
        received = swap(message, k)
        last = k == steps - 1
        outs = (
            (like(2 * border, width), like(hub, width))
            if last
            else (like(border, width), like(border + hub, width))
        )
        keep, message = call(
            functools.partial(step, k, parts, cap, last), outs, [VM, VM, VM], name=f"step{k}"
        )(keep, held, received)
        held = message
    theirs = swap(message, 0)
    total = call(
        border_terms, like(vertices, width, kind=F32), [SM, SM, VM, VM, VM], [products],
        flops=work, size=border_tiles.size * 2, name="border",
    )(border_dest, border_source, keep, border_tiles, total)
    aggregate = call(
        hub_terms, like(vertices, width), [SM, SM, VM, VM, VM, VM, VM],
        [pltpu.VMEM((2 * hub, width), BF16), pltpu.VMEM((vertices, width), F32), products],
        flops=work, size=hub_tiles.size * 2, name="hub",
    )(hub_dest, hub_source, message, theirs, hub_tiles, total, degree)
    outputs = self_weight.shape[0]
    if feats == 2:
        arrived = lax.ppermute(aggregate, "feat", [(0, 1), (1, 0)])
        base = call(
            own_part, like(outputs, vertices, kind=F32), [VM] * 6,
            flops=6 * outputs * width * vertices, size=features.size * 4, name="own",
        )(self_weight, neighbor_weight, out_bias.reshape(1, outputs), features, others, aggregate)
        return call(other_part, like(outputs, vertices), [VM] * 3, name="other")(
            neighbor_weight, arrived, base
        )
    everyone = lax.all_gather(features, "feat", axis=0, tiled=True)
    gathered = lax.all_gather(aggregate, "feat", axis=1, tiled=True)
    combined = (
        jnp.dot(self_weight, everyone, preferred_element_type=F32)
        + jnp.einsum("of,vf->ov", neighbor_weight, gathered, preferred_element_type=F32)
        + out_bias[:, None]
    )
    return jnp.maximum(combined, 0.0).astype(BF16)


def solution(mesh):
    dom, feat = P("dom"), P("feat")
    whole = P("dom", None, None)
    placed = (
        P("feat", "dom"), dom, whole, P("dom", None), P(), P(),
        dom, dom, whole, dom, dom, whole, dom, dom, whole,
        P("feat", None), P("feat", None), feat,
    )
    return jax.shard_map(
        shards, mesh=mesh, in_specs=placed, out_specs=P("feat", "dom"), check_vma=False
    )
```

time: 81.3 us -> 35.4 us (0.44)
  between operations: 13.7 us -> 0.17 us
  blocking collectives: 13 us -> 0 us
  waiting for transfers between devices: 25.4 us -> 14.3 us
  local copies, waits for them, and re-layouts: 14 us -> 5.23 us
  matrix products: 5.74 us -> 0 us
  Pallas kernels: 0 us -> 5.05 us
  starting transfers between devices: 7.43 us -> 10.4 us
  other arithmetic: 1.48 us -> 0 us
    all_gather x1 -> x0, waiting for transfers between devices: 25.4 us -> none  [shards(): everyone = lax.all_gather(owned_blocks, 'dom', axis=1, tiled=True)]
    ppermute x0 -> x7, waiting for transfers between devices: none -> 14.3 us  [the longest x5 9.59 us: swap(): return lax.ppermute(x, 'dom', [(i, i ^ 1 << k) for i in range(parts)])]
    all_gather x2 -> x0, blocking collectives: 13 us -> none  [the longest x1 6.51 us: shards(): lax.all_gather(features, 'feat', axis=0, tiled=True)]
    ppermute x0 -> x7, starting transfers between devices: none -> 10.4 us  [the longest x5 8.26 us: swap(): return lax.ppermute(x, 'dom', [(i, i ^ 1 << k) for i in range(parts)])]
    all_to_all x1 -> x0, starting transfers between devices: 7.38 us -> none  [shards(): lax.all_to_all(outgoing, 'dom', split_axis=1, concat_axis=1, tiled=True)]
    dot_general x8 -> x0, matrix products: 5.74 us -> none  [the longest x3 3.16 us: tile_terms(): jnp.einsum('fti,tr->fri', partial_value, onehot, precision=lax.Precision....]
    gather x6 -> x0, local copies, waits for them, and re-layouts: 5.45 us -> none  [the longest x3 1.94 us: tile_terms(): picked = jnp.take(blocks, source, axis=1)]
    pallas_call x0 -> x10, Pallas kernels: none -> 5.05 us  [the longest x1 1.08 us: shards(): call(pick, (like(border, width), like(border + hub, width), like(hub, wid...]
  transfers between devices with their start and end apart: 2 -> 7, of which waited for: 1 -> 5; matrix products, arithmetic and copies ran while one was open for 8% -> 0% of each run, Pallas kernels for 0% -> 9%
where the time goes in v1:
time: 35.4 us; the launch traced here: 35.2 us
  waiting for transfers between devices  14.3 us (40%)
  starting transfers between devices  10.4 us (29%)
  local copies, waits for them, and re-layouts  5.23 us (15%)
  Pallas kernels  5.05 us (14%)
    ppermute x5, waiting for transfers between devices, swap(): return lax.ppermute(x, 'dom', [(i, i ^ 1 << k) for i in range(parts)])  9.59 us
    ppermute x5, starting transfers between devices, swap(): return lax.ppermute(x, 'dom', [(i, i ^ 1 << k) for i in range(parts)])  8.26 us
    unnamed x38, local copies, waits for them, and re-layouts  5.23 us
    ppermute x1, waiting for transfers between devices, shards(): arrived = lax.ppermute(aggregate, 'feat', [(0, 1), (1, 0)])  4.72 us
    ppermute x1, starting transfers between devices, shards(): others = lax.ppermute(features, 'feat', [(0, 1), (1, 0)])  1.79 us
    pallas_call x1, Pallas kernels, shards(): call(pick, (like(border, width), like(border + hub, width), like(hub, wid...  1.08 us
    pallas_call x1, Pallas kernels, shards(): call(local_terms, (like(vertices, width, kind=F32), like(vertices, 1, kin...  1.03 us
    pallas_call x1, Pallas kernels, shards(): call(hub_terms, like(vertices, width), [SM, SM, VM, VM, VM, VM, VM], [plt...  0.9 us
  transfers between devices with their start and end apart: 7, of which 5 were waited for; matrix products, arithmetic and copies ran while one was open for 0% of the time, Pallas kernels for 9%

profile of v1, /device:TPU:0, one launch (start us, length us, event | category | flops | bytes accessed | tf_op | source)
XLA Modules:
  0.0 35.2 jit_solution(5116850317851563691)
XLA Ops:
  0.0 0.9 %copy-done = bf16[128,512]{1,0:T(8,128)(2,1)S(1)} copy-done((bf16[128,512]{1,0:T(8,128)(2,1)S(1)}, bf16[128,512]{1,0:T(8,128)(2,1)}, u32[]{:S(2)}) %copy-start) | copy-done | bytes 131096
  0.9 0.7 %copy-done.7 = s32[1,16,16]{2,1,0:T(8,128)S(1)} copy-done((s32[1,16,16]{2,1,0:T(8,128)S(1)}, s32[1,16,16]{2,1,0:T(8,128)}, u32[]{:S(2)}) %copy-start.7) | copy-done | bytes 1048
  1.6 0.7 %copy-done.8 = s32[4,128]{1,0:T(4,128)S(1)} copy-done((s32[4,128]{1,0:T(4,128)S(1)}, s32[4,128]{1,0:T(4,128)}, u32[]{:S(2)}) %copy-start.8) | copy-done | bytes 2072
  2.3 0.7 %copy-done.12 = s32[4]{0:T(128)S(1)} copy-done((s32[4]{0:T(128)S(1)}, s32[4]{0:T(128)}, u32[]{:S(2)}) %copy-start.12) | copy-done | bytes 40
  2.9 0.7 %copy-done.13 = s32[1,16]{1,0:T(1,128)S(1)} copy-done((s32[1,16]{1,0:T(1,128)S(1)}, s32[1,16]{1,0:T(1,128)}, u32[]{:S(2)}) %copy-start.13) | copy-done | bytes 88
  3.6 1.1 %pick.1 = (bf16[128,128]{1,0:T(8,128)(2,1)S(1)}, bf16[384,128]{1,0:T(8,128)(2,1)S(1)}, bf16[256,128]{1,0:T(8,128)(2,1)S(1)}) custom-call(s32[4]{0:T(128)S(1)} %copy-done.12, bf16[128,512]{1,0:T(8,128)(2,1)S(1)} %copy-done, s32[1,16,16]{2,1,0:T(8,128)S(1)} %copy-done.7, s32[1,16]{1,0:T(1,128)S(1)} %copy-done.13, s32[4,128]{1,0:T(4,128)S(1)} %copy-done.8), custom_call_target="tpu_custom_call" | custom-call | tf_op jit(solution)/shard_map/pick/pallas_call | solution.py:207
  4.7 0.5 %collective-permute-start = (bf16[384,128]{1,0:T(8,128)(2,1)S(1)}, bf16[384,128]{1,0:T(8,128)(2,1)S(1)}, u32[]{:S(2)}, u32[]{:S(2)}) collective-permute-start(bf16[384,128]{1,0:T(8,128)(2,1)S(1)} %get-tuple-element.20), channel_id=1, source_target_pairs={{0,2},{2,0},{4,6},{6,4},{8,10},{10,8},{12,14},{14,12},{16,18},{18,... | collective-permute-start | bytes 294920 | tf_op jit(solution)/shard_map/ppermute | solution.py:203
  5.2 0.9 %collective-permute-done.received = bf16[384,128]{1,0:T(8,128)(2,1)S(1)} collective-permute-done((bf16[384,128]{1,0:T(8,128)(2,1)S(1)}, bf16[384,128]{1,0:T(8,128)(2,1)S(1)}, u32[]{:S(2)}, u32[]{:S(2)}) %collective-permute-start) | collective-permute-done | bytes 98336 | tf_op jit(solution)/shard_map/ppermute | solution.py:203
  6.2 2.9 %collective-permute-start.1 = (bf16[384,128]{1,0:T(8,128)(2,1)S(1)}, bf16[384,128]{1,0:T(8,128)(2,1)S(1)}, u32[]{:S(2)}, u32[]{:S(2)}) collective-permute-start(bf16[384,128]{1,0:T(8,128)(2,1)S(1)} %get-tuple-element.22.hub), channel_id=1, source_target_pairs={{0,4},{2,6},{4,0},{6,2},{8,12},{10,14},{12,8},{14,10},{16,20},{18,... | collective-permute-start | bytes 294920 | tf_op jit(solution)/shard_map/ppermute | solution.py:203
  9.1 3.1 %collective-permute-done.1.received = bf16[384,128]{1,0:T(8,128)(2,1)S(1)} collective-permute-done((bf16[384,128]{1,0:T(8,128)(2,1)S(1)}, bf16[384,128]{1,0:T(8,128)(2,1)S(1)}, u32[]{:S(2)}, u32[]{:S(2)}) %collective-permute-start.1) | collective-permute-done | bytes 98336 | tf_op jit(solution)/shard_map/ppermute | solution.py:203
  12.3 1.9 %collective-permute-start.2 = (bf16[384,128]{1,0:T(8,128)(2,1)S(1)}, bf16[384,128]{1,0:T(8,128)(2,1)S(1)}, u32[]{:S(2)}, u32[]{:S(2)}) collective-permute-start(bf16[384,128]{1,0:T(8,128)(2,1)S(1)} %get-tuple-element.24.hub), channel_id=1, source_target_pairs={{0,8},{2,10},{4,12},{6,14},{8,0},{10,2},{12,4},{14,6},{16,24},{18,... | collective-permute-start | bytes 294920 | tf_op jit(solution)/shard_map/ppermute | solution.py:203
  14.1 2.8 %collective-permute-done.2.received = bf16[384,128]{1,0:T(8,128)(2,1)S(1)} collective-permute-done((bf16[384,128]{1,0:T(8,128)(2,1)S(1)}, bf16[384,128]{1,0:T(8,128)(2,1)S(1)}, u32[]{:S(2)}, u32[]{:S(2)}) %collective-permute-start.2) | collective-permute-done | bytes 98336 | tf_op jit(solution)/shard_map/ppermute | solution.py:203
  17.0 0.0 copy-start.1
  17.0 0.0 copy-start.3
  17.0 2.9 %collective-permute-start.3 = (bf16[384,128]{1,0:T(8,128)(2,1)S(1)}, bf16[384,128]{1,0:T(8,128)(2,1)S(1)}, u32[]{:S(2)}, u32[]{:S(2)}) collective-permute-start(bf16[384,128]{1,0:T(8,128)(2,1)S(1)} %get-tuple-element.26.hub), channel_id=1, source_target_pairs={{0,16},{2,18},{4,20},{6,22},{8,24},{10,26},{12,28},{14,30},{16,0},... | collective-permute-start | bytes 294920 | tf_op jit(solution)/shard_map/ppermute | solution.py:203
  19.9 2.7 %collective-permute-done.3.received = bf16[384,128]{1,0:T(8,128)(2,1)S(1)} collective-permute-done((bf16[384,128]{1,0:T(8,128)(2,1)S(1)}, bf16[384,128]{1,0:T(8,128)(2,1)S(1)}, u32[]{:S(2)}, u32[]{:S(2)}) %collective-permute-start.3) | collective-permute-done | bytes 98336 | tf_op jit(solution)/shard_map/ppermute | solution.py:203
  22.6 0.1 collective-permute-start.4
  22.7 1.8 %collective-permute-start.6 = (bf16[128,512]{1,0:T(8,128)(2,1)S(1)}, bf16[128,512]{1,0:T(8,128)(2,1)S(1)}, u32[]{:S(2)}, u32[]{:S(2)}) collective-permute-start(bf16[128,512]{1,0:T(8,128)(2,1)S(1)} %copy-done.1), channel_id=1, source_target_pairs={{0,1},{1,0},{2,3},{3,2},{4,5},{5,4},{6,7},{7,6},{8,9},{9,8},{10,11... | collective-permute-start | bytes 393224 | tf_op jit(solution)/shard_map/ppermute | solution.py:206
  24.5 1.0 %local.1 = (f32[512,128]{1,0:T(8,128)S(1)}, f32[512,1]{1,0:T(8,128)S(1)}) custom-call(s32[16]{0:T(128)S(1)} %copy-done.14, s32[16]{0:T(128)S(1)} %copy-done.15, bf16[128,512]{1,0:T(8,128)(2,1)S(1)} %copy-done.1, bf16[16,128,128]{2,1,0:T(8,128)(2,1)S(1)} %copy-done.2, s32[1,512]{1,0:T(1,128)S(1)} %bitcast.2), custom_call_target="tpu_custom_call" | custom-call | flops 67108864 | bytes 524288 | tf_op jit(solution)/shard_map/local/pallas_call | solution.py:214
  25.6 0.6 %copy-done.10 = s32[16]{0:T(128)S(1)} copy-done((s32[16]{0:T(128)S(1)}, s32[16]{0:T(128)}, u32[]{:S(2)}) %copy-start.10) | copy-done | bytes 88
  26.2 0.0 copy-done.11
  26.2 0.8 %border.1.before = f32[512,128]{1,0:T(8,128)S(1)} custom-call(s32[16]{0:T(128)S(1)} %copy-done.10, s32[16]{0:T(128)S(1)} %copy-done.11, bf16[256,128]{1,0:T(8,128)(2,1)S(1)} %get-tuple-element.28.lists, bf16[16,128,128]{2,1,0:T(8,128)(2,1)S(1)} %copy-done.3, f32[512,128]{1,0:T(8,128)S(1)} %get-tuple-element.29.before), custom_call_target="tpu_custom_call" | custom-call | flops 67108864 | bytes 524288 | tf_op jit(solution)/shard_map/border/pallas_call | solution.py:231
  27.1 0.1 copy-done.4
  27.3 0.5 %copy-done.16 = s32[16]{0:T(128)S(1)} copy-done((s32[16]{0:T(128)S(1)}, s32[16]{0:T(128)}, u32[]{:S(2)}) %copy-start.16) | copy-done | bytes 88
  27.8 0.0 copy-done.17
  27.8 0.9 %hub.1.aggregate = bf16[512,128]{1,0:T(8,128)(2,1)S(1)} custom-call(s32[16]{0:T(128)S(1)} %copy-done.16, s32[16]{0:T(128)S(1)} %copy-done.17, bf16[256,128]{1,0:T(8,128)(2,1)S(1)} %get-tuple-element.27.mine, bf16[256,128]{1,0:T(8,128)(2,1)S(1)} %collective-permute-done.4.theirs, bf16[16,128,128]{2,1,0:T(8,128)(2,1)S(1)} %copy-done.4, ...), custom_call_target="tpu_custom_call" | custom-call | flops 67108864 | bytes 524288 | tf_op jit(solution)/shard_map/hub/pallas_call | solution.py:235
  28.7 0.0 copy-start.18
  28.7 0.4 %collective-permute-start.5 = (bf16[512,128]{1,0:T(8,128)(2,1)S(1)}, bf16[512,128]{1,0:T(8,128)(2,1)S(1)}, u32[]{:S(2)}, u32[]{:S(2)}) collective-permute-start(bf16[512,128]{1,0:T(8,128)(2,1)S(1)} %hub.1.aggregate), channel_id=1, source_target_pairs={{0,1},{1,0},{2,3},{3,2},{4,5},{5,4},{6,7},{7,6},{8,9},{9,8},{10,11... | collective-permute-start | bytes 393224 | tf_op jit(solution)/shard_map/ppermute | solution.py:242
  29.1 0.3 copy-done.18
  29.4 0.3 own.1.base
  29.6 4.7 %collective-permute-done.5.aggregate = bf16[512,128]{1,0:T(8,128)(2,1)S(1)} collective-permute-done((bf16[512,128]{1,0:T(8,128)(2,1)S(1)}, bf16[512,128]{1,0:T(8,128)(2,1)S(1)}, u32[]{:S(2)}, u32[]{:S(2)}) %collective-permute-start.5) | collective-permute-done | bytes 131104 | tf_op jit(solution)/shard_map/ppermute | solution.py:242
  34.3 0.8 %other.1 = bf16[128,512]{1,0:T(8,128)(2,1)} custom-call(bf16[128,256]{1,0:T(8,128)(2,1)S(1)} %copy-done.5, bf16[512,128]{1,0:T(8,128)(2,1)S(1)} %collective-permute-done.5.aggregate, f32[128,512]{1,0:T(8,128)S(1)} %own.1.base), custom_call_target="tpu_custom_call" | custom-call | tf_op jit(solution)/shard_map/other/pallas_call | solution.py:247
  (30 shorter events, 0.2 us)
Async XLA Ops:
  0.0 0.9 %copy-start = (bf16[128,512]{1,0:T(8,128)(2,1)S(1)}, bf16[128,512]{1,0:T(8,128)(2,1)}, u32[]{:S(2)}) copy-start(bf16[128,512]{1,0:T(8,128)(2,1)} %features.5) | copy-start | bytes 393220
  0.9 0.7 %copy-start.7 = (s32[1,16,16]{2,1,0:T(8,128)S(1)}, s32[1,16,16]{2,1,0:T(8,128)}, u32[]{:S(2)}) copy-start(s32[1,16,16]{2,1,0:T(8,128)} %send_rows.1) | copy-start | bytes 3076
  1.6 0.7 %copy-start.8 = (s32[4,128]{1,0:T(4,128)S(1)}, s32[4,128]{1,0:T(4,128)}, u32[]{:S(2)}) copy-start(s32[4,128]{1,0:T(4,128)} %hub_rows.1) | copy-start | bytes 6148
  2.3 0.7 %copy-start.12 = (s32[4]{0:T(128)S(1)}, s32[4]{0:T(128)}, u32[]{:S(2)}) copy-start(s32[4]{0:T(128)} %owner.1) | copy-start | bytes 52
  2.9 0.7 %copy-start.13 = (s32[1,16]{1,0:T(1,128)S(1)}, s32[1,16]{1,0:T(1,128)}, u32[]{:S(2)}) copy-start(s32[1,16]{1,0:T(1,128)} %send_count.1) | copy-start | bytes 196
  3.6 20.9 %copy-start.2 = (bf16[16,128,128]{2,1,0:T(8,128)(2,1)S(1)}, bf16[16,128,128]{2,1,0:T(8,128)(2,1)}, u32[]{:S(2)}) copy-start(bf16[16,128,128]{2,1,0:T(8,128)(2,1)} %tiles.3) | copy-start | bytes 1572868
  4.7 1.5 %collective-permute-start = (bf16[384,128]{1,0:T(8,128)(2,1)S(1)}, bf16[384,128]{1,0:T(8,128)(2,1)S(1)}, u32[]{:S(2)}, u32[]{:S(2)}) collective-permute-start(bf16[384,128]{1,0:T(8,128)(2,1)S(1)} %get-tuple-element.20), channel_id=1, source_target_pairs={{0,2},{2,0},{4,6},{6,4},{8,10},{10,8},{12,14},{14,12},{16,18},{18,... | collective-permute-start | bytes 294920 | tf_op jit(solution)/shard_map/ppermute | solution.py:203
  6.2 6.0 %collective-permute-start.1 = (bf16[384,128]{1,0:T(8,128)(2,1)S(1)}, bf16[384,128]{1,0:T(8,128)(2,1)S(1)}, u32[]{:S(2)}, u32[]{:S(2)}) collective-permute-start(bf16[384,128]{1,0:T(8,128)(2,1)S(1)} %get-tuple-element.22.hub), channel_id=1, source_target_pairs={{0,4},{2,6},{4,0},{6,2},{8,12},{10,14},{12,8},{14,10},{16,20},{18,... | collective-permute-start | bytes 294920 | tf_op jit(solution)/shard_map/ppermute | solution.py:203
  12.3 4.7 %collective-permute-start.2 = (bf16[384,128]{1,0:T(8,128)(2,1)S(1)}, bf16[384,128]{1,0:T(8,128)(2,1)S(1)}, u32[]{:S(2)}, u32[]{:S(2)}) collective-permute-start(bf16[384,128]{1,0:T(8,128)(2,1)S(1)} %get-tuple-element.24.hub), channel_id=1, source_target_pairs={{0,8},{2,10},{4,12},{6,14},{8,0},{10,2},{12,4},{14,6},{16,24},{18,... | collective-permute-start | bytes 294920 | tf_op jit(solution)/shard_map/ppermute | solution.py:203
  16.9 7.5 %copy-start.9 = (s32[512]{0:T(512)S(1)}, s32[512]{0:T(512)}, u32[]{:S(2)}) copy-start(s32[512]{0:T(512)} %param.19) | copy-start | bytes 6148
  16.9 7.5 %copy-start.14 = (s32[16]{0:T(128)S(1)}, s32[16]{0:T(128)}, u32[]{:S(2)}) copy-start(s32[16]{0:T(128)} %dest.3) | copy-start | bytes 196
  16.9 7.5 %copy-start.15 = (s32[16]{0:T(128)S(1)}, s32[16]{0:T(128)}, u32[]{:S(2)}) copy-start(s32[16]{0:T(128)} %source.3) | copy-start | bytes 196
  17.0 5.7 %copy-start.1 = (bf16[128,512]{1,0:T(8,128)(2,1)S(1)}, bf16[128,512]{1,0:T(8,128)(2,1)}, u32[]{:S(2)}) copy-start(bf16[128,512]{1,0:T(8,128)(2,1)} %features.5) | copy-start | bytes 393220
  17.0 8.6 %copy-start.3 = (bf16[16,128,128]{2,1,0:T(8,128)(2,1)S(1)}, bf16[16,128,128]{2,1,0:T(8,128)(2,1)}, u32[]{:S(2)}) copy-start(bf16[16,128,128]{2,1,0:T(8,128)(2,1)} %tiles.4) | copy-start | bytes 1572868
  17.0 5.6 %collective-permute-start.3 = (bf16[384,128]{1,0:T(8,128)(2,1)S(1)}, bf16[384,128]{1,0:T(8,128)(2,1)S(1)}, u32[]{:S(2)}, u32[]{:S(2)}) collective-permute-start(bf16[384,128]{1,0:T(8,128)(2,1)S(1)} %get-tuple-element.26.hub), channel_id=1, source_target_pairs={{0,16},{2,18},{4,20},{6,22},{8,24},{10,26},{12,28},{14,30},{16,0},... | collective-permute-start | bytes 294920 | tf_op jit(solution)/shard_map/ppermute | solution.py:203
  22.6 4.5 %collective-permute-start.4 = (bf16[256,128]{1,0:T(8,128)(2,1)S(1)}, bf16[256,128]{1,0:T(8,128)(2,1)S(1)}, u32[]{:S(2)}, u32[]{:S(2)}) collective-permute-start(bf16[256,128]{1,0:T(8,128)(2,1)S(1)} %get-tuple-element.27.mine), channel_id=1, source_target_pairs={{0,2},{2,0},{4,6},{6,4},{8,10},{10,8},{12,14},{14,12},{16,18},{18,... | collective-permute-start | bytes 196616 | tf_op jit(solution)/shard_map/ppermute | solution.py:203
  22.7 6.4 %collective-permute-start.6 = (bf16[128,512]{1,0:T(8,128)(2,1)S(1)}, bf16[128,512]{1,0:T(8,128)(2,1)S(1)}, u32[]{:S(2)}, u32[]{:S(2)}) collective-permute-start(bf16[128,512]{1,0:T(8,128)(2,1)S(1)} %copy-done.1), channel_id=1, source_target_pairs={{0,1},{1,0},{2,3},{3,2},{4,5},{5,4},{6,7},{7,6},{8,9},{9,8},{10,11... | collective-permute-start | bytes 393224 | tf_op jit(solution)/shard_map/ppermute | solution.py:206
  25.5 0.7 %copy-start.10 = (s32[16]{0:T(128)S(1)}, s32[16]{0:T(128)}, u32[]{:S(2)}) copy-start(s32[16]{0:T(128)} %dest.4) | copy-start | bytes 196
  25.5 0.7 %copy-start.11 = (s32[16]{0:T(128)S(1)}, s32[16]{0:T(128)}, u32[]{:S(2)}) copy-start(s32[16]{0:T(128)} %source.4) | copy-start | bytes 196
  26.2 1.0 %copy-start.4 = (bf16[16,128,128]{2,1,0:T(8,128)(2,1)S(1)}, bf16[16,128,128]{2,1,0:T(8,128)(2,1)}, u32[]{:S(2)}) copy-start(bf16[16,128,128]{2,1,0:T(8,128)(2,1)} %tiles.5) | copy-start | bytes 1572868
  27.1 0.7 %copy-start.16 = (s32[16]{0:T(128)S(1)}, s32[16]{0:T(128)}, u32[]{:S(2)}) copy-start(s32[16]{0:T(128)} %dest.5) | copy-start | bytes 196
  27.1 0.7 %copy-start.17 = (s32[16]{0:T(128)S(1)}, s32[16]{0:T(128)}, u32[]{:S(2)}) copy-start(s32[16]{0:T(128)} %source.5) | copy-start | bytes 196
  27.8 1.3 %copy-start.5 = (bf16[128,256]{1,0:T(8,128)(2,1)S(1)}, bf16[128,256]{1,0:T(8,128)(2,1)}, u32[]{:S(2)}) copy-start(bf16[128,256]{1,0:T(8,128)(2,1)} %neighbor_weight.3) | copy-start | bytes 196612
  27.8 1.3 %copy-start.6 = (bf16[128,256]{1,0:T(8,128)(2,1)S(1)}, bf16[128,256]{1,0:T(8,128)(2,1)}, u32[]{:S(2)}) copy-start(bf16[128,256]{1,0:T(8,128)(2,1)} %self_weight.1) | copy-start | bytes 196612
  28.7 0.7 %copy-start.18 = (f32[128]{0:T(128)S(1)}, f32[128]{0:T(128)}, u32[]{:S(2)}) copy-start(f32[128]{0:T(128)} %param.35) | copy-start | bytes 1540
  28.7 5.6 %collective-permute-start.5 = (bf16[512,128]{1,0:T(8,128)(2,1)S(1)}, bf16[512,128]{1,0:T(8,128)(2,1)S(1)}, u32[]{:S(2)}, u32[]{:S(2)}) collective-permute-start(bf16[512,128]{1,0:T(8,128)(2,1)S(1)} %hub.1.aggregate), channel_id=1, source_target_pairs={{0,1},{1,0},{2,3},{3,2},{4,5},{5,4},{6,7},{7,6},{8,9},{9,8},{10,11... | collective-permute-start | bytes 393224 | tf_op jit(solution)/shard_map/ppermute | solution.py:242

commit v2 on v1

v2 whole, which is shorter than its diff:
```python
import functools

import jax
import jax.numpy as jnp
from jax import lax
from jax.experimental import pallas as pl
from jax.experimental.pallas import tpu as pltpu
from jax.sharding import PartitionSpec as P

BF16 = jnp.bfloat16
F32 = jnp.float32
VM = pl.BlockSpec(memory_space=pltpu.VMEM)
ANY = pl.BlockSpec(memory_space=pl.ANY)
HBM = pl.BlockSpec(memory_space=pltpu.HBM)
LAST = (((1,), (1,)), ((), ()))
FIRST_LAST = (((0,), (1,)), ((), ()))


def call(body, outs, specs, scratch=(), flops=0, size=0, name=None):
    return pl.pallas_call(
        body,
        out_shape=outs,
        in_specs=specs,
        out_specs=jax.tree.map(lambda _: VM, outs),
        scratch_shapes=scratch,
        compiler_params=pltpu.CompilerParams(vmem_limit_bytes=40 << 20),
        cost_estimate=pl.CostEstimate(flops=flops, bytes_accessed=size, transcendentals=0),
        name=name,
    )


def dot(a, b, contract=(((1,), (0,)), ((), ()))):
    return lax.dot_general(a, b, contract, preferred_element_type=F32)


def rows(start, size):
    return pl.ds(pl.multiple_of(start, size), size)


def column(row):
    m = row.shape[1]
    down = lax.broadcasted_iota(jnp.int32, (m, m), 0)
    across = lax.broadcasted_iota(jnp.int32, (m, m), 1)
    return jnp.sum(jnp.where(down == across, row, jnp.zeros_like(row)), axis=1, keepdims=True)


def fetch(pairs, sems):
    copies = [pltpu.make_async_copy(a, b, sems.at[i]) for i, (a, b) in enumerate(pairs)]
    for copy in copies:
        copy.start()
    return copies


def choose(owner_h, lists_h, count_h, hubs_h, choice, owner, lists, count, hubs, sems):
    for copy in fetch(
        [(owner_h, owner), (lists_h, lists), (count_h, count), (hubs_h, hubs)], sems
    ):
        copy.wait()
    me = lax.axis_index("dom")
    bit = me & 1
    parts, cap = lists.shape[1:]
    blocks, tile = hubs.shape
    vertices = choice.shape[1]
    shape = (parts, cap, cap)
    slot = lax.broadcasted_iota(jnp.int32, shape, 1)
    across = lax.broadcasted_iota(jnp.int32, shape, 2)
    index = jnp.sum(jnp.where(slot == across, lists[0][:, None, :], 0), axis=2, keepdims=True)
    shape = (parts, cap, parts)
    target = lax.broadcasted_iota(jnp.int32, shape, 0)
    across = lax.broadcasted_iota(jnp.int32, shape, 2)
    live = jnp.sum(jnp.where(target == across, count[...][None], 0), axis=2, keepdims=True)
    slot = lax.broadcasted_iota(jnp.int32, (parts, cap, 1), 1)
    index = jnp.where(slot < live, index, -1)

    def onehot(index):
        vertex = lax.broadcasted_iota(jnp.int32, (index.shape[0], vertices), 1)
        return (vertex == index).astype(F32).astype(BF16)

    for part in range(parts):
        place = (part >> 1) + ((part & 1) ^ bit) * (parts // 2)
        choice[rows(place * cap, cap), :] = onehot(index[part])
    pairs = (blocks + 1) // 2
    for b in range(2 * pairs):
        place = (b >> 1) + (1 - ((b & 1) ^ bit)) * pairs
        there = pl.ds(pl.multiple_of(parts * cap + place * tile, cap), tile)
        if b < blocks:
            mine = jnp.where(owner[b] == me, hubs[b : b + 1, :], -1)
            choice[there, :] = onehot(column(mine))
        else:
            choice[there, :] = jnp.zeros((tile, vertices), BF16)


def weight_parts(weight, feature_blocks):
    if len(feature_blocks) == 1:
        return [(weight[...], feature_blocks[0][...])]
    width = feature_blocks[0].shape[0]
    place = lax.axis_index("feat")
    return [
        (weight[:, rows(p * width, width)], block[...])
        for p, block in zip((place, 1 - place), feature_blocks)
    ]


def pick(border, hub, weight, choice, *refs):
    *feature_blocks, projected, keep, message, held = refs
    total = sum(dot(w, f) for w, f in weight_parts(weight, feature_blocks)).astype(BF16)
    projected[...] = total
    picked = dot(choice[...], total, LAST).astype(BF16)
    keep[...] = picked[:border]
    message[...] = picked[border : 2 * border + hub]
    held[...] = picked[2 * border + hub :]


def step(k, parts, cap, last, keep, hub, received, *outs):
    me = lax.axis_index("dom")
    bit = (me >> k) & 1
    border = parts * cap // 2
    merged = hub[hub.shape[0] - (received.shape[0] - border) :, :] + received[border:, :]
    run = (1 << k) * cap
    first, second = outs[-2:]
    if last:
        first[rows(bit * run, run), :] = keep[...]
        first[rows((1 - bit) * run, run), :] = received[:border, :]
        first[2 * border :, :] = merged
        second[...] = merged
        return
    ahead = (me >> (k + 1)) & 1
    for pair in range(parts >> (k + 2)):
        stay, go = rows((2 * pair + ahead) * run, run), rows((2 * pair + 1 - ahead) * run, run)
        mine, theirs = rows((2 * pair + bit) * run, run), rows((2 * pair + 1 - bit) * run, run)
        first[mine, :] = keep[stay, :]
        first[theirs, :] = received[stay, :]
        second[mine, :] = keep[go, :]
        second[theirs, :] = received[go, :]
    second[border:, :] = merged


def adjacency(kinds, degree_h, *refs):
    inputs, rest = refs[:9], refs[10:]
    local_high, local_low, far_high, far_low = rest[:4]
    degree, dests, sources, tiles, near, far, sems = rest[4:]
    copies = []
    for i in range(3):
        copies.append(
            fetch(
                [
                    (inputs[3 * i], dests.at[i]),
                    (inputs[3 * i + 1], sources.at[i]),
                    (inputs[3 * i + 2], tiles.at[i]),
                ],
                sems.at[i],
            )
        )
    whole = pltpu.make_async_copy(degree_h, degree, sems.at[3, 0])
    whole.start()
    bit = lax.axis_index("dom") & 1
    count, tile = tiles.shape[1:3]
    near[...] = jnp.zeros_like(near)
    far[...] = jnp.zeros_like(far)
    border, pairs = kinds
    for i in range(3):
        for copy in copies[i]:
            copy.wait()
        sums = far if i else near
        for t in range(count):
            source = sources[i, t]
            if i == 2:
                source = border + (source >> 1) + ((source & 1) ^ bit) * pairs
            there = (rows(dests[i, t] * tile, tile), rows(source * tile, tile))
            sums[there] = sums[there] + tiles[i, t].astype(F32)
    whole.wait()
    for r in range(near.shape[0] // tile):
        there = slice(r * tile, (r + 1) * tile)
        below = column(degree[:, there].astype(F32))
        for sums, high, low in ((near, local_high, local_low), (far, far_high, far_low)):
            mean = sums[there, :] / below
            top = mean.astype(BF16)
            high[there, :] = top
            low[there, :] = (mean - top.astype(F32)).astype(BF16)


def own_terms(local_high, local_low, projected, weight, bias, *refs):
    *feature_blocks, _, total = refs
    total[...] = (
        sum(dot(f, w, FIRST_LAST) for w, f in weight_parts(weight, feature_blocks))
        + dot(local_high[...], projected[...], LAST)
        + dot(local_low[...], projected[...], LAST)
        + bias[...]
    )


def far_terms(high, low, near, before, total):
    known = near.shape[0]
    total[...] = (
        before[...] + dot(high[:, :known], near[...]) + dot(low[:, :known], near[...])
    )


def finish(high, low, theirs, before, updated):
    known = high.shape[1] - theirs.shape[0]
    total = before[...] + dot(high[:, known:], theirs[...]) + dot(low[:, known:], theirs[...])
    updated[...] = jnp.maximum(total, 0.0).astype(BF16).T


def shards(
    features, in_degree, send_rows, send_count, hub_owner, hub_rows,
    local_dest, local_source, local_tiles, border_dest, border_source, border_tiles,
    hub_dest, hub_source, hub_tiles, self_weight, neighbor_weight, out_bias,
):
    vertices = features.shape[1]
    count, tile, _ = local_tiles.shape
    width = self_weight.shape[0]
    parts, feats = lax.axis_size("dom"), lax.axis_size("feat")
    cap = send_rows.shape[2]
    blocks = hub_owner.shape[0]
    steps = parts.bit_length() - 1
    pairs = (blocks + 1) // 2
    border, hub = parts * cap // 2, pairs * tile
    near_size, far_size = vertices, 2 * border + 2 * hub

    def like(*shape, kind=BF16):
        return jax.ShapeDtypeStruct(shape, kind)

    def swap(x, k):
        return lax.ppermute(x, "dom", [(i, i ^ (1 << k)) for i in range(parts)])

    if feats == 2:
        feature_blocks = [features, lax.ppermute(features, "feat", [(0, 1), (1, 0)])]
    else:
        feature_blocks = [lax.all_gather(features, "feat", axis=0, tiled=True)]
    choice = call(
        choose, like(2 * (border + hub), vertices), [HBM] * 4,
        [
            pltpu.SMEM(hub_owner.shape, jnp.int32),
            pltpu.VMEM(send_rows.shape, jnp.int32),
            pltpu.VMEM(send_count.shape, jnp.int32),
            pltpu.VMEM(hub_rows.shape, jnp.int32),
            pltpu.SemaphoreType.DMA((4,)),
        ],
        size=2 << 20, name="choose",
    )(hub_owner, send_rows, send_count, hub_rows)
    projected, keep, message, held = call(
        functools.partial(pick, border, hub),
        (like(width, vertices), like(border, width), like(border + hub, width), like(hub, width)),
        [VM] * (2 + len(feature_blocks)),
        size=1 << 20, name="pick",
    )(neighbor_weight, choice, *feature_blocks)
    inputs = (
        local_dest, local_source, local_tiles, border_dest, border_source, border_tiles,
        hub_dest, hub_source, hub_tiles,
    )
    waits = None
    for k in range(steps):
        received = swap(message, k)
        last = k == steps - 1
        specs, operands = [VM, VM, VM], (keep, held, received)
        body = functools.partial(step, k, parts, cap, last)
        if waits is not None:
            specs, operands = specs + [ANY], operands + (waits,)
            body = functools.partial(
                lambda inner, a, b, c, _, *outs: inner(a, b, c, *outs), body
            )
        outs = (
            (like(2 * border + hub, width), like(hub, width))
            if last
            else (like(border, width), like(border + hub, width))
        )
        keep, message = call(body, outs, specs, name=f"step{k}")(*operands)
        held = message
        waits = None
        if k == 0:
            local_high, local_low, far_high, far_low = call(
                functools.partial(adjacency, (2 * border // tile, pairs)),
                (like(vertices, near_size),) * 2 + (like(vertices, far_size),) * 2,
                [HBM] * 10 + [ANY],
                [
                    pltpu.VMEM((1, vertices), jnp.int32),
                    pltpu.SMEM((3, count), jnp.int32),
                    pltpu.SMEM((3, count), jnp.int32),
                    pltpu.VMEM((3, count, tile, tile), BF16),
                    pltpu.VMEM((vertices, near_size), F32),
                    pltpu.VMEM((vertices, far_size), F32),
                    pltpu.SemaphoreType.DMA((4, 3)),
                ],
                size=6 << 20, name="adjacency",
            )(in_degree.reshape(1, vertices), *inputs, message)
            waits = far_low
        if k == 1:
            total = call(
                own_terms, like(vertices, width, kind=F32),
                [VM] * (5 + len(feature_blocks)) + [ANY],
                flops=4 * vertices * width * (near_size + width), size=2 << 20, name="own",
            )(
                local_high, local_low, projected, self_weight, out_bias.reshape(1, width),
                *feature_blocks, message,
            )
            waits = total
    theirs = swap(message, 0)
    total = call(
        far_terms, like(vertices, width, kind=F32), [VM] * 4,
        flops=4 * vertices * width * (far_size - hub), size=2 << 20, name="far",
    )(far_high, far_low, keep, total)
    return call(finish, like(width, vertices), [VM] * 4, size=1 << 20, name="finish")(
        far_high, far_low, theirs, total
    )


def solution(mesh):
    dom, feat = P("dom"), P("feat")
    whole = P("dom", None, None)
    placed = (
        P("feat", "dom"), dom, whole, P("dom", None), P(), P(),
        dom, dom, whole, dom, dom, whole, dom, dom, whole,
        P("feat", None), P("feat", None), feat,
    )
    return jax.shard_map(
        shards, mesh=mesh, in_specs=placed, out_specs=P("feat", "dom"), check_vma=False
    )
```

time: 35.4 us -> 26.6 us (0.75)
  waiting for transfers between devices: 14.3 us -> 7.98 us
  local copies, waits for them, and re-layouts: 5.23 us -> 3.4 us
  starting transfers between devices: 10.4 us -> 9.51 us
    ppermute x2 -> x1, waiting for transfers between devices: 4.72 us -> 0.07 us  [shards(): lax.ppermute(features, 'feat', [(0, 1), (1, 0)])]
    unnamed x38 -> x36, local copies, waits for them, and re-layouts: 5.23 us -> 3.4 us
    ppermute x5, starting transfers between devices: 8.26 us -> 6.57 us  [swap(): return lax.ppermute(x, 'dom', [(i, i ^ 1 << k) for i in range(parts)])]
    ppermute x5, waiting for transfers between devices: 9.59 us -> 7.91 us  [swap(): return lax.ppermute(x, 'dom', [(i, i ^ 1 << k) for i in range(parts)])]
    ppermute x2 -> x1, starting transfers between devices: 2.16 us -> 2.94 us  [shards(): lax.ppermute(features, 'feat', [(0, 1), (1, 0)])]
  transfers between devices with their start and end apart: 7 -> 6, of which waited for: 5 -> 6; matrix products, arithmetic and copies ran while one was open for 0% -> 0% of each run, Pallas kernels for 9% -> 14%
where the time goes in v2:
time: 26.6 us; the launch traced here: 26.3 us
  starting transfers between devices  9.51 us (36%)
  waiting for transfers between devices  7.98 us (30%)
  Pallas kernels  5.26 us (20%)
  local copies, waits for them, and re-layouts  3.4 us (13%)
    ppermute x5, waiting for transfers between devices, swap(): return lax.ppermute(x, 'dom', [(i, i ^ 1 << k) for i in range(parts)])  7.91 us
    ppermute x5, starting transfers between devices, swap(): return lax.ppermute(x, 'dom', [(i, i ^ 1 << k) for i in range(parts)])  6.57 us
    unnamed x36, local copies, waits for them, and re-layouts  3.4 us
    ppermute x1, starting transfers between devices, shards(): lax.ppermute(features, 'feat', [(0, 1), (1, 0)])  2.94 us
    pallas_call x1, Pallas kernels, shards(): call(functools.partial(adjacency, (2 * border // tile, pairs)), (like(ver...  1.66 us
    pallas_call x1, Pallas kernels, shards(): call(finish, like(width, vertices), [VM] * 4, size=1 << 20, name='finish')  1.01 us
    pallas_call x1, Pallas kernels, shards(): call(choose, like(2 * (border + hub), vertices), [HBM] * 4, [pltpu.SMEM(h...  0.98 us
    pallas_call x1, Pallas kernels, shards(): call(functools.partial(pick, border, hub), (like(width, vertices), like(b...  0.54 us
  transfers between devices with their start and end apart: 6, of which 6 were waited for; matrix products, arithmetic and copies ran while one was open for 0% of the time, Pallas kernels for 14%

profile of v2, /device:TPU:0, one launch (start us, length us, event | category | flops | bytes accessed | tf_op | source)
XLA Modules:
  0.0 26.3 jit_solution(10214629327678125687)
XLA Ops:
  0.0 2.9 %collective-permute-start = (bf16[128,512]{1,0:T(8,128)(2,1)}, bf16[128,512]{1,0:T(8,128)(2,1)S(1)}, u32[]{:S(2)}, u32[]{:S(2)}) collective-permute-start(bf16[128,512]{1,0:T(8,128)(2,1)} %refs_0_.5), channel_id=1, source_target_pairs={{0,1},{1,0},{2,3},{3,2},{4,5},{5,4},{6,7},{7,6},{8,9},{9,8},{10,11... | collective-permute-start | bytes 393224 | tf_op jit(solution)/shard_map/ppermute | solution.py:228
  2.9 0.7 %copy-done.6 = s32[1,16,16]{2,1,0:T(8,128)S(1)} copy-done((s32[1,16,16]{2,1,0:T(8,128)S(1)}, s32[1,16,16]{2,1,0:T(8,128)}, u32[]{:S(2)}) %copy-start.6) | copy-done | bytes 1048
  3.6 0.7 %copy-done.7 = s32[4,128]{1,0:T(4,128)S(1)} copy-done((s32[4,128]{1,0:T(4,128)S(1)}, s32[4,128]{1,0:T(4,128)}, u32[]{:S(2)}) %copy-start.7) | copy-done | bytes 2072
  4.3 0.7 %copy-done.9 = s32[4]{0:T(128)S(1)} copy-done((s32[4]{0:T(128)S(1)}, s32[4]{0:T(128)}, u32[]{:S(2)}) %copy-start.9) | copy-done | bytes 40
  5.0 0.7 %copy-done.10 = s32[1,16]{1,0:T(1,128)S(1)} copy-done((s32[1,16]{1,0:T(1,128)S(1)}, s32[1,16]{1,0:T(1,128)}, u32[]{:S(2)}) %copy-start.10) | copy-done | bytes 88
  5.6 1.0 %choose.1.choice = bf16[768,512]{1,0:T(8,128)(2,1)S(1)} custom-call(s32[4]{0:T(128)S(1)} %copy-done.9, s32[1,16,16]{2,1,0:T(8,128)S(1)} %copy-done.6, s32[1,16]{1,0:T(1,128)S(1)} %copy-done.10, s32[4,128]{1,0:T(4,128)S(1)} %copy-done.7), custom_call_target="tpu_custom_call" | custom-call | bytes 2097152 | tf_op jit(solution)/shard_map/choose/pallas_call | solution.py:231
  6.6 0.0 copy-start
  6.6 0.0 copy-start.1
  6.6 0.1 collective-permute-done.refs_1_
  6.7 0.0 copy-done.3
  6.7 0.5 %pick.1 = (bf16[128,512]{1,0:T(8,128)(2,1)S(1)}, bf16[128,128]{1,0:T(8,128)(2,1)S(1)}, bf16[384,128]{1,0:T(8,128)(2,1)S(1)}, bf16[256,128]{1,0:T(8,128)(2,1)S(1)}) custom-call(bf16[128,256]{1,0:T(8,128)(2,1)S(1)} %copy-done.4, bf16[768,512]{1,0:T(8,128)(2,1)S(1)} %choose.1.choice, bf16[128,512]{1,0:T(8,128)(2,1)S(1)} %copy-done.3, ...), custom_call_target="tpu_custom_call" | custom-call | bytes 1048576 | tf_op jit(solution)/shard_map/pick/pallas_call | solution.py:242
  7.3 0.1 collective-permute-start.1
  7.3 1.3 %collective-permute-done.1.received = bf16[384,128]{1,0:T(8,128)(2,1)S(1)} collective-permute-done((bf16[384,128]{1,0:T(8,128)(2,1)S(1)}, bf16[384,128]{1,0:T(8,128)(2,1)S(1)}, u32[]{:S(2)}, u32[]{:S(2)}) %collective-permute-start.1) | collective-permute-done | bytes 98336 | tf_op jit(solution)/shard_map/ppermute | solution.py:225
  8.7 0.0 copy-start.8
  8.7 0.0 copy-start.11
  8.7 0.0 copy-start.12
  8.7 0.0 copy-start.13
  8.7 1.8 %collective-permute-start.2 = (bf16[384,128]{1,0:T(8,128)(2,1)S(1)}, bf16[384,128]{1,0:T(8,128)(2,1)S(1)}, u32[]{:S(2)}, u32[]{:S(2)}) collective-permute-start(bf16[384,128]{1,0:T(8,128)(2,1)S(1)} %get-tuple-element.24.refs_9_.b), channel_id=1, source_target_pairs={{0,4},{2,6},{4,0},{6,2},{8,12},{10,14},{12,8},{14,10},{16,20},{18,... | collective-permute-start | bytes 294920 | tf_op jit(solution)/shard_map/ppermute | solution.py:225
  10.5 0.0 copy-done
  10.5 0.0 copy-done.14
  10.6 1.7 %adjacency.1 = (bf16[512,512]{1,0:T(8,128)(2,1)S(1)}, bf16[512,512]{1,0:T(8,128)(2,1)S(1)}, bf16[512,768]{1,0:T(8,128)(2,1)S(1)}, bf16[512,768]{1,0:T(8,128)(2,1)S(1)}) custom-call(s32[1,512]{1,0:T(1,128)S(1)} %bitcast.2, s32[16]{0:T(128)S(1)} %copy-done.11, s32[16]{0:T(128)S(1)} %copy-done.12, bf16[16,128,128]{2,1,0:T(8,128)(2,1)S(1)} %copy-done, ...), custom_call_target="tpu_custom_call" | custom-call | bytes 6291456 | tf_op jit(solution)/shard_map/adjacency/pallas_call | solution.py:272
  12.2 1.4 %collective-permute-done.2.c = bf16[384,128]{1,0:T(8,128)(2,1)S(1)} collective-permute-done((bf16[384,128]{1,0:T(8,128)(2,1)S(1)}, bf16[384,128]{1,0:T(8,128)(2,1)S(1)}, u32[]{:S(2)}, u32[]{:S(2)}) %collective-permute-start.2) | collective-permute-done | bytes 98336 | tf_op jit(solution)/shard_map/ppermute | solution.py:225
  13.7 1.8 %collective-permute-start.3 = (bf16[384,128]{1,0:T(8,128)(2,1)S(1)}, bf16[384,128]{1,0:T(8,128)(2,1)S(1)}, u32[]{:S(2)}, u32[]{:S(2)}) collective-permute-start(bf16[384,128]{1,0:T(8,128)(2,1)S(1)} %get-tuple-element.29.refs_2_.b), channel_id=1, source_target_pairs={{0,8},{2,10},{4,12},{6,14},{8,0},{10,2},{12,4},{14,6},{16,24},{18,... | collective-permute-start | bytes 294920 | tf_op jit(solution)/shard_map/ppermute | solution.py:225
  15.5 0.7 %copy-done.17 = f32[128]{0:T(128)S(1)} copy-done((f32[128]{0:T(128)S(1)}, f32[128]{0:T(128)}, u32[]{:S(2)}) %copy-start.17) | copy-done | bytes 536
  16.2 0.5 %own.1._.before = f32[512,128]{1,0:T(8,128)S(1)} custom-call(bf16[512,512]{1,0:T(8,128)(2,1)S(1)} %get-tuple-element.30.local_high, bf16[512,512]{1,0:T(8,128)(2,1)S(1)} %get-tuple-element.31.local_low, bf16[128,512]{1,0:T(8,128)(2,1)S(1)} %get-tuple-element.32.projected, bf16[128,256]{1,0:T(8,128)(2,1)S(1)} %copy-done.5, f32[1,128]{1,0:T(1,128)S(1)} %bitcast.3, ...), custom_call_target="tpu_custom_call" | custom-call | flops 167772160 | bytes 2097152 | tf_op jit(solution)/shard_map/own/pallas_call | solution.py:289
  16.7 1.7 %collective-permute-done.3.c = bf16[384,128]{1,0:T(8,128)(2,1)S(1)} collective-permute-done((bf16[384,128]{1,0:T(8,128)(2,1)S(1)}, bf16[384,128]{1,0:T(8,128)(2,1)S(1)}, u32[]{:S(2)}, u32[]{:S(2)}) %collective-permute-start.3) | collective-permute-done | bytes 98336 | tf_op jit(solution)/shard_map/ppermute | solution.py:225
  18.4 2.8 %collective-permute-start.4 = (bf16[384,128]{1,0:T(8,128)(2,1)S(1)}, bf16[384,128]{1,0:T(8,128)(2,1)S(1)}, u32[]{:S(2)}, u32[]{:S(2)}) collective-permute-start(bf16[384,128]{1,0:T(8,128)(2,1)S(1)} %get-tuple-element.34.hub), channel_id=1, source_target_pairs={{0,16},{2,18},{4,20},{6,22},{8,24},{10,26},{12,28},{14,30},{16,0},... | collective-permute-start | bytes 294920 | tf_op jit(solution)/shard_map/ppermute | solution.py:225
  21.2 2.7 %collective-permute-done.4.received = bf16[384,128]{1,0:T(8,128)(2,1)S(1)} collective-permute-done((bf16[384,128]{1,0:T(8,128)(2,1)S(1)}, bf16[384,128]{1,0:T(8,128)(2,1)S(1)}, u32[]{:S(2)}, u32[]{:S(2)}) %collective-permute-start.4) | collective-permute-done | bytes 98336 | tf_op jit(solution)/shard_map/ppermute | solution.py:225
  24.0 0.1 collective-permute-start.5
  24.1 0.4 %far.1.before = f32[512,128]{1,0:T(8,128)S(1)} custom-call(bf16[512,768]{1,0:T(8,128)(2,1)S(1)} %get-tuple-element.25.high, bf16[512,768]{1,0:T(8,128)(2,1)S(1)} %get-tuple-element.26._.low, bf16[512,128]{1,0:T(8,128)(2,1)S(1)} %get-tuple-element.36.near, f32[512,128]{1,0:T(8,128)S(1)} %own.1._.before), custom_call_target="tpu_custom_call" | custom-call | flops 134217728 | bytes 2097152 | tf_op jit(solution)/shard_map/far/pallas_call | solution.py:299
  24.5 0.8 %collective-permute-done.5.theirs = bf16[256,128]{1,0:T(8,128)(2,1)S(1)} collective-permute-done((bf16[256,128]{1,0:T(8,128)(2,1)S(1)}, bf16[256,128]{1,0:T(8,128)(2,1)S(1)}, u32[]{:S(2)}, u32[]{:S(2)}) %collective-permute-start.5) | collective-permute-done | bytes 65568 | tf_op jit(solution)/shard_map/ppermute | solution.py:225
  25.3 1.0 %finish.1 = bf16[128,512]{1,0:T(8,128)(2,1)} custom-call(bf16[512,768]{1,0:T(8,128)(2,1)S(1)} %get-tuple-element.25.high, bf16[512,768]{1,0:T(8,128)(2,1)S(1)} %get-tuple-element.26._.low, bf16[256,128]{1,0:T(8,128)(2,1)S(1)} %collective-permute-done.5.theirs, f32[512,128]{1,0:T(8,128)S(1)} %far.1.before), custom_call_target="tpu_custom_call" | custom-call | bytes 1048576 | tf_op jit(solution)/shard_map/finish/pallas_call | solution.py:303
  (26 shorter events, 0.1 us)
Async XLA Ops:
  0.0 6.7 %copy-start.3 = (bf16[128,512]{1,0:T(8,128)(2,1)S(1)}, bf16[128,512]{1,0:T(8,128)(2,1)}, u32[]{:S(2)}) copy-start(bf16[128,512]{1,0:T(8,128)(2,1)} %refs_0_.5) | copy-start | bytes 393220
  0.0 6.7 %copy-start.4 = (bf16[128,256]{1,0:T(8,128)(2,1)S(1)}, bf16[128,256]{1,0:T(8,128)(2,1)}, u32[]{:S(2)}) copy-start(bf16[128,256]{1,0:T(8,128)(2,1)} %weight.2) | copy-start | bytes 196612
  0.0 6.7 %collective-permute-start = (bf16[128,512]{1,0:T(8,128)(2,1)}, bf16[128,512]{1,0:T(8,128)(2,1)S(1)}, u32[]{:S(2)}, u32[]{:S(2)}) collective-permute-start(bf16[128,512]{1,0:T(8,128)(2,1)} %refs_0_.5), channel_id=1, source_target_pairs={{0,1},{1,0},{2,3},{3,2},{4,5},{5,4},{6,7},{7,6},{8,9},{9,8},{10,11... | collective-permute-start | bytes 393224 | tf_op jit(solution)/shard_map/ppermute | solution.py:228
  2.9 0.7 %copy-start.6 = (s32[1,16,16]{2,1,0:T(8,128)S(1)}, s32[1,16,16]{2,1,0:T(8,128)}, u32[]{:S(2)}) copy-start(s32[1,16,16]{2,1,0:T(8,128)} %lists_h.1) | copy-start | bytes 3076
  3.6 0.7 %copy-start.7 = (s32[4,128]{1,0:T(4,128)S(1)}, s32[4,128]{1,0:T(4,128)}, u32[]{:S(2)}) copy-start(s32[4,128]{1,0:T(4,128)} %hubs_h.1) | copy-start | bytes 6148
  4.3 0.7 %copy-start.9 = (s32[4]{0:T(128)S(1)}, s32[4]{0:T(128)}, u32[]{:S(2)}) copy-start(s32[4]{0:T(128)} %owner_h.1) | copy-start | bytes 52
  5.0 0.7 %copy-start.10 = (s32[1,16]{1,0:T(1,128)S(1)}, s32[1,16]{1,0:T(1,128)}, u32[]{:S(2)}) copy-start(s32[1,16]{1,0:T(1,128)} %count_h.1) | copy-start | bytes 196
  5.6 4.9 %copy-start.2 = (bf16[16,128,128]{2,1,0:T(8,128)(2,1)S(1)}, bf16[16,128,128]{2,1,0:T(8,128)(2,1)}, u32[]{:S(2)}) copy-start(bf16[16,128,128]{2,1,0:T(8,128)(2,1)} %refs_8_.1) | copy-start | bytes 1572868
  6.6 3.9 %copy-start = (bf16[16,128,128]{2,1,0:T(8,128)(2,1)S(1)}, bf16[16,128,128]{2,1,0:T(8,128)(2,1)}, u32[]{:S(2)}) copy-start(bf16[16,128,128]{2,1,0:T(8,128)(2,1)} %refs_2_.1) | copy-start | bytes 1572868
  6.6 3.9 %copy-start.1 = (bf16[16,128,128]{2,1,0:T(8,128)(2,1)S(1)}, bf16[16,128,128]{2,1,0:T(8,128)(2,1)}, u32[]{:S(2)}) copy-start(bf16[16,128,128]{2,1,0:T(8,128)(2,1)} %refs_5_.1) | copy-start | bytes 1572868
  7.3 1.4 %collective-permute-start.1 = (bf16[384,128]{1,0:T(8,128)(2,1)S(1)}, bf16[384,128]{1,0:T(8,128)(2,1)S(1)}, u32[]{:S(2)}, u32[]{:S(2)}) collective-permute-start(bf16[384,128]{1,0:T(8,128)(2,1)S(1)} %get-tuple-element.23), channel_id=1, source_target_pairs={{0,2},{2,0},{4,6},{6,4},{8,10},{10,8},{12,14},{14,12},{16,18},{18,... | collective-permute-start | bytes 294920 | tf_op jit(solution)/shard_map/ppermute | solution.py:225
  8.6 1.9 %copy-start.14 = (s32[16]{0:T(128)S(1)}, s32[16]{0:T(128)}, u32[]{:S(2)}) copy-start(s32[16]{0:T(128)} %refs_4_.1) | copy-start | bytes 196
  8.6 1.9 %copy-start.15 = (s32[16]{0:T(128)S(1)}, s32[16]{0:T(128)}, u32[]{:S(2)}) copy-start(s32[16]{0:T(128)} %refs_6_.1) | copy-start | bytes 196
  8.6 1.9 %copy-start.16 = (s32[16]{0:T(128)S(1)}, s32[16]{0:T(128)}, u32[]{:S(2)}) copy-start(s32[16]{0:T(128)} %refs_7_.1) | copy-start | bytes 196
  8.7 1.8 %copy-start.8 = (s32[512]{0:T(512)S(1)}, s32[512]{0:T(512)}, u32[]{:S(2)}) copy-start(s32[512]{0:T(512)} %param.19) | copy-start | bytes 6148
  8.7 1.8 %copy-start.11 = (s32[16]{0:T(128)S(1)}, s32[16]{0:T(128)}, u32[]{:S(2)}) copy-start(s32[16]{0:T(128)} %refs_0_.4) | copy-start | bytes 196
  8.7 1.8 %copy-start.12 = (s32[16]{0:T(128)S(1)}, s32[16]{0:T(128)}, u32[]{:S(2)}) copy-start(s32[16]{0:T(128)} %refs_1_.1) | copy-start | bytes 196
  8.7 1.8 %copy-start.13 = (s32[16]{0:T(128)S(1)}, s32[16]{0:T(128)}, u32[]{:S(2)}) copy-start(s32[16]{0:T(128)} %refs_3_.1) | copy-start | bytes 196
  8.7 4.9 %collective-permute-start.2 = (bf16[384,128]{1,0:T(8,128)(2,1)S(1)}, bf16[384,128]{1,0:T(8,128)(2,1)S(1)}, u32[]{:S(2)}, u32[]{:S(2)}) collective-permute-start(bf16[384,128]{1,0:T(8,128)(2,1)S(1)} %get-tuple-element.24.refs_9_.b), channel_id=1, source_target_pairs={{0,4},{2,6},{4,0},{6,2},{8,12},{10,14},{12,8},{14,10},{16,20},{18,... | collective-permute-start | bytes 294920 | tf_op jit(solution)/shard_map/ppermute | solution.py:225
  13.7 1.9 %copy-start.5 = (bf16[128,256]{1,0:T(8,128)(2,1)S(1)}, bf16[128,256]{1,0:T(8,128)(2,1)}, u32[]{:S(2)}) copy-start(bf16[128,256]{1,0:T(8,128)(2,1)} %weight.3) | copy-start | bytes 196612
  13.7 4.7 %collective-permute-start.3 = (bf16[384,128]{1,0:T(8,128)(2,1)S(1)}, bf16[384,128]{1,0:T(8,128)(2,1)S(1)}, u32[]{:S(2)}, u32[]{:S(2)}) collective-permute-start(bf16[384,128]{1,0:T(8,128)(2,1)S(1)} %get-tuple-element.29.refs_2_.b), channel_id=1, source_target_pairs={{0,8},{2,10},{4,12},{6,14},{8,0},{10,2},{12,4},{14,6},{16,24},{18,... | collective-permute-start | bytes 294920 | tf_op jit(solution)/shard_map/ppermute | solution.py:225
  15.5 0.7 %copy-start.17 = (f32[128]{0:T(128)S(1)}, f32[128]{0:T(128)}, u32[]{:S(2)}) copy-start(f32[128]{0:T(128)} %param.35) | copy-start | bytes 1540
  18.4 5.6 %collective-permute-start.4 = (bf16[384,128]{1,0:T(8,128)(2,1)S(1)}, bf16[384,128]{1,0:T(8,128)(2,1)S(1)}, u32[]{:S(2)}, u32[]{:S(2)}) collective-permute-start(bf16[384,128]{1,0:T(8,128)(2,1)S(1)} %get-tuple-element.34.hub), channel_id=1, source_target_pairs={{0,16},{2,18},{4,20},{6,22},{8,24},{10,26},{12,28},{14,30},{16,0},... | collective-permute-start | bytes 294920 | tf_op jit(solution)/shard_map/ppermute | solution.py:225
  24.0 1.3 %collective-permute-start.5 = (bf16[256,128]{1,0:T(8,128)(2,1)S(1)}, bf16[256,128]{1,0:T(8,128)(2,1)S(1)}, u32[]{:S(2)}, u32[]{:S(2)}) collective-permute-start(bf16[256,128]{1,0:T(8,128)(2,1)S(1)} %get-tuple-element.35), channel_id=1, source_target_pairs={{0,2},{2,0},{4,6},{6,4},{8,10},{10,8},{12,14},{14,12},{16,18},{18,... | collective-permute-start | bytes 196616 | tf_op jit(solution)/shard_map/ppermute | solution.py:225

commit v3 on v2

--- a/solution.py
+++ b/solution.py
@@ -51,16 +51,24 @@
     return copies
 
 
-def choose(owner_h, lists_h, count_h, hubs_h, choice, owner, lists, count, hubs, sems):
-    for copy in fetch(
-        [(owner_h, owner), (lists_h, lists), (count_h, count), (hubs_h, hubs)], sems
-    ):
+def choose(*refs):
+    inputs, (choice, *parts_out), scratch = refs[:6], refs[6:-7], refs[-7:]
+    owner, lists, count, hubs, features, weight, sems = scratch
+    copies = [
+        pltpu.make_async_copy(a, b, sems.at[i])
+        for i, (a, b) in enumerate(zip(inputs, scratch[:6]))
+    ]
+    for copy in copies:
+        copy.start()
+    for copy in copies[:4]:
         copy.wait()
     me = lax.axis_index("dom")
     bit = me & 1
     parts, cap = lists.shape[1:]
     blocks, tile = hubs.shape
     vertices = choice.shape[1]
+    pairs = (blocks + 1) // 2
+    border, half = parts * cap // 2, parts * cap // 2 + pairs * tile
     shape = (parts, cap, cap)
     slot = lax.broadcasted_iota(jnp.int32, shape, 1)
     across = lax.broadcasted_iota(jnp.int32, shape, 2)
@@ -77,17 +85,26 @@
         return (vertex == index).astype(F32).astype(BF16)
 
     for part in range(parts):
-        place = (part >> 1) + ((part & 1) ^ bit) * (parts // 2)
-        choice[rows(place * cap, cap), :] = onehot(index[part])
-    pairs = (blocks + 1) // 2
+        stays = 1 - ((part & 1) ^ bit)
+        choice[pl.ds(pl.multiple_of(stays * half + (part >> 1) * cap, cap), cap), :] = onehot(
+            index[part]
+        )
     for b in range(2 * pairs):
-        place = (b >> 1) + (1 - ((b & 1) ^ bit)) * pairs
-        there = pl.ds(pl.multiple_of(parts * cap + place * tile, cap), tile)
+        stays = 1 - ((b & 1) ^ bit)
+        there = pl.ds(pl.multiple_of(stays * half + border + (b >> 1) * tile, cap), tile)
         if b < blocks:
             mine = jnp.where(owner[b] == me, hubs[b : b + 1, :], -1)
             choice[there, :] = onehot(column(mine))
         else:
             choice[there, :] = jnp.zeros((tile, vertices), BF16)
+    for copy in copies[4:]:
+        copy.wait()
+    if len(parts_out) == 2:
+        known, ahead = parts_out
+        width = features.shape[0]
+        place = lax.axis_index("feat")
+        known[...] = dot(weight[:, rows(place * width, width)], features[...])
+        ahead[...] = weight[:, rows((1 - place) * width, width)]
 
 
 def weight_parts(weight, feature_blocks):
@@ -101,14 +118,19 @@
     ]
 
 
-def pick(border, hub, weight, choice, *refs):
-    *feature_blocks, projected, keep, message, held = refs
-    total = sum(dot(w, f) for w, f in weight_parts(weight, feature_blocks)).astype(BF16)
-    projected[...] = total
-    picked = dot(choice[...], total, LAST).astype(BF16)
-    keep[...] = picked[:border]
-    message[...] = picked[border : 2 * border + hub]
-    held[...] = picked[2 * border + hub :]
+def pick(weight, features, choice, *refs):
+    *known, projected, message = refs
+    total = dot(weight[...], features[...])
+    if known:
+        total = total + known[0][...]
+    projected[...] = total.astype(BF16)
+    message[...] = dot(
+        choice[: message.shape[0], :], total.astype(BF16), LAST
+    ).astype(BF16)
+
+
+def remain(projected, choice, kept):
+    kept[...] = dot(choice[kept.shape[0] :, :], projected[...], LAST).astype(BF16)
 
 
 def step(k, parts, cap, last, keep, hub, received, *outs):
@@ -119,7 +141,7 @@
     run = (1 << k) * cap
     first, second = outs[-2:]
     if last:
-        first[rows(bit * run, run), :] = keep[...]
+        first[rows(bit * run, run), :] = keep[:border, :]
         first[rows((1 - bit) * run, run), :] = received[:border, :]
         first[2 * border :, :] = merged
         second[...] = merged
@@ -228,23 +250,34 @@
         feature_blocks = [features, lax.ppermute(features, "feat", [(0, 1), (1, 0)])]
     else:
         feature_blocks = [lax.all_gather(features, "feat", axis=0, tiled=True)]
-    choice = call(
-        choose, like(2 * (border + hub), vertices), [HBM] * 4,
+    fixed = [
+        pltpu.with_memory_space_constraint(x, pltpu.HBM)
+        for x in (hub_owner, send_rows, send_count, hub_rows, features, neighbor_weight)
+    ]
+    early = ()
+    if feats == 2:
+        early = (like(width, vertices, kind=F32), like(width, features.shape[0]))
+    choice, *early = call(
+        choose, (like(2 * (border + hub), vertices), *early), [HBM] * 6,
         [
             pltpu.SMEM(hub_owner.shape, jnp.int32),
             pltpu.VMEM(send_rows.shape, jnp.int32),
             pltpu.VMEM(send_count.shape, jnp.int32),
             pltpu.VMEM(hub_rows.shape, jnp.int32),
-            pltpu.SemaphoreType.DMA((4,)),
+            pltpu.VMEM(features.shape, BF16),
+            pltpu.VMEM(neighbor_weight.shape, BF16),
+            pltpu.SemaphoreType.DMA((6,)),
         ],
         size=2 << 20, name="choose",
-    )(hub_owner, send_rows, send_count, hub_rows)
-    projected, keep, message, held = call(
-        functools.partial(pick, border, hub),
-        (like(width, vertices), like(border, width), like(border + hub, width), like(hub, width)),
-        [VM] * (2 + len(feature_blocks)),
+    )(*fixed)
+    weight, known = (early[1], early[:1]) if early else (neighbor_weight, [])
+    projected, message = call(
+        pick, (like(width, vertices), like(border + hub, width)), [VM] * (3 + len(known)),
         size=1 << 20, name="pick",
-    )(neighbor_weight, choice, *feature_blocks)
+    )(weight, feature_blocks[-1], choice, *known)
+    keep = held = call(
+        remain, like(border + hub, width), [VM] * 2, size=1 << 20, name="remain"
+    )(projected, choice)
     inputs = (
         local_dest, local_source, local_tiles, border_dest, border_source, border_tiles,
         hub_dest, hub_source, hub_tiles,

time: 26.6 us -> 26.3 us (0.989)
  local copies, waits for them, and re-layouts: 3.4 us -> 0.71 us
  waiting for transfers between devices: 7.98 us -> 9.87 us
  Pallas kernels: 5.26 us -> 5.74 us
    unnamed x36 -> x26, local copies, waits for them, and re-layouts: 3.4 us -> 0.71 us
    ppermute x1, waiting for transfers between devices: 0.07 us -> 2.36 us  [shards(): lax.ppermute(features, 'feat', [(0, 1), (1, 0)])]
    pallas_call x2 -> x3, Pallas kernels: 1.52 us -> 2 us  [the longest x1 1.34 us: shards(): call(choose, (like(2 * (border + hub), vertices), *early), [HBM] * 6, [pl...]
    ppermute x5, waiting for transfers between devices: 7.91 us -> 7.51 us  [swap(): return lax.ppermute(x, 'dom', [(i, i ^ 1 << k) for i in range(parts)])]
  transfers between devices with their start and end apart: 6 -> 6, of which waited for: 6 -> 6; matrix products, arithmetic and copies ran while one was open for 0% -> 0% of each run, Pallas kernels for 14% -> 16%
where the time goes in v3:
time: 26.3 us; the launch traced here: 26.2 us
  waiting for transfers between devices  9.87 us (38%)
  starting transfers between devices  9.64 us (37%)
  Pallas kernels  5.74 us (22%)
  local copies, waits for them, and re-layouts  0.71 us (3%)
    ppermute x5, waiting for transfers between devices, swap(): return lax.ppermute(x, 'dom', [(i, i ^ 1 << k) for i in range(parts)])  7.51 us
    ppermute x5, starting transfers between devices, swap(): return lax.ppermute(x, 'dom', [(i, i ^ 1 << k) for i in range(parts)])  6.7 us
    ppermute x1, starting transfers between devices, shards(): lax.ppermute(features, 'feat', [(0, 1), (1, 0)])  2.94 us
    ppermute x1, waiting for transfers between devices, shards(): lax.ppermute(features, 'feat', [(0, 1), (1, 0)])  2.36 us
    pallas_call x1, Pallas kernels, shards(): call(functools.partial(adjacency, (2 * border // tile, pairs)), (like(ver...  1.66 us
    pallas_call x1, Pallas kernels, shards(): call(choose, (like(2 * (border + hub), vertices), *early), [HBM] * 6, [pl...  1.34 us
    pallas_call x1, Pallas kernels, shards(): call(finish, like(width, vertices), [VM] * 4, size=1 << 20, name='finish')  1.01 us
    unnamed x26, local copies, waits for them, and re-layouts  0.71 us
  transfers between devices with their start and end apart: 6, of which 6 were waited for; matrix products, arithmetic and copies ran while one was open for 0% of the time, Pallas kernels for 16%

profile of v3, /device:TPU:0, one launch (start us, length us, event | category | flops | bytes accessed | tf_op | source)
XLA Modules:
  0.0 26.2 jit_solution(7930538236176192313)
XLA Ops:
  0.0 2.9 %collective-permute-start = (bf16[128,512]{1,0:T(8,128)(2,1)}, bf16[128,512]{1,0:T(8,128)(2,1)S(1)}, u32[]{:S(2)}, u32[]{:S(2)}) collective-permute-start(bf16[128,512]{1,0:T(8,128)(2,1)} %refs_0_.5), channel_id=1, source_target_pairs={{0,1},{1,0},{2,3},{3,2},{4,5},{5,4},{6,7},{7,6},{8,9},{9,8},{10,11... | collective-permute-start | bytes 393224 | tf_op jit(solution)/shard_map/ppermute | solution.py:250
  2.9 1.3 %choose.1 = (bf16[768,512]{1,0:T(8,128)(2,1)S(1)}, f32[128,512]{1,0:T(8,128)S(1)}, bf16[128,128]{1,0:T(8,128)(2,1)S(1)}) custom-call(s32[4]{0:T(128)} %refs_0_.3, s32[1,16,16]{2,1,0:T(8,128)} %refs_1_.2, s32[1,16]{1,0:T(1,128)} %refs_2_.2, s32[4,128]{1,0:T(4,128)} %refs_3_.2, bf16[128,512]{1,0:T(8,128)(2,1)} %refs_0_.5, bf16[128,256]{1,0:T(8,128)(2,1)} %refs_5_.2), custom_call_target="tpu_custom_call" | custom-call | bytes 2097152 | tf_op jit(solution)/shard_map/choose/pallas_call | solution.py:260
  4.3 2.4 %collective-permute-done.features.refs_1_ = bf16[128,512]{1,0:T(8,128)(2,1)S(1)} collective-permute-done((bf16[128,512]{1,0:T(8,128)(2,1)}, bf16[128,512]{1,0:T(8,128)(2,1)S(1)}, u32[]{:S(2)}, u32[]{:S(2)}) %collective-permute-start) | collective-permute-done | bytes 131104 | tf_op jit(solution)/shard_map/ppermute | solution.py:250
  6.6 0.4 %pick.1 = (bf16[128,512]{1,0:T(8,128)(2,1)S(1)}, bf16[384,128]{1,0:T(8,128)(2,1)S(1)}) custom-call(bf16[128,128]{1,0:T(8,128)(2,1)S(1)} %get-tuple-element.22.weight, bf16[128,512]{1,0:T(8,128)(2,1)S(1)} %collective-permute-done.features.refs_1_, bf16[768,512]{1,0:T(8,128)(2,1)S(1)} %get-tuple-element.23.choice, f32[128,512]{1,0:T(8,128)S(1)} %get-tuple-element.24.refs_0_), custom_call_target="tpu_custom_call" | custom-call | bytes 1048576 | tf_op jit(solution)/shard_map/pick/pallas_call | solution.py:274
  7.1 0.1 collective-permute-start.1
  7.1 0.0 copy-start
  7.2 0.0 copy-start.1
  7.2 0.3 remain.1.keep.hub
  7.4 1.0 %collective-permute-done.1.received = bf16[384,128]{1,0:T(8,128)(2,1)S(1)} collective-permute-done((bf16[384,128]{1,0:T(8,128)(2,1)S(1)}, bf16[384,128]{1,0:T(8,128)(2,1)S(1)}, u32[]{:S(2)}, u32[]{:S(2)}) %collective-permute-start.1) | collective-permute-done | bytes 98336 | tf_op jit(solution)/shard_map/ppermute | solution.py:247
  8.5 0.0 copy-start.5
  8.5 0.0 copy-start.6
  8.5 0.0 copy-start.7
  8.5 0.0 copy-start.8
  8.5 1.8 %collective-permute-start.2 = (bf16[384,128]{1,0:T(8,128)(2,1)S(1)}, bf16[384,128]{1,0:T(8,128)(2,1)S(1)}, u32[]{:S(2)}, u32[]{:S(2)}) collective-permute-start(bf16[384,128]{1,0:T(8,128)(2,1)S(1)} %get-tuple-element.27.refs_9_.b), channel_id=1, source_target_pairs={{0,4},{2,6},{4,0},{6,2},{8,12},{10,14},{12,8},{14,10},{16,20},{18,... | collective-permute-start | bytes 294920 | tf_op jit(solution)/shard_map/ppermute | solution.py:247
  10.4 0.0 copy-done.2
  10.4 0.0 copy-done
  10.4 0.0 copy-done.1
  10.4 0.0 copy-done.9
  10.4 0.0 copy-done.10
  10.4 1.7 %adjacency.1 = (bf16[512,512]{1,0:T(8,128)(2,1)S(1)}, bf16[512,512]{1,0:T(8,128)(2,1)S(1)}, bf16[512,768]{1,0:T(8,128)(2,1)S(1)}, bf16[512,768]{1,0:T(8,128)(2,1)S(1)}) custom-call(s32[1,512]{1,0:T(1,128)S(1)} %bitcast.2, s32[16]{0:T(128)S(1)} %copy-done.6, s32[16]{0:T(128)S(1)} %copy-done.7, bf16[16,128,128]{2,1,0:T(8,128)(2,1)S(1)} %copy-done, ...), custom_call_target="tpu_custom_call" | custom-call | bytes 6291456 | tf_op jit(solution)/shard_map/adjacency/pallas_call | solution.py:305
  12.1 1.4 %collective-permute-done.2.c = bf16[384,128]{1,0:T(8,128)(2,1)S(1)} collective-permute-done((bf16[384,128]{1,0:T(8,128)(2,1)S(1)}, bf16[384,128]{1,0:T(8,128)(2,1)S(1)}, u32[]{:S(2)}, u32[]{:S(2)}) %collective-permute-start.2) | collective-permute-done | bytes 98336 | tf_op jit(solution)/shard_map/ppermute | solution.py:247
  13.5 1.9 %collective-permute-start.3 = (bf16[384,128]{1,0:T(8,128)(2,1)S(1)}, bf16[384,128]{1,0:T(8,128)(2,1)S(1)}, u32[]{:S(2)}, u32[]{:S(2)}) collective-permute-start(bf16[384,128]{1,0:T(8,128)(2,1)S(1)} %get-tuple-element.32.refs_2_.b), channel_id=1, source_target_pairs={{0,8},{2,10},{4,12},{6,14},{8,0},{10,2},{12,4},{14,6},{16,24},{18,... | collective-permute-start | bytes 294920 | tf_op jit(solution)/shard_map/ppermute | solution.py:247
  15.4 0.0 copy-done.4
  15.4 0.6 %copy-done.12 = f32[128]{0:T(128)S(1)} copy-done((f32[128]{0:T(128)S(1)}, f32[128]{0:T(128)}, u32[]{:S(2)}) %copy-start.12) | copy-done | bytes 536
  16.0 0.5 %own.1._.before = f32[512,128]{1,0:T(8,128)S(1)} custom-call(bf16[512,512]{1,0:T(8,128)(2,1)S(1)} %get-tuple-element.33.local_high, bf16[512,512]{1,0:T(8,128)(2,1)S(1)} %get-tuple-element.34.local_low, bf16[128,512]{1,0:T(8,128)(2,1)S(1)} %get-tuple-element.25.projected, bf16[128,256]{1,0:T(8,128)(2,1)S(1)} %copy-done.4, f32[1,128]{1,0:T(1,128)S(1)} %bitcast.3, ...), custom_call_target="tpu_custom_call" | custom-call | flops 167772160 | bytes 2097152 | tf_op jit(solution)/shard_map/own/pallas_call | solution.py:322
  16.6 1.6 %collective-permute-done.3.c = bf16[384,128]{1,0:T(8,128)(2,1)S(1)} collective-permute-done((bf16[384,128]{1,0:T(8,128)(2,1)S(1)}, bf16[384,128]{1,0:T(8,128)(2,1)S(1)}, u32[]{:S(2)}, u32[]{:S(2)}) %collective-permute-start.3) | collective-permute-done | bytes 98336 | tf_op jit(solution)/shard_map/ppermute | solution.py:247
  18.2 2.9 %collective-permute-start.4 = (bf16[384,128]{1,0:T(8,128)(2,1)S(1)}, bf16[384,128]{1,0:T(8,128)(2,1)S(1)}, u32[]{:S(2)}, u32[]{:S(2)}) collective-permute-start(bf16[384,128]{1,0:T(8,128)(2,1)S(1)} %get-tuple-element.36.hub), channel_id=1, source_target_pairs={{0,16},{2,18},{4,20},{6,22},{8,24},{10,26},{12,28},{14,30},{16,0},... | collective-permute-start | bytes 294920 | tf_op jit(solution)/shard_map/ppermute | solution.py:247
  21.1 2.7 %collective-permute-done.4.received = bf16[384,128]{1,0:T(8,128)(2,1)S(1)} collective-permute-done((bf16[384,128]{1,0:T(8,128)(2,1)S(1)}, bf16[384,128]{1,0:T(8,128)(2,1)S(1)}, u32[]{:S(2)}, u32[]{:S(2)}) %collective-permute-start.4) | collective-permute-done | bytes 98336 | tf_op jit(solution)/shard_map/ppermute | solution.py:247
  23.8 0.1 collective-permute-start.5
  23.9 0.4 %far.1.before = f32[512,128]{1,0:T(8,128)S(1)} custom-call(bf16[512,768]{1,0:T(8,128)(2,1)S(1)} %get-tuple-element.28.high, bf16[512,768]{1,0:T(8,128)(2,1)S(1)} %get-tuple-element.29._.low, bf16[512,128]{1,0:T(8,128)(2,1)S(1)} %get-tuple-element.38.near, f32[512,128]{1,0:T(8,128)S(1)} %own.1._.before), custom_call_target="tpu_custom_call" | custom-call | flops 134217728 | bytes 2097152 | tf_op jit(solution)/shard_map/far/pallas_call | solution.py:332
  24.3 0.8 %collective-permute-done.5.theirs = bf16[256,128]{1,0:T(8,128)(2,1)S(1)} collective-permute-done((bf16[256,128]{1,0:T(8,128)(2,1)S(1)}, bf16[256,128]{1,0:T(8,128)(2,1)S(1)}, u32[]{:S(2)}, u32[]{:S(2)}) %collective-permute-start.5) | collective-permute-done | bytes 65568 | tf_op jit(solution)/shard_map/ppermute | solution.py:247
  25.1 1.0 %finish.1 = bf16[128,512]{1,0:T(8,128)(2,1)} custom-call(bf16[512,768]{1,0:T(8,128)(2,1)S(1)} %get-tuple-element.28.high, bf16[512,768]{1,0:T(8,128)(2,1)S(1)} %get-tuple-element.29._.low, bf16[256,128]{1,0:T(8,128)(2,1)S(1)} %collective-permute-done.5.theirs, f32[512,128]{1,0:T(8,128)S(1)} %far.1.before), custom_call_target="tpu_custom_call" | custom-call | bytes 1048576 | tf_op jit(solution)/shard_map/finish/pallas_call | solution.py:336
  (17 shorter events, 0.1 us)
Async XLA Ops:
  0.0 6.6 %collective-permute-start = (bf16[128,512]{1,0:T(8,128)(2,1)}, bf16[128,512]{1,0:T(8,128)(2,1)S(1)}, u32[]{:S(2)}, u32[]{:S(2)}) collective-permute-start(bf16[128,512]{1,0:T(8,128)(2,1)} %refs_0_.5), channel_id=1, source_target_pairs={{0,1},{1,0},{2,3},{3,2},{4,5},{5,4},{6,7},{7,6},{8,9},{9,8},{10,11... | collective-permute-start | bytes 393224 | tf_op jit(solution)/shard_map/ppermute | solution.py:250
  6.6 3.7 %copy-start.2 = (bf16[16,128,128]{2,1,0:T(8,128)(2,1)S(1)}, bf16[16,128,128]{2,1,0:T(8,128)(2,1)}, u32[]{:S(2)}) copy-start(bf16[16,128,128]{2,1,0:T(8,128)(2,1)} %refs_8_.1) | copy-start | bytes 1572868
  7.1 1.4 %collective-permute-start.1 = (bf16[384,128]{1,0:T(8,128)(2,1)S(1)}, bf16[384,128]{1,0:T(8,128)(2,1)S(1)}, u32[]{:S(2)}, u32[]{:S(2)}) collective-permute-start(bf16[384,128]{1,0:T(8,128)(2,1)S(1)} %get-tuple-element.26), channel_id=1, source_target_pairs={{0,2},{2,0},{4,6},{6,4},{8,10},{10,8},{12,14},{14,12},{16,18},{18,... | collective-permute-start | bytes 294920 | tf_op jit(solution)/shard_map/ppermute | solution.py:247
  7.1 3.2 %copy-start = (bf16[16,128,128]{2,1,0:T(8,128)(2,1)S(1)}, bf16[16,128,128]{2,1,0:T(8,128)(2,1)}, u32[]{:S(2)}) copy-start(bf16[16,128,128]{2,1,0:T(8,128)(2,1)} %refs_2_.3) | copy-start | bytes 1572868
  7.2 3.2 %copy-start.1 = (bf16[16,128,128]{2,1,0:T(8,128)(2,1)S(1)}, bf16[16,128,128]{2,1,0:T(8,128)(2,1)}, u32[]{:S(2)}) copy-start(bf16[16,128,128]{2,1,0:T(8,128)(2,1)} %refs_5_.3) | copy-start | bytes 1572868
  8.4 1.9 %copy-start.9 = (s32[16]{0:T(128)S(1)}, s32[16]{0:T(128)}, u32[]{:S(2)}) copy-start(s32[16]{0:T(128)} %refs_4_.3) | copy-start | bytes 196
  8.4 1.9 %copy-start.10 = (s32[16]{0:T(128)S(1)}, s32[16]{0:T(128)}, u32[]{:S(2)}) copy-start(s32[16]{0:T(128)} %refs_6_.1) | copy-start | bytes 196
  8.4 2.0 %copy-start.11 = (s32[16]{0:T(128)S(1)}, s32[16]{0:T(128)}, u32[]{:S(2)}) copy-start(s32[16]{0:T(128)} %refs_7_.1) | copy-start | bytes 196
  8.5 1.9 %copy-start.5 = (s32[512]{0:T(512)S(1)}, s32[512]{0:T(512)}, u32[]{:S(2)}) copy-start(s32[512]{0:T(512)} %param.19) | copy-start | bytes 6148
  8.5 1.9 %copy-start.6 = (s32[16]{0:T(128)S(1)}, s32[16]{0:T(128)}, u32[]{:S(2)}) copy-start(s32[16]{0:T(128)} %refs_0_.4) | copy-start | bytes 196
  8.5 1.9 %copy-start.7 = (s32[16]{0:T(128)S(1)}, s32[16]{0:T(128)}, u32[]{:S(2)}) copy-start(s32[16]{0:T(128)} %refs_1_.3) | copy-start | bytes 196
  8.5 1.9 %copy-start.8 = (s32[16]{0:T(128)S(1)}, s32[16]{0:T(128)}, u32[]{:S(2)}) copy-start(s32[16]{0:T(128)} %refs_3_.3) | copy-start | bytes 196
  8.5 4.9 %collective-permute-start.2 = (bf16[384,128]{1,0:T(8,128)(2,1)S(1)}, bf16[384,128]{1,0:T(8,128)(2,1)S(1)}, u32[]{:S(2)}, u32[]{:S(2)}) collective-permute-start(bf16[384,128]{1,0:T(8,128)(2,1)S(1)} %get-tuple-element.27.refs_9_.b), channel_id=1, source_target_pairs={{0,4},{2,6},{4,0},{6,2},{8,12},{10,14},{12,8},{14,10},{16,20},{18,... | collective-permute-start | bytes 294920 | tf_op jit(solution)/shard_map/ppermute | solution.py:247
  13.5 1.9 %copy-start.3 = (bf16[128,512]{1,0:T(8,128)(2,1)S(1)}, bf16[128,512]{1,0:T(8,128)(2,1)}, u32[]{:S(2)}) copy-start(bf16[128,512]{1,0:T(8,128)(2,1)} %refs_0_.5) | copy-start | bytes 393220
  13.5 1.9 %copy-start.4 = (bf16[128,256]{1,0:T(8,128)(2,1)S(1)}, bf16[128,256]{1,0:T(8,128)(2,1)}, u32[]{:S(2)}) copy-start(bf16[128,256]{1,0:T(8,128)(2,1)} %weight.1) | copy-start | bytes 196612
  13.5 4.7 %collective-permute-start.3 = (bf16[384,128]{1,0:T(8,128)(2,1)S(1)}, bf16[384,128]{1,0:T(8,128)(2,1)S(1)}, u32[]{:S(2)}, u32[]{:S(2)}) collective-permute-start(bf16[384,128]{1,0:T(8,128)(2,1)S(1)} %get-tuple-element.32.refs_2_.b), channel_id=1, source_target_pairs={{0,8},{2,10},{4,12},{6,14},{8,0},{10,2},{12,4},{14,6},{16,24},{18,... | collective-permute-start | bytes 294920 | tf_op jit(solution)/shard_map/ppermute | solution.py:247
  15.4 0.7 %copy-start.12 = (f32[128]{0:T(128)S(1)}, f32[128]{0:T(128)}, u32[]{:S(2)}) copy-start(f32[128]{0:T(128)} %param.35) | copy-start | bytes 1540
  18.2 5.6 %collective-permute-start.4 = (bf16[384,128]{1,0:T(8,128)(2,1)S(1)}, bf16[384,128]{1,0:T(8,128)(2,1)S(1)}, u32[]{:S(2)}, u32[]{:S(2)}) collective-permute-start(bf16[384,128]{1,0:T(8,128)(2,1)S(1)} %get-tuple-element.36.hub), channel_id=1, source_target_pairs={{0,16},{2,18},{4,20},{6,22},{8,24},{10,26},{12,28},{14,30},{16,0},... | collective-permute-start | bytes 294920 | tf_op jit(solution)/shard_map/ppermute | solution.py:247
  23.8 1.3 %collective-permute-start.5 = (bf16[256,128]{1,0:T(8,128)(2,1)S(1)}, bf16[256,128]{1,0:T(8,128)(2,1)S(1)}, u32[]{:S(2)}, u32[]{:S(2)}) collective-permute-start(bf16[256,128]{1,0:T(8,128)(2,1)S(1)} %get-tuple-element.37), channel_id=1, source_target_pairs={{0,2},{2,0},{4,6},{6,4},{8,10},{10,8},{12,14},{14,12},{16,18},{18,... | collective-permute-start | bytes 196616 | tf_op jit(solution)/shard_map/ppermute | solution.py:247

commit v4 on v3

--- a/solution.py
+++ b/solution.py
@@ -35,6 +35,29 @@
 
 def rows(start, size):
     return pl.ds(pl.multiple_of(start, size), size)
+
+
+def line_of(place):
+    for shift in (8, 4, 2, 1):
+        place = place ^ (place >> shift)
+    return place & 1
+
+
+def turned(chip, line, bits):
+    return (chip >> line) | ((chip & line) << (bits - 1))
+
+
+def relative(place, bits):
+    line = line_of(place)
+    return 2 * turned(place >> 1, line, bits) + line
+
+
+def partners(parts, k):
+    if k == 0:
+        return [(i, i ^ 1) for i in range(parts)]
+    bits = parts.bit_length() - 2
+    place = {relative(i, bits): i for i in range(parts)}
+    return [(i, place[relative(i, bits) ^ (1 << k)]) for i in range(parts)]
 
 
 def column(row):
@@ -63,7 +86,7 @@
     for copy in copies[:4]:
         copy.wait()
     me = lax.axis_index("dom")
-    bit = me & 1
+    line = line_of(me)
     parts, cap = lists.shape[1:]
     blocks, tile = hubs.shape
     vertices = choice.shape[1]
@@ -85,12 +108,11 @@
         return (vertex == index).astype(F32).astype(BF16)
 
     for part in range(parts):
-        stays = 1 - ((part & 1) ^ bit)
-        choice[pl.ds(pl.multiple_of(stays * half + (part >> 1) * cap, cap), cap), :] = onehot(
-            index[part]
-        )
+        stays = 1 - (line_of(part) ^ line)
+        place = turned(part >> 1, line_of(part), parts.bit_length() - 2)
+        choice[pl.ds(pl.multiple_of(stays * half + place * cap, cap), cap), :] = onehot(index[part])
     for b in range(2 * pairs):
-        stays = 1 - ((b & 1) ^ bit)
+        stays = 1 - ((b & 1) ^ line)
         there = pl.ds(pl.multiple_of(stays * half + border + (b >> 1) * tile, cap), tile)
         if b < blocks:
             mine = jnp.where(owner[b] == me, hubs[b : b + 1, :], -1)
@@ -134,15 +156,21 @@
 
 
 def step(k, parts, cap, last, keep, hub, received, *outs):
-    me = lax.axis_index("dom")
+    bits = parts.bit_length() - 2
+    me = relative(lax.axis_index("dom"), bits)
     bit = (me >> k) & 1
     border = parts * cap // 2
     merged = hub[hub.shape[0] - (received.shape[0] - border) :, :] + received[border:, :]
     run = (1 << k) * cap
     first, second = outs[-2:]
     if last:
-        first[rows(bit * run, run), :] = keep[:border, :]
-        first[rows((1 - bit) * run, run), :] = received[:border, :]
+        for group in range(parts // 2):
+            here = slice(group * cap, (group + 1) * cap)
+            chip = group >> 1
+            for top, values in ((bit, keep), (1 - bit, received)):
+                origin = jnp.where((me & 1) == 1, 2 * chip + top, chip + (top << (bits - 1)))
+                place = 2 * origin + (line_of(group) ^ top)
+                first[rows(place * cap, cap), :] = values[here, :]
         first[2 * border :, :] = merged
         second[...] = merged
         return
@@ -175,7 +203,7 @@
         )
     whole = pltpu.make_async_copy(degree_h, degree, sems.at[3, 0])
     whole.start()
-    bit = lax.axis_index("dom") & 1
+    line = line_of(lax.axis_index("dom"))
     count, tile = tiles.shape[1:3]
     near[...] = jnp.zeros_like(near)
     far[...] = jnp.zeros_like(far)
@@ -187,7 +215,7 @@
         for t in range(count):
             source = sources[i, t]
             if i == 2:
-                source = border + (source >> 1) + ((source & 1) ^ bit) * pairs
+                source = border + (source >> 1) + ((source & 1) ^ line) * pairs
             there = (rows(dests[i, t] * tile, tile), rows(source * tile, tile))
             sums[there] = sums[there] + tiles[i, t].astype(F32)
     whole.wait()
@@ -244,7 +272,7 @@
         return jax.ShapeDtypeStruct(shape, kind)
 
     def swap(x, k):
-        return lax.ppermute(x, "dom", [(i, i ^ (1 << k)) for i in range(parts)])
+        return lax.ppermute(x, "dom", partners(parts, k))
 
     if feats == 2:
         feature_blocks = [features, lax.ppermute(features, "feat", [(0, 1), (1, 0)])]

time: 26.3 us -> 25.6 us (0.973); the launches traced: 26.2 us -> 25.1 us
  waiting for transfers between devices: 9.87 us -> 8.51 us
    ppermute x5, waiting for transfers between devices: 7.51 us -> 6.15 us  [swap(): return lax.ppermute(x, 'dom', partners(parts, k))]
  transfers between devices with their start and end apart: 6 -> 6, of which waited for: 6 -> 6; matrix products, arithmetic and copies ran while one was open for 0% -> 0% of each run, Pallas kernels for 16% -> 17%
where the time goes in v4:
time: 25.6 us; the launch traced here: 25.1 us
  starting transfers between devices  9.89 us (39%)
  waiting for transfers between devices  8.51 us (33%)
  Pallas kernels  5.79 us (23%)
  local copies, waits for them, and re-layouts  0.71 us (3%)
    ppermute x5, starting transfers between devices, swap(): return lax.ppermute(x, 'dom', partners(parts, k))  6.95 us
    ppermute x5, waiting for transfers between devices, swap(): return lax.ppermute(x, 'dom', partners(parts, k))  6.15 us
    ppermute x1, starting transfers between devices, shards(): lax.ppermute(features, 'feat', [(0, 1), (1, 0)])  2.94 us
    ppermute x1, waiting for transfers between devices, shards(): lax.ppermute(features, 'feat', [(0, 1), (1, 0)])  2.35 us
    pallas_call x1, Pallas kernels, shards(): call(functools.partial(adjacency, (2 * border // tile, pairs)), (like(ver...  1.66 us
    pallas_call x1, Pallas kernels, shards(): call(choose, (like(2 * (border + hub), vertices), *early), [HBM] * 6, [pl...  1.34 us
    pallas_call x1, Pallas kernels, shards(): call(finish, like(width, vertices), [VM] * 4, size=1 << 20, name='finish')  1.02 us
    unnamed x26, local copies, waits for them, and re-layouts  0.71 us
  transfers between devices with their start and end apart: 6, of which 6 were waited for; matrix products, arithmetic and copies ran while one was open for 0% of the time, Pallas kernels for 17%

profile of v4, /device:TPU:0, one launch (start us, length us, event | category | flops | bytes accessed | tf_op | source)
XLA Modules:
  0.0 25.1 jit_solution(4454564041365859112)
XLA Ops:
  0.0 2.9 %collective-permute-start = (bf16[128,512]{1,0:T(8,128)(2,1)}, bf16[128,512]{1,0:T(8,128)(2,1)S(1)}, u32[]{:S(2)}, u32[]{:S(2)}) collective-permute-start(bf16[128,512]{1,0:T(8,128)(2,1)} %refs_0_.5), channel_id=1, source_target_pairs={{0,1},{1,0},{2,3},{3,2},{4,5},{5,4},{6,7},{7,6},{8,9},{9,8},{10,11... | collective-permute-start | bytes 393224 | tf_op jit(solution)/shard_map/ppermute | solution.py:278
  2.9 1.3 %choose.1 = (bf16[768,512]{1,0:T(8,128)(2,1)S(1)}, f32[128,512]{1,0:T(8,128)S(1)}, bf16[128,128]{1,0:T(8,128)(2,1)S(1)}) custom-call(s32[4]{0:T(128)} %refs_0_.3, s32[1,16,16]{2,1,0:T(8,128)} %refs_1_.2, s32[1,16]{1,0:T(1,128)} %refs_2_.2, s32[4,128]{1,0:T(4,128)} %refs_3_.2, bf16[128,512]{1,0:T(8,128)(2,1)} %refs_0_.5, bf16[128,256]{1,0:T(8,128)(2,1)} %refs_5_.2), custom_call_target="tpu_custom_call" | custom-call | bytes 2097152 | tf_op jit(solution)/shard_map/choose/pallas_call | solution.py:288
  4.3 2.4 %collective-permute-done.features.refs_1_ = bf16[128,512]{1,0:T(8,128)(2,1)S(1)} collective-permute-done((bf16[128,512]{1,0:T(8,128)(2,1)}, bf16[128,512]{1,0:T(8,128)(2,1)S(1)}, u32[]{:S(2)}, u32[]{:S(2)}) %collective-permute-start) | collective-permute-done | bytes 131104 | tf_op jit(solution)/shard_map/ppermute | solution.py:278
  6.6 0.4 %pick.1 = (bf16[128,512]{1,0:T(8,128)(2,1)S(1)}, bf16[384,128]{1,0:T(8,128)(2,1)S(1)}) custom-call(bf16[128,128]{1,0:T(8,128)(2,1)S(1)} %get-tuple-element.22.weight, bf16[128,512]{1,0:T(8,128)(2,1)S(1)} %collective-permute-done.features.refs_1_, bf16[768,512]{1,0:T(8,128)(2,1)S(1)} %get-tuple-element.23.choice, f32[128,512]{1,0:T(8,128)S(1)} %get-tuple-element.24.refs_0_), custom_call_target="tpu_custom_call" | custom-call | bytes 1048576 | tf_op jit(solution)/shard_map/pick/pallas_call | solution.py:302
  7.1 0.1 collective-permute-start.1
  7.1 0.0 copy-start
  7.2 0.0 copy-start.1
  7.2 0.3 %remain.1.keep.hub = bf16[384,128]{1,0:T(8,128)(2,1)S(1)} custom-call(bf16[128,512]{1,0:T(8,128)(2,1)S(1)} %get-tuple-element.25.projected, bf16[768,512]{1,0:T(8,128)(2,1)S(1)} %get-tuple-element.23.choice), custom_call_target="tpu_custom_call" | custom-call | bytes 1048576 | tf_op jit(solution)/shard_map/remain/pallas_call | solution.py:306
  7.4 1.0 %collective-permute-done.1.received = bf16[384,128]{1,0:T(8,128)(2,1)S(1)} collective-permute-done((bf16[384,128]{1,0:T(8,128)(2,1)S(1)}, bf16[384,128]{1,0:T(8,128)(2,1)S(1)}, u32[]{:S(2)}, u32[]{:S(2)}) %collective-permute-start.1) | collective-permute-done | bytes 98336 | tf_op jit(solution)/shard_map/ppermute | solution.py:275
  8.5 0.0 copy-start.5
  8.5 0.0 copy-start.6
  8.5 0.0 copy-start.7
  8.5 0.0 copy-start.8
  8.5 1.6 %collective-permute-start.2 = (bf16[384,128]{1,0:T(8,128)(2,1)S(1)}, bf16[384,128]{1,0:T(8,128)(2,1)S(1)}, u32[]{:S(2)}, u32[]{:S(2)}) collective-permute-start(bf16[384,128]{1,0:T(8,128)(2,1)S(1)} %get-tuple-element.27.refs_9_.b), channel_id=1, source_target_pairs={{0,6},{2,8},{4,14},{6,0},{8,2},{10,12},{12,10},{14,4},{16,26},{18,... | collective-permute-start | bytes 294920 | tf_op jit(solution)/shard_map/ppermute | solution.py:275
  10.1 0.0 copy-done.2
  10.1 0.0 copy-done.10
  10.1 0.0 copy-done.11
  10.2 0.0 copy-done.5
  10.2 0.0 copy-done.6
  10.2 1.7 %adjacency.1 = (bf16[512,512]{1,0:T(8,128)(2,1)S(1)}, bf16[512,512]{1,0:T(8,128)(2,1)S(1)}, bf16[512,768]{1,0:T(8,128)(2,1)S(1)}, bf16[512,768]{1,0:T(8,128)(2,1)S(1)}) custom-call(s32[1,512]{1,0:T(1,128)S(1)} %bitcast.2, s32[16]{0:T(128)S(1)} %copy-done.6, s32[16]{0:T(128)S(1)} %copy-done.7, bf16[16,128,128]{2,1,0:T(8,128)(2,1)S(1)} %copy-done, ...), custom_call_target="tpu_custom_call" | custom-call | bytes 6291456 | tf_op jit(solution)/shard_map/adjacency/pallas_call | solution.py:333
  11.9 0.8 %collective-permute-done.2.c = bf16[384,128]{1,0:T(8,128)(2,1)S(1)} collective-permute-done((bf16[384,128]{1,0:T(8,128)(2,1)S(1)}, bf16[384,128]{1,0:T(8,128)(2,1)S(1)}, u32[]{:S(2)}, u32[]{:S(2)}) %collective-permute-start.2) | collective-permute-done | bytes 98336 | tf_op jit(solution)/shard_map/ppermute | solution.py:275
  12.7 1.7 %collective-permute-start.3 = (bf16[384,128]{1,0:T(8,128)(2,1)S(1)}, bf16[384,128]{1,0:T(8,128)(2,1)S(1)}, u32[]{:S(2)}, u32[]{:S(2)}) collective-permute-start(bf16[384,128]{1,0:T(8,128)(2,1)S(1)} %get-tuple-element.32.refs_2_.b), channel_id=1, source_target_pairs={{0,10},{2,16},{4,22},{6,12},{8,26},{10,0},{12,6},{14,28},{16,2},{1... | collective-permute-start | bytes 294920 | tf_op jit(solution)/shard_map/ppermute | solution.py:275
  14.3 0.6 %copy-done.12 = f32[128]{0:T(128)S(1)} copy-done((f32[128]{0:T(128)S(1)}, f32[128]{0:T(128)}, u32[]{:S(2)}) %copy-start.12) | copy-done | bytes 536
  15.0 0.5 %own.1._.before = f32[512,128]{1,0:T(8,128)S(1)} custom-call(bf16[512,512]{1,0:T(8,128)(2,1)S(1)} %get-tuple-element.33.local_high, bf16[512,512]{1,0:T(8,128)(2,1)S(1)} %get-tuple-element.34.local_low, bf16[128,512]{1,0:T(8,128)(2,1)S(1)} %get-tuple-element.25.projected, bf16[128,256]{1,0:T(8,128)(2,1)S(1)} %copy-done.4, f32[1,128]{1,0:T(1,128)S(1)} %bitcast.3, ...), custom_call_target="tpu_custom_call" | custom-call | flops 167772160 | bytes 2097152 | tf_op jit(solution)/shard_map/own/pallas_call | solution.py:350
  15.5 1.4 %collective-permute-done.3.c = bf16[384,128]{1,0:T(8,128)(2,1)S(1)} collective-permute-done((bf16[384,128]{1,0:T(8,128)(2,1)S(1)}, bf16[384,128]{1,0:T(8,128)(2,1)S(1)}, u32[]{:S(2)}, u32[]{:S(2)}) %collective-permute-start.3) | collective-permute-done | bytes 98336 | tf_op jit(solution)/shard_map/ppermute | solution.py:275
  16.9 3.5 %collective-permute-start.4 = (bf16[384,128]{1,0:T(8,128)(2,1)S(1)}, bf16[384,128]{1,0:T(8,128)(2,1)S(1)}, u32[]{:S(2)}, u32[]{:S(2)}) collective-permute-start(bf16[384,128]{1,0:T(8,128)(2,1)S(1)} %get-tuple-element.36.hub), channel_id=1, source_target_pairs={{0,18},{2,4},{4,2},{6,20},{8,14},{10,24},{12,30},{14,8},{16,22},{1... | collective-permute-start | bytes 294920 | tf_op jit(solution)/shard_map/ppermute | solution.py:275
  20.4 2.3 %collective-permute-done.4.received = bf16[384,128]{1,0:T(8,128)(2,1)S(1)} collective-permute-done((bf16[384,128]{1,0:T(8,128)(2,1)S(1)}, bf16[384,128]{1,0:T(8,128)(2,1)S(1)}, u32[]{:S(2)}, u32[]{:S(2)}) %collective-permute-start.4) | collective-permute-done | bytes 98336 | tf_op jit(solution)/shard_map/ppermute | solution.py:275
  22.7 0.1 step3.1
  22.8 0.2 collective-permute-start.5
  22.9 0.4 %far.1.before = f32[512,128]{1,0:T(8,128)S(1)} custom-call(bf16[512,768]{1,0:T(8,128)(2,1)S(1)} %get-tuple-element.28.high, bf16[512,768]{1,0:T(8,128)(2,1)S(1)} %get-tuple-element.29._.low, bf16[512,128]{1,0:T(8,128)(2,1)S(1)} %get-tuple-element.38.near, f32[512,128]{1,0:T(8,128)S(1)} %own.1._.before), custom_call_target="tpu_custom_call" | custom-call | flops 134217728 | bytes 2097152 | tf_op jit(solution)/shard_map/far/pallas_call | solution.py:360
  23.4 0.7 %collective-permute-done.5.theirs = bf16[256,128]{1,0:T(8,128)(2,1)S(1)} collective-permute-done((bf16[256,128]{1,0:T(8,128)(2,1)S(1)}, bf16[256,128]{1,0:T(8,128)(2,1)S(1)}, u32[]{:S(2)}, u32[]{:S(2)}) %collective-permute-start.5) | collective-permute-done | bytes 65568 | tf_op jit(solution)/shard_map/ppermute | solution.py:275
  24.1 1.0 %finish.1 = bf16[128,512]{1,0:T(8,128)(2,1)} custom-call(bf16[512,768]{1,0:T(8,128)(2,1)S(1)} %get-tuple-element.28.high, bf16[512,768]{1,0:T(8,128)(2,1)S(1)} %get-tuple-element.29._.low, bf16[256,128]{1,0:T(8,128)(2,1)S(1)} %collective-permute-done.5.theirs, f32[512,128]{1,0:T(8,128)S(1)} %far.1.before), custom_call_target="tpu_custom_call" | custom-call | bytes 1048576 | tf_op jit(solution)/shard_map/finish/pallas_call | solution.py:364
  (17 shorter events, 0.1 us)
Async XLA Ops:
  0.0 6.6 %collective-permute-start = (bf16[128,512]{1,0:T(8,128)(2,1)}, bf16[128,512]{1,0:T(8,128)(2,1)S(1)}, u32[]{:S(2)}, u32[]{:S(2)}) collective-permute-start(bf16[128,512]{1,0:T(8,128)(2,1)} %refs_0_.5), channel_id=1, source_target_pairs={{0,1},{1,0},{2,3},{3,2},{4,5},{5,4},{6,7},{7,6},{8,9},{9,8},{10,11... | collective-permute-start | bytes 393224 | tf_op jit(solution)/shard_map/ppermute | solution.py:278
  6.6 3.5 %copy-start.2 = (bf16[16,128,128]{2,1,0:T(8,128)(2,1)S(1)}, bf16[16,128,128]{2,1,0:T(8,128)(2,1)}, u32[]{:S(2)}) copy-start(bf16[16,128,128]{2,1,0:T(8,128)(2,1)} %refs_8_.1) | copy-start | bytes 1572868
  7.1 1.4 %collective-permute-start.1 = (bf16[384,128]{1,0:T(8,128)(2,1)S(1)}, bf16[384,128]{1,0:T(8,128)(2,1)S(1)}, u32[]{:S(2)}, u32[]{:S(2)}) collective-permute-start(bf16[384,128]{1,0:T(8,128)(2,1)S(1)} %get-tuple-element.26), channel_id=1, source_target_pairs={{0,2},{2,0},{4,6},{6,4},{8,10},{10,8},{12,14},{14,12},{16,18},{18,... | collective-permute-start | bytes 294920 | tf_op jit(solution)/shard_map/ppermute | solution.py:275
  7.1 3.0 %copy-start = (bf16[16,128,128]{2,1,0:T(8,128)(2,1)S(1)}, bf16[16,128,128]{2,1,0:T(8,128)(2,1)}, u32[]{:S(2)}) copy-start(bf16[16,128,128]{2,1,0:T(8,128)(2,1)} %refs_2_.3) | copy-start | bytes 1572868
  7.2 3.0 %copy-start.1 = (bf16[16,128,128]{2,1,0:T(8,128)(2,1)S(1)}, bf16[16,128,128]{2,1,0:T(8,128)(2,1)}, u32[]{:S(2)}) copy-start(bf16[16,128,128]{2,1,0:T(8,128)(2,1)} %refs_5_.3) | copy-start | bytes 1572868
  8.4 1.7 %copy-start.9 = (s32[16]{0:T(128)S(1)}, s32[16]{0:T(128)}, u32[]{:S(2)}) copy-start(s32[16]{0:T(128)} %refs_4_.3) | copy-start | bytes 196
  8.4 1.7 %copy-start.10 = (s32[16]{0:T(128)S(1)}, s32[16]{0:T(128)}, u32[]{:S(2)}) copy-start(s32[16]{0:T(128)} %refs_6_.1) | copy-start | bytes 196
  8.4 1.7 %copy-start.11 = (s32[16]{0:T(128)S(1)}, s32[16]{0:T(128)}, u32[]{:S(2)}) copy-start(s32[16]{0:T(128)} %refs_7_.1) | copy-start | bytes 196
  8.5 1.7 %copy-start.5 = (s32[512]{0:T(512)S(1)}, s32[512]{0:T(512)}, u32[]{:S(2)}) copy-start(s32[512]{0:T(512)} %param.19) | copy-start | bytes 6148
  8.5 1.7 %copy-start.6 = (s32[16]{0:T(128)S(1)}, s32[16]{0:T(128)}, u32[]{:S(2)}) copy-start(s32[16]{0:T(128)} %refs_0_.4) | copy-start | bytes 196
  8.5 1.7 %copy-start.7 = (s32[16]{0:T(128)S(1)}, s32[16]{0:T(128)}, u32[]{:S(2)}) copy-start(s32[16]{0:T(128)} %refs_1_.3) | copy-start | bytes 196
  8.5 1.7 %copy-start.8 = (s32[16]{0:T(128)S(1)}, s32[16]{0:T(128)}, u32[]{:S(2)}) copy-start(s32[16]{0:T(128)} %refs_3_.3) | copy-start | bytes 196
  8.5 4.1 %collective-permute-start.2 = (bf16[384,128]{1,0:T(8,128)(2,1)S(1)}, bf16[384,128]{1,0:T(8,128)(2,1)S(1)}, u32[]{:S(2)}, u32[]{:S(2)}) collective-permute-start(bf16[384,128]{1,0:T(8,128)(2,1)S(1)} %get-tuple-element.27.refs_9_.b), channel_id=1, source_target_pairs={{0,6},{2,8},{4,14},{6,0},{8,2},{10,12},{12,10},{14,4},{16,26},{18,... | collective-permute-start | bytes 294920 | tf_op jit(solution)/shard_map/ppermute | solution.py:275
  12.6 1.7 %copy-start.3 = (bf16[128,512]{1,0:T(8,128)(2,1)S(1)}, bf16[128,512]{1,0:T(8,128)(2,1)}, u32[]{:S(2)}) copy-start(bf16[128,512]{1,0:T(8,128)(2,1)} %refs_0_.5) | copy-start | bytes 393220
  12.6 1.7 %copy-start.4 = (bf16[128,256]{1,0:T(8,128)(2,1)S(1)}, bf16[128,256]{1,0:T(8,128)(2,1)}, u32[]{:S(2)}) copy-start(bf16[128,256]{1,0:T(8,128)(2,1)} %weight.1) | copy-start | bytes 196612
  12.7 4.2 %collective-permute-start.3 = (bf16[384,128]{1,0:T(8,128)(2,1)S(1)}, bf16[384,128]{1,0:T(8,128)(2,1)S(1)}, u32[]{:S(2)}, u32[]{:S(2)}) collective-permute-start(bf16[384,128]{1,0:T(8,128)(2,1)S(1)} %get-tuple-element.32.refs_2_.b), channel_id=1, source_target_pairs={{0,10},{2,16},{4,22},{6,12},{8,26},{10,0},{12,6},{14,28},{16,2},{1... | collective-permute-start | bytes 294920 | tf_op jit(solution)/shard_map/ppermute | solution.py:275
  14.3 0.7 %copy-start.12 = (f32[128]{0:T(128)S(1)}, f32[128]{0:T(128)}, u32[]{:S(2)}) copy-start(f32[128]{0:T(128)} %param.35) | copy-start | bytes 1540
  16.9 5.8 %collective-permute-start.4 = (bf16[384,128]{1,0:T(8,128)(2,1)S(1)}, bf16[384,128]{1,0:T(8,128)(2,1)S(1)}, u32[]{:S(2)}, u32[]{:S(2)}) collective-permute-start(bf16[384,128]{1,0:T(8,128)(2,1)S(1)} %get-tuple-element.36.hub), channel_id=1, source_target_pairs={{0,18},{2,4},{4,2},{6,20},{8,14},{10,24},{12,30},{14,8},{16,22},{1... | collective-permute-start | bytes 294920 | tf_op jit(solution)/shard_map/ppermute | solution.py:275
  22.8 1.3 %collective-permute-start.5 = (bf16[256,128]{1,0:T(8,128)(2,1)S(1)}, bf16[256,128]{1,0:T(8,128)(2,1)S(1)}, u32[]{:S(2)}, u32[]{:S(2)}) collective-permute-start(bf16[256,128]{1,0:T(8,128)(2,1)S(1)} %get-tuple-element.37), channel_id=1, source_target_pairs={{0,2},{2,0},{4,6},{6,4},{8,10},{10,8},{12,14},{14,12},{16,18},{18,... | collective-permute-start | bytes 196616 | tf_op jit(solution)/shard_map/ppermute | solution.py:275

commit v5 on v4

--- a/solution.py
+++ b/solution.py
@@ -43,13 +43,19 @@
     return place & 1
 
 
+def order(line, bits):
+    down = list(range(bits))[::-1]
+    return down if line else down[-1:] + down[:-1]
+
+
 def turned(chip, line, bits):
-    return (chip >> line) | ((chip & line) << (bits - 1))
+    return sum(((chip >> b) & 1) << i for i, b in enumerate(order(line, bits)))
 
 
 def relative(place, bits):
     line = line_of(place)
-    return 2 * turned(place >> 1, line, bits) + line
+    chips = [turned(place >> 1, each, bits) for each in (0, 1)]
+    return 2 * (chips[0] + (chips[1] - chips[0]) * line) + line
 
 
 def partners(parts, k):
@@ -166,9 +172,16 @@
     if last:
         for group in range(parts // 2):
             here = slice(group * cap, (group + 1) * cap)
-            chip = group >> 1
+            chips = [
+                sum(((group >> (i + 1)) & 1) << b for i, b in enumerate(order(line, bits)))
+                for line in (0, 1)
+            ]
             for top, values in ((bit, keep), (1 - bit, received)):
-                origin = jnp.where((me & 1) == 1, 2 * chip + top, chip + (top << (bits - 1)))
+                origin = jnp.where(
+                    (me & 1) == 1,
+                    chips[1] + (top << order(1, bits)[-1]),
+                    chips[0] + (top << order(0, bits)[-1]),
+                )
                 place = 2 * origin + (line_of(group) ^ top)
                 first[rows(place * cap, cap), :] = values[here, :]
         first[2 * border :, :] = merged

time: 25.6 us -> 25.4 us (level); the launches traced: 25.1 us -> 25.2 us
  starting transfers between devices: 9.89 us -> 10.2 us
    ppermute x5, starting transfers between devices: 6.95 us -> 7.3 us  [swap(): return lax.ppermute(x, 'dom', partners(parts, k))]
where the time goes in v5:
time: 25.4 us; the launch traced here: 25.2 us
  starting transfers between devices  10.2 us (40%)
  waiting for transfers between devices  8.3 us (33%)
  Pallas kernels  5.8 us (23%)
  local copies, waits for them, and re-layouts  0.71 us (3%)
    ppermute x5, starting transfers between devices, swap(): return lax.ppermute(x, 'dom', partners(parts, k))  7.3 us
    ppermute x5, waiting for transfers between devices, swap(): return lax.ppermute(x, 'dom', partners(parts, k))  5.95 us
    ppermute x1, starting transfers between devices, shards(): lax.ppermute(features, 'feat', [(0, 1), (1, 0)])  2.94 us
    ppermute x1, waiting for transfers between devices, shards(): lax.ppermute(features, 'feat', [(0, 1), (1, 0)])  2.35 us
    pallas_call x1, Pallas kernels, shards(): call(functools.partial(adjacency, (2 * border // tile, pairs)), (like(ver...  1.66 us
    pallas_call x1, Pallas kernels, shards(): call(choose, (like(2 * (border + hub), vertices), *early), [HBM] * 6, [pl...  1.34 us
    pallas_call x1, Pallas kernels, shards(): call(finish, like(width, vertices), [VM] * 4, size=1 << 20, name='finish')  1.01 us
    unnamed x26, local copies, waits for them, and re-layouts  0.71 us
  transfers between devices with their start and end apart: 6, of which 6 were waited for; matrix products, arithmetic and copies ran while one was open for 0% of the time, Pallas kernels for 17%

profile of v5, /device:TPU:0, one launch (start us, length us, event | category | flops | bytes accessed | tf_op | source)
XLA Modules:
  0.0 25.2 jit_solution(9846642458105933401)
XLA Ops:
  0.0 2.9 %collective-permute-start = (bf16[128,512]{1,0:T(8,128)(2,1)}, bf16[128,512]{1,0:T(8,128)(2,1)S(1)}, u32[]{:S(2)}, u32[]{:S(2)}) collective-permute-start(bf16[128,512]{1,0:T(8,128)(2,1)} %refs_0_.5), channel_id=1, source_target_pairs={{0,1},{1,0},{2,3},{3,2},{4,5},{5,4},{6,7},{7,6},{8,9},{9,8},{10,11... | collective-permute-start | bytes 393224 | tf_op jit(solution)/shard_map/ppermute | solution.py:291
  2.9 1.3 %choose.1 = (bf16[768,512]{1,0:T(8,128)(2,1)S(1)}, f32[128,512]{1,0:T(8,128)S(1)}, bf16[128,128]{1,0:T(8,128)(2,1)S(1)}) custom-call(s32[4]{0:T(128)} %refs_0_.3, s32[1,16,16]{2,1,0:T(8,128)} %refs_1_.2, s32[1,16]{1,0:T(1,128)} %refs_2_.2, s32[4,128]{1,0:T(4,128)} %refs_3_.2, bf16[128,512]{1,0:T(8,128)(2,1)} %refs_0_.5, bf16[128,256]{1,0:T(8,128)(2,1)} %refs_5_.2), custom_call_target="tpu_custom_call" | custom-call | bytes 2097152 | tf_op jit(solution)/shard_map/choose/pallas_call | solution.py:301
  4.3 2.4 %collective-permute-done.features.refs_1_ = bf16[128,512]{1,0:T(8,128)(2,1)S(1)} collective-permute-done((bf16[128,512]{1,0:T(8,128)(2,1)}, bf16[128,512]{1,0:T(8,128)(2,1)S(1)}, u32[]{:S(2)}, u32[]{:S(2)}) %collective-permute-start) | collective-permute-done | bytes 131104 | tf_op jit(solution)/shard_map/ppermute | solution.py:291
  6.6 0.4 %pick.1 = (bf16[128,512]{1,0:T(8,128)(2,1)S(1)}, bf16[384,128]{1,0:T(8,128)(2,1)S(1)}) custom-call(bf16[128,128]{1,0:T(8,128)(2,1)S(1)} %get-tuple-element.22.weight, bf16[128,512]{1,0:T(8,128)(2,1)S(1)} %collective-permute-done.features.refs_1_, bf16[768,512]{1,0:T(8,128)(2,1)S(1)} %get-tuple-element.23.choice, f32[128,512]{1,0:T(8,128)S(1)} %get-tuple-element.24.refs_0_), custom_call_target="tpu_custom_call" | custom-call | bytes 1048576 | tf_op jit(solution)/shard_map/pick/pallas_call | solution.py:315
  7.1 0.1 collective-permute-start.1
  7.1 0.0 copy-start
  7.2 0.0 copy-start.1
  7.2 0.3 %remain.1.keep.hub = bf16[384,128]{1,0:T(8,128)(2,1)S(1)} custom-call(bf16[128,512]{1,0:T(8,128)(2,1)S(1)} %get-tuple-element.25.projected, bf16[768,512]{1,0:T(8,128)(2,1)S(1)} %get-tuple-element.23.choice), custom_call_target="tpu_custom_call" | custom-call | bytes 1048576 | tf_op jit(solution)/shard_map/remain/pallas_call | solution.py:319
  7.4 1.0 %collective-permute-done.1.received = bf16[384,128]{1,0:T(8,128)(2,1)S(1)} collective-permute-done((bf16[384,128]{1,0:T(8,128)(2,1)S(1)}, bf16[384,128]{1,0:T(8,128)(2,1)S(1)}, u32[]{:S(2)}, u32[]{:S(2)}) %collective-permute-start.1) | collective-permute-done | bytes 98336 | tf_op jit(solution)/shard_map/ppermute | solution.py:288
  8.5 0.0 copy-start.5
  8.5 0.0 copy-start.6
  8.5 0.0 copy-start.7
  8.5 0.0 copy-start.8
  8.5 1.6 %collective-permute-start.2 = (bf16[384,128]{1,0:T(8,128)(2,1)S(1)}, bf16[384,128]{1,0:T(8,128)(2,1)S(1)}, u32[]{:S(2)}, u32[]{:S(2)}) collective-permute-start(bf16[384,128]{1,0:T(8,128)(2,1)S(1)} %get-tuple-element.27.refs_9_.b), channel_id=1, source_target_pairs={{0,6},{2,16},{4,22},{6,0},{8,26},{10,12},{12,10},{14,28},{16,2},{1... | collective-permute-start | bytes 294920 | tf_op jit(solution)/shard_map/ppermute | solution.py:288
  10.1 0.0 copy-done.2
  10.1 0.0 copy-done
  10.1 0.0 copy-done.1
  10.1 0.0 copy-done.9
  10.1 0.0 copy-done.10
  10.2 1.7 %adjacency.1 = (bf16[512,512]{1,0:T(8,128)(2,1)S(1)}, bf16[512,512]{1,0:T(8,128)(2,1)S(1)}, bf16[512,768]{1,0:T(8,128)(2,1)S(1)}, bf16[512,768]{1,0:T(8,128)(2,1)S(1)}) custom-call(s32[1,512]{1,0:T(1,128)S(1)} %bitcast.2, s32[16]{0:T(128)S(1)} %copy-done.6, s32[16]{0:T(128)S(1)} %copy-done.7, bf16[16,128,128]{2,1,0:T(8,128)(2,1)S(1)} %copy-done, ...), custom_call_target="tpu_custom_call" | custom-call | bytes 6291456 | tf_op jit(solution)/shard_map/adjacency/pallas_call | solution.py:346
  11.9 0.8 %collective-permute-done.2.c = bf16[384,128]{1,0:T(8,128)(2,1)S(1)} collective-permute-done((bf16[384,128]{1,0:T(8,128)(2,1)S(1)}, bf16[384,128]{1,0:T(8,128)(2,1)S(1)}, u32[]{:S(2)}, u32[]{:S(2)}) %collective-permute-start.2) | collective-permute-done | bytes 98336 | tf_op jit(solution)/shard_map/ppermute | solution.py:288
  12.7 2.9 %collective-permute-start.3 = (bf16[384,128]{1,0:T(8,128)(2,1)S(1)}, bf16[384,128]{1,0:T(8,128)(2,1)S(1)}, u32[]{:S(2)}, u32[]{:S(2)}) collective-permute-start(bf16[384,128]{1,0:T(8,128)(2,1)S(1)} %get-tuple-element.32.refs_2_.b), channel_id=1, source_target_pairs={{0,18},{2,8},{4,14},{6,20},{8,2},{10,24},{12,30},{14,4},{16,26},{1... | collective-permute-start | bytes 294920 | tf_op jit(solution)/shard_map/ppermute | solution.py:288
  15.6 0.6 %copy-done.12 = f32[128]{0:T(128)S(1)} copy-done((f32[128]{0:T(128)S(1)}, f32[128]{0:T(128)}, u32[]{:S(2)}) %copy-start.12) | copy-done | bytes 536
  16.3 0.5 %own.1._.before = f32[512,128]{1,0:T(8,128)S(1)} custom-call(bf16[512,512]{1,0:T(8,128)(2,1)S(1)} %get-tuple-element.33.local_high, bf16[512,512]{1,0:T(8,128)(2,1)S(1)} %get-tuple-element.34.local_low, bf16[128,512]{1,0:T(8,128)(2,1)S(1)} %get-tuple-element.25.projected, bf16[128,256]{1,0:T(8,128)(2,1)S(1)} %copy-done.4, f32[1,128]{1,0:T(1,128)S(1)} %bitcast.3, ...), custom_call_target="tpu_custom_call" | custom-call | flops 167772160 | bytes 2097152 | tf_op jit(solution)/shard_map/own/pallas_call | solution.py:363
  16.8 1.4 %collective-permute-done.3.c = bf16[384,128]{1,0:T(8,128)(2,1)S(1)} collective-permute-done((bf16[384,128]{1,0:T(8,128)(2,1)S(1)}, bf16[384,128]{1,0:T(8,128)(2,1)S(1)}, u32[]{:S(2)}, u32[]{:S(2)}) %collective-permute-start.3) | collective-permute-done | bytes 98336 | tf_op jit(solution)/shard_map/ppermute | solution.py:288
  18.3 1.9 %collective-permute-start.4 = (bf16[384,128]{1,0:T(8,128)(2,1)S(1)}, bf16[384,128]{1,0:T(8,128)(2,1)S(1)}, u32[]{:S(2)}, u32[]{:S(2)}) collective-permute-start(bf16[384,128]{1,0:T(8,128)(2,1)S(1)} %get-tuple-element.36.hub), channel_id=1, source_target_pairs={{0,10},{2,4},{4,2},{6,12},{8,14},{10,0},{12,6},{14,8},{16,22},{18,... | collective-permute-start | bytes 294920 | tf_op jit(solution)/shard_map/ppermute | solution.py:288
  20.2 2.3 %collective-permute-done.4.received = bf16[384,128]{1,0:T(8,128)(2,1)S(1)} collective-permute-done((bf16[384,128]{1,0:T(8,128)(2,1)S(1)}, bf16[384,128]{1,0:T(8,128)(2,1)S(1)}, u32[]{:S(2)}, u32[]{:S(2)}) %collective-permute-start.4) | collective-permute-done | bytes 98336 | tf_op jit(solution)/shard_map/ppermute | solution.py:288
  22.5 0.1 step3.1
  22.6 0.7 %collective-permute-start.5 = (bf16[256,128]{1,0:T(8,128)(2,1)S(1)}, bf16[256,128]{1,0:T(8,128)(2,1)S(1)}, u32[]{:S(2)}, u32[]{:S(2)}) collective-permute-start(bf16[256,128]{1,0:T(8,128)(2,1)S(1)} %get-tuple-element.37), channel_id=1, source_target_pairs={{0,2},{2,0},{4,6},{6,4},{8,10},{10,8},{12,14},{14,12},{16,18},{18,... | collective-permute-start | bytes 196616 | tf_op jit(solution)/shard_map/ppermute | solution.py:288
  23.3 0.4 %far.1.before = f32[512,128]{1,0:T(8,128)S(1)} custom-call(bf16[512,768]{1,0:T(8,128)(2,1)S(1)} %get-tuple-element.28.high, bf16[512,768]{1,0:T(8,128)(2,1)S(1)} %get-tuple-element.29._.low, bf16[512,128]{1,0:T(8,128)(2,1)S(1)} %get-tuple-element.38.near, f32[512,128]{1,0:T(8,128)S(1)} %own.1._.before), custom_call_target="tpu_custom_call" | custom-call | flops 134217728 | bytes 2097152 | tf_op jit(solution)/shard_map/far/pallas_call | solution.py:373
  23.8 0.5 %collective-permute-done.5.theirs = bf16[256,128]{1,0:T(8,128)(2,1)S(1)} collective-permute-done((bf16[256,128]{1,0:T(8,128)(2,1)S(1)}, bf16[256,128]{1,0:T(8,128)(2,1)S(1)}, u32[]{:S(2)}, u32[]{:S(2)}) %collective-permute-start.5) | collective-permute-done | bytes 65568 | tf_op jit(solution)/shard_map/ppermute | solution.py:288
  24.2 1.0 %finish.1 = bf16[128,512]{1,0:T(8,128)(2,1)} custom-call(bf16[512,768]{1,0:T(8,128)(2,1)S(1)} %get-tuple-element.28.high, bf16[512,768]{1,0:T(8,128)(2,1)S(1)} %get-tuple-element.29._.low, bf16[256,128]{1,0:T(8,128)(2,1)S(1)} %collective-permute-done.5.theirs, f32[512,128]{1,0:T(8,128)S(1)} %far.1.before), custom_call_target="tpu_custom_call" | custom-call | bytes 1048576 | tf_op jit(solution)/shard_map/finish/pallas_call | solution.py:377
  (17 shorter events, 0.1 us)
Async XLA Ops:
  0.0 6.6 %collective-permute-start = (bf16[128,512]{1,0:T(8,128)(2,1)}, bf16[128,512]{1,0:T(8,128)(2,1)S(1)}, u32[]{:S(2)}, u32[]{:S(2)}) collective-permute-start(bf16[128,512]{1,0:T(8,128)(2,1)} %refs_0_.5), channel_id=1, source_target_pairs={{0,1},{1,0},{2,3},{3,2},{4,5},{5,4},{6,7},{7,6},{8,9},{9,8},{10,11... | collective-permute-start | bytes 393224 | tf_op jit(solution)/shard_map/ppermute | solution.py:291
  6.6 3.5 %copy-start.2 = (bf16[16,128,128]{2,1,0:T(8,128)(2,1)S(1)}, bf16[16,128,128]{2,1,0:T(8,128)(2,1)}, u32[]{:S(2)}) copy-start(bf16[16,128,128]{2,1,0:T(8,128)(2,1)} %refs_8_.1) | copy-start | bytes 1572868
  7.1 1.4 %collective-permute-start.1 = (bf16[384,128]{1,0:T(8,128)(2,1)S(1)}, bf16[384,128]{1,0:T(8,128)(2,1)S(1)}, u32[]{:S(2)}, u32[]{:S(2)}) collective-permute-start(bf16[384,128]{1,0:T(8,128)(2,1)S(1)} %get-tuple-element.26), channel_id=1, source_target_pairs={{0,2},{2,0},{4,6},{6,4},{8,10},{10,8},{12,14},{14,12},{16,18},{18,... | collective-permute-start | bytes 294920 | tf_op jit(solution)/shard_map/ppermute | solution.py:288
  7.1 3.0 %copy-start = (bf16[16,128,128]{2,1,0:T(8,128)(2,1)S(1)}, bf16[16,128,128]{2,1,0:T(8,128)(2,1)}, u32[]{:S(2)}) copy-start(bf16[16,128,128]{2,1,0:T(8,128)(2,1)} %refs_2_.3) | copy-start | bytes 1572868
  7.2 3.0 %copy-start.1 = (bf16[16,128,128]{2,1,0:T(8,128)(2,1)S(1)}, bf16[16,128,128]{2,1,0:T(8,128)(2,1)}, u32[]{:S(2)}) copy-start(bf16[16,128,128]{2,1,0:T(8,128)(2,1)} %refs_5_.3) | copy-start | bytes 1572868
  8.4 1.7 %copy-start.9 = (s32[16]{0:T(128)S(1)}, s32[16]{0:T(128)}, u32[]{:S(2)}) copy-start(s32[16]{0:T(128)} %refs_4_.3) | copy-start | bytes 196
  8.4 1.7 %copy-start.10 = (s32[16]{0:T(128)S(1)}, s32[16]{0:T(128)}, u32[]{:S(2)}) copy-start(s32[16]{0:T(128)} %refs_6_.1) | copy-start | bytes 196
  8.4 1.7 %copy-start.11 = (s32[16]{0:T(128)S(1)}, s32[16]{0:T(128)}, u32[]{:S(2)}) copy-start(s32[16]{0:T(128)} %refs_7_.1) | copy-start | bytes 196
  8.5 1.7 %copy-start.5 = (s32[512]{0:T(512)S(1)}, s32[512]{0:T(512)}, u32[]{:S(2)}) copy-start(s32[512]{0:T(512)} %param.19) | copy-start | bytes 6148
  8.5 1.7 %copy-start.6 = (s32[16]{0:T(128)S(1)}, s32[16]{0:T(128)}, u32[]{:S(2)}) copy-start(s32[16]{0:T(128)} %refs_0_.4) | copy-start | bytes 196
  8.5 1.7 %copy-start.7 = (s32[16]{0:T(128)S(1)}, s32[16]{0:T(128)}, u32[]{:S(2)}) copy-start(s32[16]{0:T(128)} %refs_1_.3) | copy-start | bytes 196
  8.5 1.7 %copy-start.8 = (s32[16]{0:T(128)S(1)}, s32[16]{0:T(128)}, u32[]{:S(2)}) copy-start(s32[16]{0:T(128)} %refs_3_.3) | copy-start | bytes 196
  8.5 4.1 %collective-permute-start.2 = (bf16[384,128]{1,0:T(8,128)(2,1)S(1)}, bf16[384,128]{1,0:T(8,128)(2,1)S(1)}, u32[]{:S(2)}, u32[]{:S(2)}) collective-permute-start(bf16[384,128]{1,0:T(8,128)(2,1)S(1)} %get-tuple-element.27.refs_9_.b), channel_id=1, source_target_pairs={{0,6},{2,16},{4,22},{6,0},{8,26},{10,12},{12,10},{14,28},{16,2},{1... | collective-permute-start | bytes 294920 | tf_op jit(solution)/shard_map/ppermute | solution.py:288
  12.6 3.0 %copy-start.3 = (bf16[128,512]{1,0:T(8,128)(2,1)S(1)}, bf16[128,512]{1,0:T(8,128)(2,1)}, u32[]{:S(2)}) copy-start(bf16[128,512]{1,0:T(8,128)(2,1)} %refs_0_.5) | copy-start | bytes 393220
  12.6 3.0 %copy-start.4 = (bf16[128,256]{1,0:T(8,128)(2,1)S(1)}, bf16[128,256]{1,0:T(8,128)(2,1)}, u32[]{:S(2)}) copy-start(bf16[128,256]{1,0:T(8,128)(2,1)} %weight.1) | copy-start | bytes 196612
  12.7 5.5 %collective-permute-start.3 = (bf16[384,128]{1,0:T(8,128)(2,1)S(1)}, bf16[384,128]{1,0:T(8,128)(2,1)S(1)}, u32[]{:S(2)}, u32[]{:S(2)}) collective-permute-start(bf16[384,128]{1,0:T(8,128)(2,1)S(1)} %get-tuple-element.32.refs_2_.b), channel_id=1, source_target_pairs={{0,18},{2,8},{4,14},{6,20},{8,2},{10,24},{12,30},{14,4},{16,26},{1... | collective-permute-start | bytes 294920 | tf_op jit(solution)/shard_map/ppermute | solution.py:288
  15.6 0.7 %copy-start.12 = (f32[128]{0:T(128)S(1)}, f32[128]{0:T(128)}, u32[]{:S(2)}) copy-start(f32[128]{0:T(128)} %param.35) | copy-start | bytes 1540
  18.3 4.3 %collective-permute-start.4 = (bf16[384,128]{1,0:T(8,128)(2,1)S(1)}, bf16[384,128]{1,0:T(8,128)(2,1)S(1)}, u32[]{:S(2)}, u32[]{:S(2)}) collective-permute-start(bf16[384,128]{1,0:T(8,128)(2,1)S(1)} %get-tuple-element.36.hub), channel_id=1, source_target_pairs={{0,10},{2,4},{4,2},{6,12},{8,14},{10,0},{12,6},{14,8},{16,22},{18,... | collective-permute-start | bytes 294920 | tf_op jit(solution)/shard_map/ppermute | solution.py:288
  22.6 1.6 %collective-permute-start.5 = (bf16[256,128]{1,0:T(8,128)(2,1)S(1)}, bf16[256,128]{1,0:T(8,128)(2,1)S(1)}, u32[]{:S(2)}, u32[]{:S(2)}) collective-permute-start(bf16[256,128]{1,0:T(8,128)(2,1)S(1)} %get-tuple-element.37), channel_id=1, source_target_pairs={{0,2},{2,0},{4,6},{6,4},{8,10},{10,8},{12,14},{14,12},{16,18},{18,... | collective-permute-start | bytes 196616 | tf_op jit(solution)/shard_map/ppermute | solution.py:288

commit v6 on v5

--- a/solution.py
+++ b/solution.py
@@ -52,10 +52,25 @@
     return sum(((chip >> b) & 1) << i for i, b in enumerate(order(line, bits)))
 
 
+def relative_chip(place, line, bits):
+    chips = [turned(place >> 1, each, bits) for each in (0, 1)]
+    return chips[0] + (chips[1] - chips[0]) * line
+
+
 def relative(place, bits):
     line = line_of(place)
-    chips = [turned(place >> 1, each, bits) for each in (0, 1)]
-    return 2 * (chips[0] + (chips[1] - chips[0]) * line) + line
+    return 2 * relative_chip(place, line, bits) + line
+
+
+def short_exchanges(hub_owner, parts):
+    bits = parts.bit_length() - 2
+    places = [relative_chip(hub_owner, line, bits) for line in (0, 1)]
+    block = jnp.arange(hub_owner.shape[0], dtype=jnp.int32)
+    place = jnp.where(block % 2 == 1, places[1], places[0])
+    apart = place[:, None] ^ place[None, :]
+    paired = (block[:, None] < block[None, :]) & ((block[:, None] - block[None, :]) % 2 == 0)
+    least = jnp.min(jnp.where(paired, apart, parts - 1))
+    return sum((least >> i > 0).astype(jnp.int32) for i in range(bits))
 
 
 def partners(parts, k):
@@ -81,7 +96,7 @@
 
 
 def choose(*refs):
-    inputs, (choice, *parts_out), scratch = refs[:6], refs[6:-7], refs[-7:]
+    inputs, (choice, marks, *parts_out), scratch = refs[:6], refs[6:-7], refs[-7:]
     owner, lists, count, hubs, features, weight, sems = scratch
     copies = [
         pltpu.make_async_copy(a, b, sems.at[i])
@@ -125,6 +140,18 @@
             choice[there, :] = onehot(column(mine))
         else:
             choice[there, :] = jnp.zeros((tile, vertices), BF16)
+    bits = parts.bit_length() - 2
+    mine = relative(me, bits) >> 1
+    for i in range(pairs):
+        block = jnp.minimum(2 * i + line, blocks - 1)
+        owned = relative_chip(owner[block], line, bits)
+        for k in range(bits):
+            there = ((mine >> k) ^ 1) == (owned >> k)
+            if 2 * i + 1 >= blocks:
+                there = there & (2 * i + line < blocks)
+            marks[k * pairs + i : k * pairs + i + 1, :] = jnp.full(
+                (1, marks.shape[1]), jnp.where(there, 1.0, 0.0), F32
+            )
     for copy in copies[4:]:
         copy.wait()
     if len(parts_out) == 2:
@@ -147,7 +174,7 @@
 
 
 def pick(weight, features, choice, *refs):
-    *known, projected, message = refs
+    *known, _, projected, message = refs
     total = dot(weight[...], features[...])
     if known:
         total = total + known[0][...]
@@ -161,14 +188,29 @@
     kept[...] = dot(choice[kept.shape[0] :, :], projected[...], LAST).astype(BF16)
 
 
-def step(k, parts, cap, last, keep, hub, received, *outs):
+def step(k, parts, cap, last, short, shorten, keep, hub, received, marks, _, *outs):
     bits = parts.bit_length() - 2
     me = relative(lax.axis_index("dom"), bits)
     bit = (me >> k) & 1
     border = parts * cap // 2
-    merged = hub[hub.shape[0] - (received.shape[0] - border) :, :] + received[border:, :]
+    size = outs[1].shape[0] if last else outs[2].shape[0]
+    held = hub[hub.shape[0] - size :, :]
+    if short:
+        tile = received.shape[0] - border
+        arrived = received[border:, :].astype(F32)
+        pairs = size // tile
+        merged = jnp.concatenate(
+            [
+                held[i * tile : (i + 1) * tile]
+                + (arrived * marks[(k - 1) * pairs + i : (k - 1) * pairs + i + 1, :]).astype(BF16)
+                for i in range(pairs)
+            ],
+            axis=0,
+        )
+    else:
+        merged = held + received[border:, :]
     run = (1 << k) * cap
-    first, second = outs[-2:]
+    first, second = outs[:2]
     if last:
         for group in range(parts // 2):
             here = slice(group * cap, (group + 1) * cap)
@@ -195,11 +237,17 @@
         first[theirs, :] = received[stay, :]
         second[mine, :] = keep[go, :]
         second[theirs, :] = received[go, :]
-    second[border:, :] = merged
+    outs[2][...] = merged
+    if shorten:
+        tile = second.shape[0] - border
+        pairs = size // tile
+        second[border:, :] = sum(merged[i * tile : (i + 1) * tile] for i in range(pairs))
+    else:
+        second[border:, :] = merged
 
 
 def adjacency(kinds, degree_h, *refs):
-    inputs, rest = refs[:9], refs[10:]
+    inputs, rest = refs[:9], refs[9:]
     local_high, local_low, far_high, far_low = rest[:4]
     degree, dests, sources, tiles, near, far, sems = rest[4:]
     copies = []
@@ -243,7 +291,7 @@
 
 
 def own_terms(local_high, local_low, projected, weight, bias, *refs):
-    *feature_blocks, _, total = refs
+    *feature_blocks, total = refs
     total[...] = (
         sum(dot(f, w, FIRST_LAST) for w, f in weight_parts(weight, feature_blocks))
         + dot(local_high[...], projected[...], LAST)
@@ -298,8 +346,14 @@
     early = ()
     if feats == 2:
         early = (like(width, vertices, kind=F32), like(width, features.shape[0]))
-    choice, *early = call(
-        choose, (like(2 * (border + hub), vertices), *early), [HBM] * 6,
+    choice, marks, *early = call(
+        choose,
+        (
+            like(2 * (border + hub), vertices),
+            like((steps - 1) * pairs, width, kind=F32),
+            *early,
+        ),
+        [HBM] * 6,
         [
             pltpu.SMEM(hub_owner.shape, jnp.int32),
             pltpu.VMEM(send_rows.shape, jnp.int32),
@@ -311,64 +365,71 @@
         ],
         size=2 << 20, name="choose",
     )(*fixed)
+    inputs = [
+        pltpu.with_memory_space_constraint(x, pltpu.HBM)
+        for x in (
+            in_degree.reshape(1, vertices), local_dest, local_source, local_tiles,
+            border_dest, border_source, border_tiles, hub_dest, hub_source, hub_tiles,
+        )
+    ]
+    local_high, local_low, far_high, far_low = call(
+        functools.partial(adjacency, (2 * border // tile, pairs)),
+        (like(vertices, near_size),) * 2 + (like(vertices, far_size),) * 2,
+        [HBM] * 10,
+        [
+            pltpu.VMEM((1, vertices), jnp.int32),
+            pltpu.SMEM((3, count), jnp.int32),
+            pltpu.SMEM((3, count), jnp.int32),
+            pltpu.VMEM((3, count, tile, tile), BF16),
+            pltpu.VMEM((vertices, near_size), F32),
+            pltpu.VMEM((vertices, far_size), F32),
+            pltpu.SemaphoreType.DMA((4, 3)),
+        ],
+        size=6 << 20, name="adjacency",
+    )(*inputs)
     weight, known = (early[1], early[:1]) if early else (neighbor_weight, [])
     projected, message = call(
-        pick, (like(width, vertices), like(border + hub, width)), [VM] * (3 + len(known)),
-        size=1 << 20, name="pick",
-    )(weight, feature_blocks[-1], choice, *known)
-    keep = held = call(
+        pick, (like(width, vertices), like(border + hub, width)),
+        [VM] * (3 + len(known)) + [ANY], size=1 << 20, name="pick",
+    )(weight, feature_blocks[-1], choice, *known, far_low)
+    received = swap(message, 0)
+    kept = call(
         remain, like(border + hub, width), [VM] * 2, size=1 << 20, name="remain"
     )(projected, choice)
-    inputs = (
-        local_dest, local_source, local_tiles, border_dest, border_source, border_tiles,
-        hub_dest, hub_source, hub_tiles,
-    )
-    waits = None
-    for k in range(steps):
-        received = swap(message, k)
-        last = k == steps - 1
-        specs, operands = [VM, VM, VM], (keep, held, received)
-        body = functools.partial(step, k, parts, cap, last)
-        if waits is not None:
-            specs, operands = specs + [ANY], operands + (waits,)
-            body = functools.partial(
-                lambda inner, a, b, c, _, *outs: inner(a, b, c, *outs), body
+    total = call(
+        own_terms, like(vertices, width, kind=F32), [VM] * (5 + len(feature_blocks)),
+        flops=4 * vertices * width * (near_size + width), size=2 << 20, name="own",
+    )(
+        local_high, local_low, projected, self_weight, out_bias.reshape(1, width), *feature_blocks
+    )
+
+    def chain(level, kept, received, marks, total):
+        keep = held = kept
+        for k in range(steps):
+            if k:
+                received = swap(message, k)
+            last, shorten = k == steps - 1, k + 1 <= level
+            outs = (
+                (like(2 * border + hub, width), like(hub, width))
+                if last
+                else (
+                    like(border, width),
+                    like(border + (tile if shorten else hub), width),
+                    like(hub, width),
+                )
             )
-        outs = (
-            (like(2 * border + hub, width), like(hub, width))
-            if last
-            else (like(border, width), like(border + hub, width))
-        )
-        keep, message = call(body, outs, specs, name=f"step{k}")(*operands)
-        held = message
-        waits = None
-        if k == 0:
-            local_high, local_low, far_high, far_low = call(
-                functools.partial(adjacency, (2 * border // tile, pairs)),
-                (like(vertices, near_size),) * 2 + (like(vertices, far_size),) * 2,
-                [HBM] * 10 + [ANY],
-                [
-                    pltpu.VMEM((1, vertices), jnp.int32),
-                    pltpu.SMEM((3, count), jnp.int32),
-                    pltpu.SMEM((3, count), jnp.int32),
-                    pltpu.VMEM((3, count, tile, tile), BF16),
-                    pltpu.VMEM((vertices, near_size), F32),
-                    pltpu.VMEM((vertices, far_size), F32),
-                    pltpu.SemaphoreType.DMA((4, 3)),
-                ],
-                size=6 << 20, name="adjacency",
-            )(in_degree.reshape(1, vertices), *inputs, message)
-            waits = far_low
-        if k == 1:
-            total = call(
-                own_terms, like(vertices, width, kind=F32),
-                [VM] * (5 + len(feature_blocks)) + [ANY],
-                flops=4 * vertices * width * (near_size + width), size=2 << 20, name="own",
-            )(
-                local_high, local_low, projected, self_weight, out_bias.reshape(1, width),
-                *feature_blocks, message,
-            )
-            waits = total
+            keep, message, *rest = call(
+                functools.partial(step, k, parts, cap, last, 1 <= k <= level, shorten),
+                outs, [VM] * 4 + [ANY], name=f"step{k}_{level}",
+            )(keep, held, received, marks, total)
+            held = rest[0] if rest else None
+        return keep, message
+
+    keep, message = lax.switch(
+        short_exchanges(hub_owner, parts),
+        [functools.partial(chain, level) for level in range(steps)],
+        kept, received, marks, total,
+    )
     theirs = swap(message, 0)
     total = call(
         far_terms, like(vertices, width, kind=F32), [VM] * 4,

time: 25.4 us -> 29.5 us (1.16)
  Pallas kernels: 5.8 us -> 8.57 us
  between operations: 0.19 us -> 1.75 us
  waiting for transfers between devices: 8.3 us -> 6.78 us
  other arithmetic: 0 us -> 0.68 us
  starting transfers between devices: 10.2 us -> 10.5 us
    ppermute x1, waiting for transfers between devices: 2.35 us -> 0.16 us  [shards(): lax.ppermute(features, 'feat', [(0, 1), (1, 0)])]
    pallas_call x5, Pallas kernels: 1.5 us -> 2.5 us  [the longest x1 1.34 us: shards(): call(choose, (like(2 * (border + hub), vertices), like((steps - 1) * pair...]
    reduce_min x0 -> x1, other arithmetic: none -> 0.67 us  [short_exchanges(): least = jnp.min(jnp.where(paired, apart, parts - 1))]
    ppermute x5, waiting for transfers between devices: 5.95 us -> 6.62 us  [swap(): return lax.ppermute(x, 'dom', partners(parts, k))]
    pallas_call x1, Pallas kernels: 0.25 us -> 0.91 us  [shards(): call(remain, like(border + hub, width), [VM] * 2, size=1 << 20, name='rem...]
    pallas_call x1, Pallas kernels: 0.41 us -> 1.04 us  [shards(): call(pick, (like(width, vertices), like(border + hub, width)), [VM] * (3...]
    pallas_call x1, Pallas kernels: 1.66 us -> 2.15 us  [shards(): call(functools.partial(adjacency, (2 * border // tile, pairs)), (like(ver...]
    unnamed x26 -> x12, local copies, waits for them, and re-layouts: 0.71 us -> 0.69 us
  transfers between devices with their start and end apart: 6 -> 6, of which waited for: 6 -> 5; matrix products, arithmetic and copies ran while one was open for 0% -> 2% of each run, Pallas kernels for 17% -> 18%
where the time goes in v6:
time: 29.5 us; the launch traced here: 29.1 us
  starting transfers between devices  10.5 us (36%)
  Pallas kernels  8.57 us (29%)
  waiting for transfers between devices  6.78 us (23%)
  between operations  1.75 us (6%)
  local copies, waits for them, and re-layouts  0.69 us (2%)
  other arithmetic  0.68 us (2%)
    ppermute x5, starting transfers between devices, swap(): return lax.ppermute(x, 'dom', partners(parts, k))  7.59 us
    ppermute x5, waiting for transfers between devices, swap(): return lax.ppermute(x, 'dom', partners(parts, k))  6.62 us
    ppermute x1, starting transfers between devices, shards(): lax.ppermute(features, 'feat', [(0, 1), (1, 0)])  2.94 us
    pallas_call x1, Pallas kernels, shards(): call(functools.partial(adjacency, (2 * border // tile, pairs)), (like(ver...  2.15 us
    pallas_call x1, Pallas kernels, shards(): call(choose, (like(2 * (border + hub), vertices), like((steps - 1) * pair...  1.34 us
    pallas_call x4, Pallas kernels, chain(): call(functools.partial(step, k, parts, cap, last, 1 <= k <= level, shorte...  1.16 us
    pallas_call x1, Pallas kernels, shards(): call(pick, (like(width, vertices), like(border + hub, width)), [VM] * (3...  1.04 us
    pallas_call x1, Pallas kernels, shards(): call(finish, like(width, vertices), [VM] * 4, size=1 << 20, name='finish')  1.01 us
  transfers between devices with their start and end apart: 6, of which 5 were waited for; matrix products, arithmetic and copies ran while one was open for 2% of the time, Pallas kernels for 18%

profile of v6, /device:TPU:0, one launch (start us, length us, event | category | flops | bytes accessed | tf_op | source)
XLA Modules:
  0.0 29.1 jit_solution(3989503212443324411)
XLA Ops:
  0.0 2.9 %collective-permute-start.12 = (bf16[128,512]{1,0:T(8,128)(2,1)}, bf16[128,512]{1,0:T(8,128)(2,1)S(1)}, u32[]{:S(2)}, u32[]{:S(2)}) collective-permute-start(bf16[128,512]{1,0:T(8,128)(2,1)} %refs_0_.5), channel_id=1, source_target_pairs={{0,1},{1,0},{2,3},{3,2},{4,5},{5,4},{6,7},{7,6},{8,9},{9,8},{10,11... | collective-permute-start | bytes 393224 | tf_op jit(solution)/shard_map/ppermute | solution.py:339
  2.9 1.3 %choose.1 = (bf16[768,512]{1,0:T(8,128)(2,1)S(1)}, f32[6,128]{1,0:T(8,128)S(1)}, f32[128,512]{1,0:T(8,128)S(1)}, bf16[128,128]{1,0:T(8,128)(2,1)S(1)}) custom-call(s32[4]{0:T(128)} %refs_0_.4, s32[1,16,16]{2,1,0:T(8,128)} %refs_1_.3, s32[1,16]{1,0:T(1,128)} %refs_2_.3, s32[4,128]{1,0:T(4,128)} %refs_3_.3, bf16[128,512]{1,0:T(8,128)(2,1)} %refs_0_.5, ...), custom_call_target="tpu_custom_call" | custom-call | bytes 2097152 | tf_op jit(solution)/shard_map/choose/pallas_call | solution.py:349
  4.3 0.0 copy-start.5
  4.3 2.1 %adjacency.1 = (bf16[512,512]{1,0:T(8,128)(2,1)S(1)}, bf16[512,512]{1,0:T(8,128)(2,1)S(1)}, bf16[512,768]{1,0:T(8,128)(2,1)S(1)}, bf16[512,768]{1,0:T(8,128)(2,1)S(1)}) custom-call(s32[1,512]{1,0:T(1,128)} %bitcast.3, s32[16]{0:T(128)} %refs_0_.3, s32[16]{0:T(128)} %refs_1_.2, bf16[16,128,128]{2,1,0:T(8,128)(2,1)} %refs_2_.2, s32[16]{0:T(128)} %refs_3_.2, ...), custom_call_target="tpu_custom_call" | custom-call | bytes 6291456 | tf_op jit(solution)/shard_map/adjacency/pallas_call | solution.py:375
  6.5 0.0 copy-done.5
  6.5 0.2 collective-permute-done.12.features.refs_1_
  6.6 1.0 %pick.1 = (bf16[128,512]{1,0:T(8,128)(2,1)S(1)}, bf16[384,128]{1,0:T(8,128)(2,1)}) custom-call(bf16[128,128]{1,0:T(8,128)(2,1)S(1)} %get-tuple-element.103.weight, bf16[128,512]{1,0:T(8,128)(2,1)S(1)} %collective-permute-done.12.features.refs_1_, bf16[768,512]{1,0:T(8,128)(2,1)S(1)} %get-tuple-element.104.choice, f32[128,512]{1,0:T(8,128)S(1)} %get-tuple-element.105.refs_0_, ...), custom_call_target="tpu_custom_call" | custom-call | bytes 1048576 | tf_op jit(solution)/shard_map/pick/pallas_call | solution.py:391
  7.7 0.0 copy-done.1
  7.7 0.0 collective-permute-start.13
  7.7 0.7 %select_reduce_fusion = s32[]{:T(128)} fusion(s32[4]{0:T(128)S(1)} %compare_select_fusion), kind=kLoop, calls=%fused_computation.8 | loop fusion | flops 287 | bytes 20 | tf_op jit(solution)/shard_map/reduce_min | solution.py:72
  10.0 0.0 copy-start
  10.0 0.0 copy-start.2
  10.1 0.0 copy-start.3
  10.1 0.9 %remain.1 = bf16[384,128]{1,0:T(8,128)(2,1)} custom-call(bf16[128,512]{1,0:T(8,128)(2,1)S(1)} %get-tuple-element.106.projected, bf16[768,512]{1,0:T(8,128)(2,1)S(1)} %get-tuple-element.104.choice), custom_call_target="tpu_custom_call" | custom-call | bytes 1048576 | tf_op jit(solution)/shard_map/remain/pallas_call | solution.py:396
  11.0 0.0 copy-done.2
  11.0 0.0 copy-done.3
  11.0 0.6 %copy-done.4 = f32[128]{0:T(128)S(1)} copy-done((f32[128]{0:T(128)S(1)}, f32[128]{0:T(128)}, u32[]{:S(2)}) %copy-start.4) | copy-done | bytes 536
  11.6 0.5 %own.1.before = f32[512,128]{1,0:T(8,128)S(1)} custom-call(bf16[512,512]{1,0:T(8,128)(2,1)S(1)} %get-tuple-element.109.local_high, bf16[512,512]{1,0:T(8,128)(2,1)S(1)} %get-tuple-element.110.local_low, bf16[128,512]{1,0:T(8,128)(2,1)S(1)} %get-tuple-element.106.projected, bf16[128,256]{1,0:T(8,128)(2,1)S(1)} %copy-done.3, f32[1,128]{1,0:T(1,128)S(1)} %bitcast.2, ...), custom_call_target="tpu_custom_call" | custom-call | flops 167772160 | bytes 2097152 | tf_op jit(solution)/shard_map/own/pallas_call | solution.py:399
  12.2 0.0 collective-permute-done.13
  12.2 14.5 %conditional.1 = ((bf16[512,128]{1,0:T(8,128)(2,1)S(1)}, bf16[256,128]{1,0:T(8,128)(2,1)S(1)})) conditional(s32[]{:T(128)} %clamp.3, (bf16[384,128]{1,0:T(8,128)(2,1)}, bf16[384,128]{1,0:T(8,128)(2,1)}, f32[6,128]{1,0:T(8,128)S(1)}, f32[512,128]{1,0:T(8,128)S(1)}) %tuple.17, (bf16[384,128]{1,0:T(8,128)(2,1)}, ...), branch_computations={%region_1.2_spmd, %region_2.3_spmd, %region_3.4_spmd, %region_4.5_... | conditional | bytes 1179776 | solution.py:428
  12.2 1.0 %step0_3.1 = (bf16[128,128]{1,0:T(8,128)(2,1)S(1)}, bf16[256,128]{1,0:T(8,128)(2,1)S(1)}, bf16[256,128]{1,0:T(8,128)(2,1)S(1)}) custom-call(bf16[384,128]{1,0:T(8,128)(2,1)} %get-tuple-element.76.keep.hub, bf16[384,128]{1,0:T(8,128)(2,1)} %get-tuple-element.76.keep.hub, bf16[384,128]{1,0:T(8,128)(2,1)} %get-tuple-element.77.received, ...), custom_call_target="tpu_custom_call" | custom-call | tf_op jit(solution)/shard_map/cond/branch_3_fun/step0_3/pallas_call | solution.py:421
  13.3 1.9 %collective-permute-start.9 = (bf16[256,128]{1,0:T(8,128)(2,1)S(1)}, bf16[256,128]{1,0:T(8,128)(2,1)S(1)}, u32[]{:S(2)}, u32[]{:S(2)}) collective-permute-start(bf16[256,128]{1,0:T(8,128)(2,1)S(1)} %get-tuple-element.82), channel_id=1, source_target_pairs={{0,6},{2,16},{4,22},{6,0},{8,26},{10,12},{12,10},{14,28},{16,2},{1... | collective-permute-start | bytes 196616 | tf_op jit(solution)/shard_map/cond/branch_3_fun/ppermute | solution.py:336
  15.2 2.0 %collective-permute-done.9.received = bf16[256,128]{1,0:T(8,128)(2,1)S(1)} collective-permute-done((bf16[256,128]{1,0:T(8,128)(2,1)S(1)}, bf16[256,128]{1,0:T(8,128)(2,1)S(1)}, u32[]{:S(2)}, u32[]{:S(2)}) %collective-permute-start.9) | collective-permute-done | bytes 65568 | tf_op jit(solution)/shard_map/cond/branch_3_fun/ppermute | solution.py:336
  17.2 3.2 %collective-permute-start.10 = (bf16[256,128]{1,0:T(8,128)(2,1)S(1)}, bf16[256,128]{1,0:T(8,128)(2,1)S(1)}, u32[]{:S(2)}, u32[]{:S(2)}) collective-permute-start(bf16[256,128]{1,0:T(8,128)(2,1)S(1)} %get-tuple-element.85), channel_id=1, source_target_pairs={{0,18},{2,8},{4,14},{6,20},{8,2},{10,24},{12,30},{14,4},{16,26},{1... | collective-permute-start | bytes 196616 | tf_op jit(solution)/shard_map/cond/branch_3_fun/ppermute | solution.py:336
  20.4 2.0 %collective-permute-done.10.received = bf16[256,128]{1,0:T(8,128)(2,1)S(1)} collective-permute-done((bf16[256,128]{1,0:T(8,128)(2,1)S(1)}, bf16[256,128]{1,0:T(8,128)(2,1)S(1)}, u32[]{:S(2)}, u32[]{:S(2)}) %collective-permute-start.10) | collective-permute-done | bytes 65568 | tf_op jit(solution)/shard_map/cond/branch_3_fun/ppermute | solution.py:336
  22.4 2.3 %collective-permute-start.11 = (bf16[256,128]{1,0:T(8,128)(2,1)S(1)}, bf16[256,128]{1,0:T(8,128)(2,1)S(1)}, u32[]{:S(2)}, u32[]{:S(2)}) collective-permute-start(bf16[256,128]{1,0:T(8,128)(2,1)S(1)} %get-tuple-element.88), channel_id=1, source_target_pairs={{0,10},{2,4},{4,2},{6,12},{8,14},{10,0},{12,6},{14,8},{16,22},{18,... | collective-permute-start | bytes 196616 | tf_op jit(solution)/shard_map/cond/branch_3_fun/ppermute | solution.py:336
  24.7 2.0 %collective-permute-done.11.received = bf16[256,128]{1,0:T(8,128)(2,1)S(1)} collective-permute-done((bf16[256,128]{1,0:T(8,128)(2,1)S(1)}, bf16[256,128]{1,0:T(8,128)(2,1)S(1)}, u32[]{:S(2)}, u32[]{:S(2)}) %collective-permute-start.11) | collective-permute-done | bytes 65568 | tf_op jit(solution)/shard_map/cond/branch_3_fun/ppermute | solution.py:336
  26.7 0.1 step3_3.1
  26.7 0.2 collective-permute-start.14
  26.9 0.4 %far.1.before = f32[512,128]{1,0:T(8,128)S(1)} custom-call(bf16[512,768]{1,0:T(8,128)(2,1)S(1)} %get-tuple-element.101.high, bf16[512,768]{1,0:T(8,128)(2,1)S(1)} %get-tuple-element.102.refs_1_.low, bf16[512,128]{1,0:T(8,128)(2,1)S(1)} %get-tuple-element.112.near, f32[512,128]{1,0:T(8,128)S(1)} %own.1.before), custom_call_target="tpu_custom_call" | custom-call | flops 134217728 | bytes 2097152 | tf_op jit(solution)/shard_map/far/pallas_call | solution.py:434
  27.3 0.7 %collective-permute-done.14.theirs = bf16[256,128]{1,0:T(8,128)(2,1)S(1)} collective-permute-done((bf16[256,128]{1,0:T(8,128)(2,1)S(1)}, bf16[256,128]{1,0:T(8,128)(2,1)S(1)}, u32[]{:S(2)}, u32[]{:S(2)}) %collective-permute-start.14) | collective-permute-done | bytes 65568 | tf_op jit(solution)/shard_map/ppermute | solution.py:336
  28.0 1.0 %finish.1 = bf16[128,512]{1,0:T(8,128)(2,1)} custom-call(bf16[512,768]{1,0:T(8,128)(2,1)S(1)} %get-tuple-element.101.high, bf16[512,768]{1,0:T(8,128)(2,1)S(1)} %get-tuple-element.102.refs_1_.low, bf16[256,128]{1,0:T(8,128)(2,1)S(1)} %collective-permute-done.14.theirs, f32[512,128]{1,0:T(8,128)S(1)} %far.1.before), custom_call_target="tpu_custom_call" | custom-call | bytes 1048576 | tf_op jit(solution)/shard_map/finish/pallas_call | solution.py:438
  (6 shorter events, 0.1 us)
Async XLA Ops:
  0.0 6.6 %collective-permute-start.12 = (bf16[128,512]{1,0:T(8,128)(2,1)}, bf16[128,512]{1,0:T(8,128)(2,1)S(1)}, u32[]{:S(2)}, u32[]{:S(2)}) collective-permute-start(bf16[128,512]{1,0:T(8,128)(2,1)} %refs_0_.5), channel_id=1, source_target_pairs={{0,1},{1,0},{2,3},{3,2},{4,5},{5,4},{6,7},{7,6},{8,9},{9,8},{10,11... | collective-permute-start | bytes 393224 | tf_op jit(solution)/shard_map/ppermute | solution.py:339
  4.3 2.2 %copy-start.5 = (s32[4]{0:T(128)S(1)}, s32[4]{0:T(128)}, u32[]{:S(2)}) copy-start(s32[4]{0:T(128)} %refs_0_.4) | copy-start | bytes 52
  6.6 1.0 %copy-start.1 = (bf16[128,512]{1,0:T(8,128)(2,1)}, bf16[128,512]{1,0:T(8,128)(2,1)S(1)}, u32[]{:S(2)}) copy-start(bf16[128,512]{1,0:T(8,128)(2,1)S(1)} %collective-permute-done.12.features.refs_1_) | copy-start | bytes 393220
  7.7 4.5 %collective-permute-start.13 = (bf16[384,128]{1,0:T(8,128)(2,1)}, bf16[384,128]{1,0:T(8,128)(2,1)}, u32[]{:S(2)}, u32[]{:S(2)}) collective-permute-start(bf16[384,128]{1,0:T(8,128)(2,1)} %get-tuple-element.107), channel_id=1, source_target_pairs={{0,2},{2,0},{4,6},{6,4},{8,10},{10,8},{12,14},{14,12},{16,18},{18,... | collective-permute-start | bytes 294920 | tf_op jit(solution)/shard_map/ppermute | solution.py:336
  10.0 0.9 %copy-start = (bf16[128,512]{1,0:T(8,128)(2,1)S(1)}, bf16[128,512]{1,0:T(8,128)(2,1)}, u32[]{:S(2)}) copy-start(bf16[128,512]{1,0:T(8,128)(2,1)} %refs_0_.5) | copy-start | bytes 393220
  10.0 1.0 %copy-start.2 = (bf16[128,512]{1,0:T(8,128)(2,1)S(1)}, bf16[128,512]{1,0:T(8,128)(2,1)}, u32[]{:S(2)}) copy-start(bf16[128,512]{1,0:T(8,128)(2,1)} %copy-done.1) | copy-start | bytes 393220
  10.1 1.0 %copy-start.3 = (bf16[128,256]{1,0:T(8,128)(2,1)S(1)}, bf16[128,256]{1,0:T(8,128)(2,1)}, u32[]{:S(2)}) copy-start(bf16[128,256]{1,0:T(8,128)(2,1)} %weight.1) | copy-start | bytes 196612
  11.0 0.7 %copy-start.4 = (f32[128]{0:T(128)S(1)}, f32[128]{0:T(128)}, u32[]{:S(2)}) copy-start(f32[128]{0:T(128)} %param.39) | copy-start | bytes 1540
  13.3 3.9 %collective-permute-start.9 = (bf16[256,128]{1,0:T(8,128)(2,1)S(1)}, bf16[256,128]{1,0:T(8,128)(2,1)S(1)}, u32[]{:S(2)}, u32[]{:S(2)}) collective-permute-start(bf16[256,128]{1,0:T(8,128)(2,1)S(1)} %get-tuple-element.82), channel_id=1, source_target_pairs={{0,6},{2,16},{4,22},{6,0},{8,26},{10,12},{12,10},{14,28},{16,2},{1... | collective-permute-start | bytes 196616 | tf_op jit(solution)/shard_map/cond/branch_3_fun/ppermute | solution.py:336
  17.2 5.2 %collective-permute-start.10 = (bf16[256,128]{1,0:T(8,128)(2,1)S(1)}, bf16[256,128]{1,0:T(8,128)(2,1)S(1)}, u32[]{:S(2)}, u32[]{:S(2)}) collective-permute-start(bf16[256,128]{1,0:T(8,128)(2,1)S(1)} %get-tuple-element.85), channel_id=1, source_target_pairs={{0,18},{2,8},{4,14},{6,20},{8,2},{10,24},{12,30},{14,4},{16,26},{1... | collective-permute-start | bytes 196616 | tf_op jit(solution)/shard_map/cond/branch_3_fun/ppermute | solution.py:336
  22.4 4.2 %collective-permute-start.11 = (bf16[256,128]{1,0:T(8,128)(2,1)S(1)}, bf16[256,128]{1,0:T(8,128)(2,1)S(1)}, u32[]{:S(2)}, u32[]{:S(2)}) collective-permute-start(bf16[256,128]{1,0:T(8,128)(2,1)S(1)} %get-tuple-element.88), channel_id=1, source_target_pairs={{0,10},{2,4},{4,2},{6,12},{8,14},{10,0},{12,6},{14,8},{16,22},{18,... | collective-permute-start | bytes 196616 | tf_op jit(solution)/shard_map/cond/branch_3_fun/ppermute | solution.py:336
  26.7 1.3 %collective-permute-start.14 = (bf16[256,128]{1,0:T(8,128)(2,1)S(1)}, bf16[256,128]{1,0:T(8,128)(2,1)S(1)}, u32[]{:S(2)}, u32[]{:S(2)}) collective-permute-start(bf16[256,128]{1,0:T(8,128)(2,1)S(1)} %get-tuple-element.111), channel_id=1, source_target_pairs={{0,2},{2,0},{4,6},{6,4},{8,10},{10,8},{12,14},{14,12},{16,18},{18,... | collective-permute-start | bytes 196616 | tf_op jit(solution)/shard_map/ppermute | solution.py:336

commit v7 on v6

--- a/solution.py
+++ b/solution.py
@@ -10,20 +10,21 @@
 BF16 = jnp.bfloat16
 F32 = jnp.float32
 VM = pl.BlockSpec(memory_space=pltpu.VMEM)
+SM = pl.BlockSpec(memory_space=pltpu.SMEM)
 ANY = pl.BlockSpec(memory_space=pl.ANY)
 HBM = pl.BlockSpec(memory_space=pltpu.HBM)
 LAST = (((1,), (1,)), ((), ()))
 FIRST_LAST = (((0,), (1,)), ((), ()))
 
 
-def call(body, outs, specs, scratch=(), flops=0, size=0, name=None):
+def call(body, outs, specs, scratch=(), flops=0, size=0, name=None, room=8 << 20):
     return pl.pallas_call(
         body,
         out_shape=outs,
         in_specs=specs,
-        out_specs=jax.tree.map(lambda _: VM, outs),
+        out_specs=jax.tree.map(lambda out: SM if out.dtype == jnp.int32 else VM, outs),
         scratch_shapes=scratch,
-        compiler_params=pltpu.CompilerParams(vmem_limit_bytes=40 << 20),
+        compiler_params=pltpu.CompilerParams(vmem_limit_bytes=room),
         cost_estimate=pl.CostEstimate(flops=flops, bytes_accessed=size, transcendentals=0),
         name=name,
     )
@@ -62,14 +63,13 @@
     return 2 * relative_chip(place, line, bits) + line
 
 
-def short_exchanges(hub_owner, parts):
+def short_exchanges(owner, blocks, parts):
     bits = parts.bit_length() - 2
-    places = [relative_chip(hub_owner, line, bits) for line in (0, 1)]
-    block = jnp.arange(hub_owner.shape[0], dtype=jnp.int32)
-    place = jnp.where(block % 2 == 1, places[1], places[0])
-    apart = place[:, None] ^ place[None, :]
-    paired = (block[:, None] < block[None, :]) & ((block[:, None] - block[None, :]) % 2 == 0)
-    least = jnp.min(jnp.where(paired, apart, parts - 1))
+    place = [turned(owner[b] >> 1, b & 1, bits) for b in range(blocks)]
+    least = jnp.int32(parts - 1)
+    for b in range(blocks):
+        for other in range(b % 2, b, 2):
+            least = jnp.minimum(least, place[b] ^ place[other])
     return sum((least >> i > 0).astype(jnp.int32) for i in range(bits))
 
 
@@ -96,11 +96,12 @@
 
 
 def choose(*refs):
-    inputs, (choice, marks, *parts_out), scratch = refs[:6], refs[6:-7], refs[-7:]
-    owner, lists, count, hubs, features, weight, sems = scratch
+    inputs, outs, scratch = refs[:8], refs[8:-6], refs[-6:]
+    choice, marks, level, features, self_weight, bias, *parts_out = outs
+    owner, lists, count, hubs, weight, sems = scratch
+    landing = (owner, lists, count, hubs, features, weight, self_weight, bias)
     copies = [
-        pltpu.make_async_copy(a, b, sems.at[i])
-        for i, (a, b) in enumerate(zip(inputs, scratch[:6]))
+        pltpu.make_async_copy(a, b, sems.at[i]) for i, (a, b) in enumerate(zip(inputs, landing))
     ]
     for copy in copies:
         copy.start()
@@ -140,6 +141,7 @@
             choice[there, :] = onehot(column(mine))
         else:
             choice[there, :] = jnp.zeros((tile, vertices), BF16)
+    level[0] = short_exchanges(owner, blocks, parts)
     bits = parts.bit_length() - 2
     mine = relative(me, bits) >> 1
     for i in range(pairs):
@@ -238,18 +240,23 @@
         second[mine, :] = keep[go, :]
         second[theirs, :] = received[go, :]
     outs[2][...] = merged
-    if shorten:
-        tile = second.shape[0] - border
+    brief = outs[3] if shorten is None else second
+    if shorten is None:
+        second[border:, :] = merged
+        brief[:border, :] = second[:border, :]
+    if shorten is False:
+        second[border:, :] = merged
+    else:
+        tile = brief.shape[0] - border
         pairs = size // tile
-        second[border:, :] = sum(merged[i * tile : (i + 1) * tile] for i in range(pairs))
-    else:
-        second[border:, :] = merged
+        brief[border:, :] = sum(merged[i * tile : (i + 1) * tile] for i in range(pairs))
 
 
 def adjacency(kinds, degree_h, *refs):
     inputs, rest = refs[:9], refs[9:]
-    local_high, local_low, far_high, far_low = rest[:4]
-    degree, dests, sources, tiles, near, far, sems = rest[4:]
+    local_high, local_low, far_high, far_low, token = rest[:5]
+    degree, dests, sources, tiles, near, far, sems = rest[5:]
+    token[...] = jnp.zeros_like(token)
     copies = []
     for i in range(3):
         copies.append(
@@ -341,27 +348,33 @@
         feature_blocks = [lax.all_gather(features, "feat", axis=0, tiled=True)]
     fixed = [
         pltpu.with_memory_space_constraint(x, pltpu.HBM)
-        for x in (hub_owner, send_rows, send_count, hub_rows, features, neighbor_weight)
+        for x in (
+            hub_owner, send_rows, send_count, hub_rows, features, neighbor_weight, self_weight,
+            out_bias.reshape(1, width),
+        )
     ]
     early = ()
     if feats == 2:
         early = (like(width, vertices, kind=F32), like(width, features.shape[0]))
-    choice, marks, *early = call(
+    choice, marks, level, near_features, near_weight, bias, *early = call(
         choose,
         (
             like(2 * (border + hub), vertices),
             like((steps - 1) * pairs, width, kind=F32),
+            like(1, kind=jnp.int32),
+            like(*features.shape),
+            like(*self_weight.shape),
+            like(1, width, kind=F32),
             *early,
         ),
-        [HBM] * 6,
+        [HBM] * 8,
         [
             pltpu.SMEM(hub_owner.shape, jnp.int32),
             pltpu.VMEM(send_rows.shape, jnp.int32),
             pltpu.VMEM(send_count.shape, jnp.int32),
             pltpu.VMEM(hub_rows.shape, jnp.int32),
-            pltpu.VMEM(features.shape, BF16),
             pltpu.VMEM(neighbor_weight.shape, BF16),
-            pltpu.SemaphoreType.DMA((6,)),
+            pltpu.SemaphoreType.DMA((8,)),
         ],
         size=2 << 20, name="choose",
     )(*fixed)
@@ -372,9 +385,9 @@
             border_dest, border_source, border_tiles, hub_dest, hub_source, hub_tiles,
         )
     ]
-    local_high, local_low, far_high, far_low = call(
+    local_high, local_low, far_high, far_low, token = call(
         functools.partial(adjacency, (2 * border // tile, pairs)),
-        (like(vertices, near_size),) * 2 + (like(vertices, far_size),) * 2,
+        (like(vertices, near_size),) * 2 + (like(vertices, far_size),) * 2 + (like(8, 128, kind=F32),),
         [HBM] * 10,
         [
             pltpu.VMEM((1, vertices), jnp.int32),
@@ -385,13 +398,15 @@
             pltpu.VMEM((vertices, far_size), F32),
             pltpu.SemaphoreType.DMA((4, 3)),
         ],
-        size=6 << 20, name="adjacency",
+        size=6 << 20, name="adjacency", room=(4 << 20) + 8 * vertices * (near_size + far_size),
     )(*inputs)
+    if early:
+        feature_blocks[0] = near_features
     weight, known = (early[1], early[:1]) if early else (neighbor_weight, [])
     projected, message = call(
         pick, (like(width, vertices), like(border + hub, width)),
         [VM] * (3 + len(known)) + [ANY], size=1 << 20, name="pick",
-    )(weight, feature_blocks[-1], choice, *known, far_low)
+    )(weight, feature_blocks[-1], choice, *known, token)
     received = swap(message, 0)
     kept = call(
         remain, like(border + hub, width), [VM] * 2, size=1 << 20, name="remain"
@@ -400,14 +415,18 @@
         own_terms, like(vertices, width, kind=F32), [VM] * (5 + len(feature_blocks)),
         flops=4 * vertices * width * (near_size + width), size=2 << 20, name="own",
     )(
-        local_high, local_low, projected, self_weight, out_bias.reshape(1, width), *feature_blocks
-    )
-
-    def chain(level, kept, received, marks, total):
-        keep = held = kept
-        for k in range(steps):
-            if k:
-                received = swap(message, k)
+        local_high, local_low, projected, near_weight, bias, *feature_blocks
+    )
+
+    keep, message, held, brief = call(
+        functools.partial(step, 0, parts, cap, False, False, None),
+        (like(border, width), like(border + hub, width), like(hub, width), like(border + tile, width)),
+        [VM] * 4 + [ANY], name="step0",
+    )(kept, kept, received, marks, total)
+
+    def chain(level, keep, message, held, brief, marks):
+        for k in range(1, steps):
+            received = swap(brief if k == 1 <= level else message, k)
             last, shorten = k == steps - 1, k + 1 <= level
             outs = (
                 (like(2 * border + hub, width), like(hub, width))
@@ -419,16 +438,16 @@
                 )
             )
             keep, message, *rest = call(
-                functools.partial(step, k, parts, cap, last, 1 <= k <= level, shorten),
+                functools.partial(step, k, parts, cap, last, k <= level, shorten),
                 outs, [VM] * 4 + [ANY], name=f"step{k}_{level}",
-            )(keep, held, received, marks, total)
+            )(keep, held, received, marks, marks)
             held = rest[0] if rest else None
         return keep, message
 
     keep, message = lax.switch(
-        short_exchanges(hub_owner, parts),
+        level[0],
         [functools.partial(chain, level) for level in range(steps)],
-        kept, received, marks, total,
+        keep, message, held, brief, marks,
     )
     theirs = swap(message, 0)
     total = call(

time: 29.5 us -> 25.7 us (0.87)
  Pallas kernels: 8.57 us -> 6.68 us
  between operations: 1.75 us -> 0.73 us
  local copies, waits for them, and re-layouts: 0.69 us -> 0 us
  other arithmetic: 0.68 us -> 0 us
  waiting for transfers between devices: 6.78 us -> 7.31 us
    pallas_call x4, Pallas kernels: 1.16 us -> 0.17 us  [the longest x3 0.11 us: chain(): call(functools.partial(step, k, parts, cap, last, k <= level, shorten), o...]
    ppermute x5, waiting for transfers between devices: 6.62 us -> 7.31 us  [swap(): return lax.ppermute(x, 'dom', partners(parts, k))]
    unnamed x12 -> x0, local copies, waits for them, and re-layouts: 0.69 us -> none
    reduce_min x1 -> x0, other arithmetic: 0.67 us -> none  [short_exchanges(): least = jnp.min(jnp.where(paired, apart, parts - 1))]
    pallas_call x1, Pallas kernels: 0.91 us -> 0.25 us  [shards(): call(remain, like(border + hub, width), [VM] * 2, size=1 << 20, name='rem...]
    pallas_call x1, Pallas kernels: 1.04 us -> 0.4 us  [shards(): call(pick, (like(width, vertices), like(border + hub, width)), [VM] * (3...]
    pallas_call x1, Pallas kernels: 1.34 us -> 1.72 us  [shards(): call(choose, (like(2 * (border + hub), vertices), like((steps - 1) * pair...]
  transfers between devices with their start and end apart: 6 -> 6, of which waited for: 5 -> 4; matrix products, arithmetic and copies ran while one was open for 2% -> 0% of each run, Pallas kernels for 18% -> 20%
where the time goes in v7:
time: 25.7 us; the launch traced here: 25.5 us
  starting transfers between devices  10.7 us (42%)
  waiting for transfers between devices  7.31 us (28%)
  Pallas kernels  6.68 us (26%)
  between operations  0.73 us (3%)
    ppermute x5, starting transfers between devices, swap(): return lax.ppermute(x, 'dom', partners(parts, k))  7.81 us
    ppermute x5, waiting for transfers between devices, swap(): return lax.ppermute(x, 'dom', partners(parts, k))  7.31 us
    ppermute x1, starting transfers between devices, shards(): lax.ppermute(features, 'feat', [(0, 1), (1, 0)])  2.94 us
    pallas_call x1, Pallas kernels, shards(): call(functools.partial(adjacency, (2 * border // tile, pairs)), (like(ver...  2.15 us
    pallas_call x1, Pallas kernels, shards(): call(choose, (like(2 * (border + hub), vertices), like((steps - 1) * pair...  1.72 us
    pallas_call x1, Pallas kernels, shards(): call(finish, like(width, vertices), [VM] * 4, size=1 << 20, name='finish')  1.01 us
    pallas_call x1, Pallas kernels, shards(): call(own_terms, like(vertices, width, kind=F32), [VM] * (5 + len(feature_...  0.54 us
  transfers between devices with their start and end apart: 6, of which 4 were waited for; matrix products, arithmetic and copies ran while one was open for 0% of the time, Pallas kernels for 20%

profile of v7, /device:TPU:0, one launch (start us, length us, event | category | flops | bytes accessed | tf_op | source)
XLA Modules:
  0.0 25.5 jit_solution(7690712305809364634)
XLA Ops:
  0.0 2.9 %collective-permute-start.12 = (bf16[128,512]{1,0:T(8,128)(2,1)}, bf16[128,512]{1,0:T(8,128)(2,1)S(1)}, u32[]{:S(2)}, u32[]{:S(2)}) collective-permute-start(bf16[128,512]{1,0:T(8,128)(2,1)} %refs_4_.3), channel_id=1, source_target_pairs={{0,1},{1,0},{2,3},{3,2},{4,5},{5,4},{6,7},{7,6},{8,9},{9,8},{10,11... | collective-permute-start | bytes 393224 | tf_op jit(solution)/shard_map/ppermute | solution.py:346
  2.9 1.7 %choose.1 = (bf16[768,512]{1,0:T(8,128)(2,1)S(1)}, f32[6,128]{1,0:T(8,128)S(1)}, s32[1]{0:T(128)}, bf16[128,512]{1,0:T(8,128)(2,1)S(1)}, bf16[128,256]{1,0:T(8,1...) custom-call(s32[4]{0:T(128)} %refs_0_.3, s32[1,16,16]{2,1,0:T(8,128)} %refs_1_.3, ...), custom_call_target="tpu_custom_call" | custom-call | bytes 2097152 | tf_op jit(solution)/shard_map/choose/pallas_call | solution.py:359
  4.7 2.2 %adjacency.1 = (bf16[512,512]{1,0:T(8,128)(2,1)S(1)}, bf16[512,512]{1,0:T(8,128)(2,1)S(1)}, bf16[512,768]{1,0:T(8,128)(2,1)S(1)}, bf16[512,768]{1,0:T(8,128)(2,1)S(1)}, f32[8,128]{1,0:T(8,128)S(1)}) custom-call(s32[1,512]{1,0:T(1,128)} %bitcast.3, s32[16]{0:T(128)} %refs_0_.2, s32[16]{0:T(128)} %refs_1_.2, bf16[16,128,128]{2,1,0:T(8,128)(2,1)} %refs_2_.2, ...), custom_call_target="tpu_custom_call" | custom-call | bytes 6291456 | tf_op jit(solution)/shard_map/adjacency/pallas_call | solution.py:388
  6.8 0.0 collective-permute-done.12.features.refs_1_
  6.8 0.4 %pick.1 = (bf16[128,512]{1,0:T(8,128)(2,1)S(1)}, bf16[384,128]{1,0:T(8,128)(2,1)S(1)}) custom-call(bf16[128,128]{1,0:T(8,128)(2,1)S(1)} %get-tuple-element.101.weight, bf16[128,512]{1,0:T(8,128)(2,1)S(1)} %collective-permute-done.12.features.refs_1_, bf16[768,512]{1,0:T(8,128)(2,1)S(1)} %get-tuple-element.102.choice, ...), custom_call_target="tpu_custom_call" | custom-call | bytes 1048576 | tf_op jit(solution)/shard_map/pick/pallas_call | solution.py:406
  7.2 0.1 collective-permute-start.13
  8.0 0.3 remain.1.keep.hub
  8.2 0.5 %own.1._.before = f32[512,128]{1,0:T(8,128)S(1)} custom-call(bf16[512,512]{1,0:T(8,128)(2,1)S(1)} %get-tuple-element.108.local_high, bf16[512,512]{1,0:T(8,128)(2,1)S(1)} %get-tuple-element.109.local_low, bf16[128,512]{1,0:T(8,128)(2,1)S(1)} %get-tuple-element.105.projected, bf16[128,256]{1,0:T(8,128)(2,1)S(1)} %get-tuple-element.110.weight, ...), custom_call_target="tpu_custom_call" | custom-call | flops 167772160 | bytes 2097152 | tf_op jit(solution)/shard_map/own/pallas_call | solution.py:414
  8.8 0.0 collective-permute-done.13.received
  8.8 0.1 step0.1
  8.8 14.3 %conditional.1 = ((bf16[512,128]{1,0:T(8,128)(2,1)S(1)}, bf16[256,128]{1,0:T(8,128)(2,1)S(1)})) conditional(s32[]{:T(128)} %bitcast.2, (bf16[384,128]{1,0:T(8,128)(2,1)S(1)}, bf16[128,128]{1,0:T(8,128)(2,1)S(1)}, bf16[256,128]{1,0:T(8,128)(2,1)S(1)}, f32[6,128]{1,0:T(8,128)S(1)}) %tuple.17, ...), branch_computations={%region_0.0_spmd, %region_1.0_spmd, %region_2.0_spmd, %region_3.0_... | conditional | bytes 1179776 | solution.py:447
  8.9 1.8 %collective-permute-start.3 = (bf16[256,128]{1,0:T(8,128)(2,1)S(1)}, bf16[256,128]{1,0:T(8,128)(2,1)S(1)}, u32[]{:S(2)}, u32[]{:S(2)}) collective-permute-start(bf16[256,128]{1,0:T(8,128)(2,1)S(1)} %get-tuple-element.49), channel_id=1, source_target_pairs={{0,6},{2,16},{4,22},{6,0},{8,26},{10,12},{12,10},{14,28},{16,2},{1... | collective-permute-start | bytes 196616 | tf_op jit(solution)/shard_map/cond/branch_1_fun/ppermute | solution.py:343
  10.6 2.0 %collective-permute-done.3.received = bf16[256,128]{1,0:T(8,128)(2,1)S(1)} collective-permute-done((bf16[256,128]{1,0:T(8,128)(2,1)S(1)}, bf16[256,128]{1,0:T(8,128)(2,1)S(1)}, u32[]{:S(2)}, u32[]{:S(2)}) %collective-permute-start.3) | collective-permute-done | bytes 65568 | tf_op jit(solution)/shard_map/cond/branch_1_fun/ppermute | solution.py:343
  12.7 3.1 %collective-permute-start.4 = (bf16[384,128]{1,0:T(8,128)(2,1)S(1)}, bf16[384,128]{1,0:T(8,128)(2,1)S(1)}, u32[]{:S(2)}, u32[]{:S(2)}) collective-permute-start(bf16[384,128]{1,0:T(8,128)(2,1)S(1)} %get-tuple-element.53), channel_id=1, source_target_pairs={{0,18},{2,8},{4,14},{6,20},{8,2},{10,24},{12,30},{14,4},{16,26},{1... | collective-permute-start | bytes 294920 | tf_op jit(solution)/shard_map/cond/branch_1_fun/ppermute | solution.py:343
  15.8 2.3 %collective-permute-done.4.received = bf16[384,128]{1,0:T(8,128)(2,1)S(1)} collective-permute-done((bf16[384,128]{1,0:T(8,128)(2,1)S(1)}, bf16[384,128]{1,0:T(8,128)(2,1)S(1)}, u32[]{:S(2)}, u32[]{:S(2)}) %collective-permute-start.4) | collective-permute-done | bytes 98336 | tf_op jit(solution)/shard_map/cond/branch_1_fun/ppermute | solution.py:343
  18.1 2.7 %collective-permute-start.5 = (bf16[384,128]{1,0:T(8,128)(2,1)S(1)}, bf16[384,128]{1,0:T(8,128)(2,1)S(1)}, u32[]{:S(2)}, u32[]{:S(2)}) collective-permute-start(bf16[384,128]{1,0:T(8,128)(2,1)S(1)} %get-tuple-element.56), channel_id=1, source_target_pairs={{0,10},{2,4},{4,2},{6,12},{8,14},{10,0},{12,6},{14,8},{16,22},{18,... | collective-permute-start | bytes 294920 | tf_op jit(solution)/shard_map/cond/branch_1_fun/ppermute | solution.py:343
  20.8 2.3 %collective-permute-done.5.received = bf16[384,128]{1,0:T(8,128)(2,1)S(1)} collective-permute-done((bf16[384,128]{1,0:T(8,128)(2,1)S(1)}, bf16[384,128]{1,0:T(8,128)(2,1)S(1)}, u32[]{:S(2)}, u32[]{:S(2)}) %collective-permute-start.5) | collective-permute-done | bytes 98336 | tf_op jit(solution)/shard_map/cond/branch_1_fun/ppermute | solution.py:343
  23.1 0.1 step3_1.1
  23.2 0.2 collective-permute-start.14
  23.4 0.4 %far.1.before = f32[512,128]{1,0:T(8,128)S(1)} custom-call(bf16[512,768]{1,0:T(8,128)(2,1)S(1)} %get-tuple-element.98.high, bf16[512,768]{1,0:T(8,128)(2,1)S(1)} %get-tuple-element.99.low, bf16[512,128]{1,0:T(8,128)(2,1)S(1)} %get-tuple-element.118.near, f32[512,128]{1,0:T(8,128)S(1)} %own.1._.before), custom_call_target="tpu_custom_call" | custom-call | flops 134217728 | bytes 2097152 | tf_op jit(solution)/shard_map/far/pallas_call | solution.py:453
  23.8 0.7 %collective-permute-done.14.theirs = bf16[256,128]{1,0:T(8,128)(2,1)S(1)} collective-permute-done((bf16[256,128]{1,0:T(8,128)(2,1)S(1)}, bf16[256,128]{1,0:T(8,128)(2,1)S(1)}, u32[]{:S(2)}, u32[]{:S(2)}) %collective-permute-start.14) | collective-permute-done | bytes 65568 | tf_op jit(solution)/shard_map/ppermute | solution.py:343
  24.5 1.0 %finish.1 = bf16[128,512]{1,0:T(8,128)(2,1)} custom-call(bf16[512,768]{1,0:T(8,128)(2,1)S(1)} %get-tuple-element.98.high, bf16[512,768]{1,0:T(8,128)(2,1)S(1)} %get-tuple-element.99.low, bf16[256,128]{1,0:T(8,128)(2,1)S(1)} %collective-permute-done.14.theirs, f32[512,128]{1,0:T(8,128)S(1)} %far.1.before), custom_call_target="tpu_custom_call" | custom-call | bytes 1048576 | tf_op jit(solution)/shard_map/finish/pallas_call | solution.py:457
  (2 shorter events, 0.1 us)
Async XLA Ops:
  0.0 6.8 %collective-permute-start.12 = (bf16[128,512]{1,0:T(8,128)(2,1)}, bf16[128,512]{1,0:T(8,128)(2,1)S(1)}, u32[]{:S(2)}, u32[]{:S(2)}) collective-permute-start(bf16[128,512]{1,0:T(8,128)(2,1)} %refs_4_.3), channel_id=1, source_target_pairs={{0,1},{1,0},{2,3},{3,2},{4,5},{5,4},{6,7},{7,6},{8,9},{9,8},{10,11... | collective-permute-start | bytes 393224 | tf_op jit(solution)/shard_map/ppermute | solution.py:346
  7.2 1.5 %collective-permute-start.13 = (bf16[384,128]{1,0:T(8,128)(2,1)S(1)}, bf16[384,128]{1,0:T(8,128)(2,1)S(1)}, u32[]{:S(2)}, u32[]{:S(2)}) collective-permute-start(bf16[384,128]{1,0:T(8,128)(2,1)S(1)} %get-tuple-element.106), channel_id=1, source_target_pairs={{0,2},{2,0},{4,6},{6,4},{8,10},{10,8},{12,14},{14,12},{16,18},{18,... | collective-permute-start | bytes 294920 | tf_op jit(solution)/shard_map/ppermute | solution.py:343
  8.9 3.8 %collective-permute-start.3 = (bf16[256,128]{1,0:T(8,128)(2,1)S(1)}, bf16[256,128]{1,0:T(8,128)(2,1)S(1)}, u32[]{:S(2)}, u32[]{:S(2)}) collective-permute-start(bf16[256,128]{1,0:T(8,128)(2,1)S(1)} %get-tuple-element.49), channel_id=1, source_target_pairs={{0,6},{2,16},{4,22},{6,0},{8,26},{10,12},{12,10},{14,28},{16,2},{1... | collective-permute-start | bytes 196616 | tf_op jit(solution)/shard_map/cond/branch_1_fun/ppermute | solution.py:343
  12.7 5.4 %collective-permute-start.4 = (bf16[384,128]{1,0:T(8,128)(2,1)S(1)}, bf16[384,128]{1,0:T(8,128)(2,1)S(1)}, u32[]{:S(2)}, u32[]{:S(2)}) collective-permute-start(bf16[384,128]{1,0:T(8,128)(2,1)S(1)} %get-tuple-element.53), channel_id=1, source_target_pairs={{0,18},{2,8},{4,14},{6,20},{8,2},{10,24},{12,30},{14,4},{16,26},{1... | collective-permute-start | bytes 294920 | tf_op jit(solution)/shard_map/cond/branch_1_fun/ppermute | solution.py:343
  18.1 5.0 %collective-permute-start.5 = (bf16[384,128]{1,0:T(8,128)(2,1)S(1)}, bf16[384,128]{1,0:T(8,128)(2,1)S(1)}, u32[]{:S(2)}, u32[]{:S(2)}) collective-permute-start(bf16[384,128]{1,0:T(8,128)(2,1)S(1)} %get-tuple-element.56), channel_id=1, source_target_pairs={{0,10},{2,4},{4,2},{6,12},{8,14},{10,0},{12,6},{14,8},{16,22},{18,... | collective-permute-start | bytes 294920 | tf_op jit(solution)/shard_map/cond/branch_1_fun/ppermute | solution.py:343
  23.2 1.3 %collective-permute-start.14 = (bf16[256,128]{1,0:T(8,128)(2,1)S(1)}, bf16[256,128]{1,0:T(8,128)(2,1)S(1)}, u32[]{:S(2)}, u32[]{:S(2)}) collective-permute-start(bf16[256,128]{1,0:T(8,128)(2,1)S(1)} %get-tuple-element.117), channel_id=1, source_target_pairs={{0,2},{2,0},{4,6},{6,4},{8,10},{10,8},{12,14},{14,12},{16,18},{18,... | collective-permute-start | bytes 196616 | tf_op jit(solution)/shard_map/ppermute | solution.py:343
